TPU v7x, 256 devices: a whole 4x4x8 slice. The times are simulated.
256 devices in a mesh: rep: 4 (over z_lo, core), shard: 64 (over z_hi, y, x).
Axes of the slice: x: 4, y: 4, z: 8 (z_hi: 4, z_lo: 2; z = z_hi * 2 + z_lo), core: 2. Of those that a mesh axis runs over, the one named last changes fastest.
Arguments:
- conv_input: bfloat16 [256, 256, 6144], P(('rep', 'shard')), may hold values from -24 to 24
- cotangent: bfloat16 [256, 256, 6144], P(('rep', 'shard')), may hold values from -24 to 24
- kernel: bfloat16 [31, 6144], P(None, 'shard'), may hold values from -1 to 1
- conv_bias: bfloat16 [6144], P('shard'), may hold values from -3 to 3
- ln_gain: bfloat16 [6144], P('shard'), may hold values from 0.25 to 1.75
- ln_bias: bfloat16 [6144], P('shard'), may hold values from -3 to 3
Outputs:
- activated: bfloat16 [256, 256, 6144], P(('rep', 'shard'))
- grad_input: bfloat16 [256, 256, 6144], P(('rep', 'shard'))
- grad_kernel: float32 [31, 6144], P(None, 'shard')
- grad_conv_bias: float32 [6144], P('shard')
- grad_gain: float32 [6144], P('shard')
- grad_ln_bias: float32 [6144], P('shard')
All inputs are finite; a program needn't handle non-finite values.
Results may differ from a plain program's by a relative error of at most 0.0012.
Values may be sent and summed in bfloat16 or wider, within the bound.
No kernel may reach another device: no remote copies, remote signals or barrier semaphores. Data moves between devices by JAX's collectives and lax.ppermute only.
A program may use at most 128 MiB of HBM per device.

v0:
```python
import math

import jax
import jax.numpy as jnp
from jax import lax
from jax.sharding import PartitionSpec as P


def forward_part(frames_in, params):
    taps = params.shape[0] - 3
    half_width = (taps - 1) // 2
    length = frames_in.shape[0]
    padded = jnp.pad(frames_in, ((half_width, half_width), (0, 0)))
    conv_out = params[taps].astype(jnp.float32)[None, :] + params[0].astype(jnp.float32) * padded[
        0:length
    ].astype(jnp.float32)
    for lag_index in range(1, taps):
        conv_out = conv_out + params[lag_index].astype(jnp.float32) * padded[
            lag_index : lag_index + length
        ].astype(jnp.float32)
    row_mean = jnp.mean(conv_out, axis=-1, keepdims=True)
    centered = conv_out - row_mean
    inverse = lax.rsqrt(jnp.mean(centered * centered, axis=-1, keepdims=True) + 1e-05)
    normed = centered * inverse
    affine = params[taps + 1].astype(jnp.float32) * normed + params[taps + 2].astype(jnp.float32)
    squash = jax.nn.sigmoid(affine)
    activated = (affine * squash).astype(jnp.bfloat16)
    return (activated, normed, inverse, affine, squash)


def backward_part(frames_in, upstream, params, normed, inverse, affine, squash):
    taps = params.shape[0] - 3
    half_width = (taps - 1) // 2
    length = frames_in.shape[0]
    grad_affine = upstream.astype(jnp.float32) * squash * (1.0 + affine * (1.0 - squash))
    grad_normed = grad_affine * params[taps + 1].astype(jnp.float32)
    grad_conv = inverse * (
        grad_normed
        - jnp.mean(grad_normed, axis=-1, keepdims=True)
        - normed * jnp.mean(grad_normed * normed, axis=-1, keepdims=True)
    )
    padded_in = jnp.pad(frames_in, ((half_width, half_width), (0, 0)))
    kernel_rows = [
        jnp.sum(grad_conv * padded_in[lag_index : lag_index + length].astype(jnp.float32), axis=0)
        for lag_index in range(taps)
    ]
    padded_grad = jnp.pad(grad_conv, ((half_width, half_width), (0, 0)))
    back_start = 2 * half_width
    grad_input = params[0].astype(jnp.float32) * padded_grad[back_start : back_start + length]
    for lag_index in range(1, taps):
        first = back_start - lag_index
        grad_input = (
            grad_input + params[lag_index].astype(jnp.float32) * padded_grad[first : first + length]
        )
    terms = jnp.concatenate(
        [
            jnp.stack(kernel_rows, 0),
            jnp.sum(grad_conv, axis=0)[None],
            jnp.sum(grad_affine * normed, axis=0)[None],
            jnp.sum(grad_affine, axis=0)[None],
        ],
        0,
    )
    return (grad_input.astype(jnp.bfloat16), terms)


def per_device(conv_input, cotangent, kernel, conv_bias, ln_gain, ln_bias):
    taps = kernel.shape[0]
    packed = jnp.concatenate([kernel, conv_bias[None], ln_gain[None], ln_bias[None]], 0)
    gathered = lax.all_gather(packed, "shard", axis=1, tiled=True)
    activated, normed, inverse, affine, squash = jax.vmap(forward_part, in_axes=(0, None))(
        conv_input, gathered
    )
    again = lax.all_gather(packed, "shard", axis=1, tiled=True)
    grad_input, terms = jax.vmap(backward_part, in_axes=(0, 0, None, 0, 0, 0, 0))(
        conv_input, cotangent, again, normed, inverse, affine, squash
    )
    terms = jnp.sum(terms, axis=0)
    replicas = lax.axis_size("rep")
    groups = lax.axis_size("shard")
    share_sum = lax.psum_scatter(terms, "shard", scatter_dimension=1, tiled=True)
    summed = lax.psum(share_sum, "rep")
    factor = 1.0 / math.sqrt(conv_input.shape[0] * conv_input.shape[1] * replicas * groups)
    grads = summed * factor
    return (activated, grad_input, grads[:taps], grads[taps], grads[taps + 1], grads[taps + 2])


def solution(mesh):
    in_specs = (
        P(("rep", "shard"), None, None),
        P(("rep", "shard"), None, None),
        P(None, "shard"),
        P("shard"),
        P("shard"),
        P("shard"),
    )
    out_specs = (
        P(("rep", "shard"), None, None),
        P(("rep", "shard"), None, None),
        P(None, "shard"),
        P("shard"),
        P("shard"),
        P("shard"),
    )
    return jax.shard_map(
        per_device, mesh=mesh, in_specs=in_specs, out_specs=out_specs, check_vma=False
    )
```

profile of v0, /device:TPU:1, one launch (start us, length us, event | category | flops | bytes accessed | tf_op | source)
XLA Modules:
  0.0 571.3 jit_solution(10006896554556620029)
XLA Ops:
  7.2 0.0 copy-start.2
  7.2 0.0 reduce-scatter.4.cloned.1.call-start
  7.2 0.9 maximum_bitcast_fusion.1
  8.1 171.1 %all-gather = bf16[64,96,34]{1,2,0:T(8,128)(2,1)S(1)} all-gather(bf16[1,96,34]{1,2,0:T(8,128)(2,1)S(1)} %maximum_bitcast_fusion.1), channel_id=1, replica_groups=mesh['rep'=4,'shard'=64] {'shard'}, dimensions={0}, use_global_device_ids=true | all-gather | bytes 424320 | tf_op jit(solution)/shard_map/all_gather | solution.py:70
  179.2 0.9 copy.13
  180.1 2.6 reshape.462
  182.8 2.5 slice_convert_fusion.32
  185.3 3.1 slice_convert_fusion.33
  188.4 0.0 copy-done.2
  188.4 37.1 %fusion.123 = (f32[256]{0:T(256)S(1)}, f32[1,256,6144]{2,1,0:T(8,128)}) fusion(f32[6144]{0:T(1024)S(1)} %bitcast.121, f32[6144]{0:T(1024)S(1)} %bitcast.123, f32[6144]{0:T(1024)} %bitcast.125, f32[6144]{0:T(1024)} %bitcast.127, f32[6144]{0:T(1024)} %bitcast.129, f32[6144]{0:T(1024)} %bitcast.131, f32[6144]{0:T(1024)} %bitcast.133, f32[6144]{0:T(1024)} %bitcast.135, ...), kind=kLoop, calls=%fused_computation.269 | loop fusion | flops 147848960 | bytes 10224640 | tf_op jit(solution)/shard_map/vmap()/reduce_sum | solution.py:21
  225.5 0.0 copy-start.1
  225.5 3.7 multiply_reduce_fusion.2
  229.3 0.9 copy-done.1
  230.1 0.0 copy-start.18
  230.1 9.2 %multiply_reduce_fusion = (f32[6144]{0:T(1024)}, f32[256]{0:T(256)S(1)}, f32[256]{0:T(256)S(1)}, f32[6144]{0:T(1024)}, f32[1,256,6144]{2,1,0:T(8,128)S(1)}, /*index=5*/bf16[1,256,6144]{2,1,0:T(8,128)(2,1)}) fusion(f32[1,256,6144]{2,1,0:T(8,128)S(1)} %copy-done.1, f32[256]{0:T(256)S(1)} %add_rsqrt_fusion, f32[256]{0:T(256)S(1)} %broadcast_multiply_fusion.3, ...), kind=kLoop, calls=%fused_computation.215 | loop fusion | flops 34590208 | bytes 18976768 | tf_op jit(solution)/shard_map/vmap()/reduce_sum | solution.py:59
  239.4 0.0 copy-done.18
  239.4 11.6 %fusion.122 = (f32[6144]{0:T(1024)}, f32[6144]{0:T(1024)}, f32[6144]{0:T(1024)}, f32[6144]{0:T(1024)}, f32[6144]{0:T(1024)}, /*index=5*/f32[6144]{0:T(1024)}, f3...) fusion(bf16[1,256,6144]{2,1,0:T(8,128)(2,1)S(1)} %copy-done.2, f32[256]{0:T(256)S(1)} %get-tuple-element.84, ...), kind=kLoop, calls=%fused_computation.214 | loop fusion | flops 53422080 | bytes 22269952 | tf_op jit(solution)/shard_map/vmap()/reduce_sum | solution.py:44
  251.0 0.0 copy-start
  251.0 4.3 fusion.89
  255.3 8.5 %fusion.98 = (f32[6144]{0:T(1024)}, f32[6144]{0:T(1024)}, f32[6144]{0:T(1024)}, f32[6144]{0:T(1024)}, f32[6144]{0:T(1024)}, /*index=5*/f32[6144]{0:T(1024)}, f32[6144]{0:T(1024)}, f32[6144]{0:T(1024)}, f32[6144]{0:T(1024)}) fusion(f32[1,256,6144]{2,1,0:T(8,128)S(1)} %get-tuple-element.42, bf16[1,256,6144]{2,1,0:T(8,128)(2,1)S(1)} %copy-done.2), kind=kLoop, calls=%fused_computation.190 | loop fusion | flops 42412032 | bytes 9658368 | tf_op jit(solution)/shard_map/vmap()/reduce_sum | solution.py:44
  263.8 0.0 copy-done
  263.8 8.9 %fusion.107 = (f32[6144]{0:T(1024)}, f32[6144]{0:T(1024)}, f32[6144]{0:T(1024)}, f32[6144]{0:T(1024)}, f32[6144]{0:T(1024)}, /*index=5*/f32[6144]{0:T(1024)}, f3...) fusion(f32[1,256,6144]{2,1,0:T(8,128)S(1)} %get-tuple-element.42, bf16[1,256,6144]{2,1,0:T(8,128)(2,1)S(1)} %copy-done.2), kind=kLoop, calls=%fused_computation.199 | loop fusion | flops 43978752 | bytes 9682944 | tf_op jit(solution)/shard_map/vmap()/reduce_sum | solution.py:44
  272.7 0.0 copy-start.3
  272.7 0.0 copy-start.4
  272.7 0.0 copy-start.5
  272.7 0.0 copy-start.6
  272.7 0.0 copy-start.7
  272.8 0.0 copy-start.8
  272.8 0.0 copy-start.9
  272.8 0.0 copy-start.10
  272.8 0.0 copy-start.11
  272.8 0.0 copy-start.12
  272.8 0.0 copy-start.13
  272.8 0.0 copy-start.14
  272.8 0.0 copy-start.15
  272.8 0.0 copy-start.16
  272.8 0.0 copy-start.17
  272.9 4.5 stack.127
  277.4 0.9 maximum_bitcast_fusion
  278.3 2.3 copy.14
  280.6 0.0 reduce-scatter.4.cloned.1.call-update
  280.6 0.0 copy-done.3
  280.7 0.0 copy-done.4
  280.7 0.0 copy-done.5
  280.7 0.0 copy-done.6
  280.7 0.0 copy-done.7
  280.7 0.0 copy-done.8
  280.7 0.0 copy-done.9
  280.7 0.0 copy-done.10
  280.7 0.0 copy-done.11
  280.7 0.0 copy-done.12
  280.7 0.0 copy-done.13
  280.8 0.0 copy-done.14
  280.8 0.0 copy-done.15
  280.8 0.0 copy-done.16
  280.8 0.0 copy-done.17
  280.8 88.0 %fusion.54 = bf16[1,256,6144]{2,1,0:T(8,128)(2,1)} fusion(f32[1,256,6144]{2,1,0:T(8,128)} %copy-done, f32[6144]{0:T(1024)S(1)} %bitcast.122, f32[6144]{0:T(1024)S(1)} %bitcast.124, f32[6144]{0:T(1024)S(1)} %bitcast.126, f32[6144]{0:T(1024)S(1)} %bitcast.128, f32[6144]{0:T(1024)S(1)} %bitcast.130, f32[6144]{0:T(1024)S(1)} %bitcast.132, ...), kind=kLoop, calls=%fused_computation.146 | loop fusion | flops 97517568 | bytes 10199040 | tf_op jit(solution)/shard_map/vmap()/convert_element_type | solution.py:64
  368.8 181.7 %reduce-scatter.4.cloned.1.call-done = f32[96,34]{1,0:T(8,128)} async-done(((f32[6144,34]{1,0:T(8,128)}), f32[96,34]{1,0:T(8,128)}) %reduce-scatter.4.cloned.1.call-update) | async-done | bytes 13072
  550.6 0.9 copy.15
  551.4 11.9 %psum.7 = f32[34,96]{1,0:T(8,128)S(1)} all-reduce(f32[34,96]{1,0:T(8,128)S(1)} %copy.15), channel_id=1, replica_groups=mesh['rep'=4,'shard'=64] {'rep'}, use_global_device_ids=true, to_apply=%region_39.40 | all-reduce | flops 3264 | bytes 26112 | tf_op jit(solution)/shard_map/psum | solution.py:82
  563.3 0.5 slice_bitcast_fusion
  563.9 0.6 slice.491
  (4 shorter events, 0.0 us)
Async XLA Ops:
  7.2 181.2 %copy-start.2 = (bf16[1,256,6144]{2,1,0:T(8,128)(2,1)S(1)}, bf16[1,256,6144]{2,1,0:T(8,128)(2,1)}, u32[]{:S(2)}) copy-start(bf16[1,256,6144]{2,1,0:T(8,128)(2,1)} %param.6) | copy-start | bytes 9437188
  7.2 543.4 %reduce-scatter.4.cloned.1.call-start = ((), (), s32[]{:S(2)}) async-start(), calls=%async_computation.1 | async-start | bytes 3194880
  225.5 4.6 copy-start.1
  230.1 9.2 %copy-start.18 = (f32[1,6144]{1,0:T(1,128)S(1)}, f32[1,6144]{1,0:T(1,128)}, u32[]{:S(2)}) copy-start(f32[1,6144]{1,0:T(1,128)} %get-tuple-element.47) | copy-start | bytes 73732
  251.0 12.8 %copy-start = (f32[1,256,6144]{2,1,0:T(8,128)}, f32[1,256,6144]{2,1,0:T(8,128)S(1)}, u32[]{:S(2)}) copy-start(f32[1,256,6144]{2,1,0:T(8,128)S(1)} %get-tuple-element.42) | copy-start | bytes 18874372
  272.7 7.9 %copy-start.3 = (f32[1,6144]{1,0:T(1,128)S(1)}, f32[1,6144]{1,0:T(1,128)}, u32[]{:S(2)}) copy-start(f32[1,6144]{1,0:T(1,128)} %get-tuple-element.51) | copy-start | bytes 73732
  272.7 7.9 %copy-start.4 = (f32[1,6144]{1,0:T(1,128)S(1)}, f32[1,6144]{1,0:T(1,128)}, u32[]{:S(2)}) copy-start(f32[1,6144]{1,0:T(1,128)} %get-tuple-element.52) | copy-start | bytes 73732
  272.7 7.9 %copy-start.5 = (f32[1,6144]{1,0:T(1,128)S(1)}, f32[1,6144]{1,0:T(1,128)}, u32[]{:S(2)}) copy-start(f32[1,6144]{1,0:T(1,128)} %get-tuple-element.53) | copy-start | bytes 73732
  272.7 7.9 %copy-start.6 = (f32[1,6144]{1,0:T(1,128)S(1)}, f32[1,6144]{1,0:T(1,128)}, u32[]{:S(2)}) copy-start(f32[1,6144]{1,0:T(1,128)} %get-tuple-element.54) | copy-start | bytes 73732
  272.7 7.9 %copy-start.7 = (f32[1,6144]{1,0:T(1,128)S(1)}, f32[1,6144]{1,0:T(1,128)}, u32[]{:S(2)}) copy-start(f32[1,6144]{1,0:T(1,128)} %get-tuple-element.55) | copy-start | bytes 73732
  272.8 7.9 %copy-start.8 = (f32[1,6144]{1,0:T(1,128)S(1)}, f32[1,6144]{1,0:T(1,128)}, u32[]{:S(2)}) copy-start(f32[1,6144]{1,0:T(1,128)} %get-tuple-element.56) | copy-start | bytes 73732
  272.8 7.9 %copy-start.9 = (f32[1,6144]{1,0:T(1,128)S(1)}, f32[1,6144]{1,0:T(1,128)}, u32[]{:S(2)}) copy-start(f32[1,6144]{1,0:T(1,128)} %get-tuple-element.57) | copy-start | bytes 73732
  272.8 7.9 %copy-start.10 = (f32[1,6144]{1,0:T(1,128)S(1)}, f32[1,6144]{1,0:T(1,128)}, u32[]{:S(2)}) copy-start(f32[1,6144]{1,0:T(1,128)} %get-tuple-element.58) | copy-start | bytes 73732
  272.8 7.9 %copy-start.11 = (f32[1,6144]{1,0:T(1,128)S(1)}, f32[1,6144]{1,0:T(1,128)}, u32[]{:S(2)}) copy-start(f32[1,6144]{1,0:T(1,128)} %get-tuple-element.59) | copy-start | bytes 73732
  272.8 7.9 %copy-start.12 = (f32[1,6144]{1,0:T(1,128)S(1)}, f32[1,6144]{1,0:T(1,128)}, u32[]{:S(2)}) copy-start(f32[1,6144]{1,0:T(1,128)} %get-tuple-element.60) | copy-start | bytes 73732
  272.8 7.9 %copy-start.13 = (f32[1,6144]{1,0:T(1,128)S(1)}, f32[1,6144]{1,0:T(1,128)}, u32[]{:S(2)}) copy-start(f32[1,6144]{1,0:T(1,128)} %get-tuple-element.61) | copy-start | bytes 73732
  272.8 7.9 %copy-start.14 = (f32[1,6144]{1,0:T(1,128)S(1)}, f32[1,6144]{1,0:T(1,128)}, u32[]{:S(2)}) copy-start(f32[1,6144]{1,0:T(1,128)} %get-tuple-element.62) | copy-start | bytes 73732
  272.8 7.9 %copy-start.15 = (f32[1,6144]{1,0:T(1,128)S(1)}, f32[1,6144]{1,0:T(1,128)}, u32[]{:S(2)}) copy-start(f32[1,6144]{1,0:T(1,128)} %get-tuple-element.63) | copy-start | bytes 73732
  272.8 7.9 %copy-start.16 = (f32[1,6144]{1,0:T(1,128)S(1)}, f32[1,6144]{1,0:T(1,128)}, u32[]{:S(2)}) copy-start(f32[1,6144]{1,0:T(1,128)} %get-tuple-element.64) | copy-start | bytes 73732
  272.8 7.9 %copy-start.17 = (f32[1,6144]{1,0:T(1,128)S(1)}, f32[1,6144]{1,0:T(1,128)}, u32[]{:S(2)}) copy-start(f32[1,6144]{1,0:T(1,128)} %get-tuple-element.65) | copy-start | bytes 73732
Sparse Core Ops, SparseCore 0:
  280.8 269.7 reduce-scatter.3
where the time goes:
time: 572 us; the launch traced here: 571 us
  blocking collectives  183 us (32%)
  waiting for transfers between devices  182 us (32%)
  other arithmetic  179 us (31%)
  between operations  14.3 us (2%)
  local copies, waits for them, and re-layouts  13.4 us (2%)
    unnamed x2, waiting for transfers between devices  182 us
    all_gather x1, blocking collectives, per_device(): gathered = lax.all_gather(packed, 'shard', axis=1, tiled=True)  171 us
    convert_element_type x1, other arithmetic, backward_part(): return (grad_input.astype(jnp.bfloat16), terms)  88 us
    reduce_sum x1, other arithmetic, forward_part(): row_mean = jnp.mean(conv_out, axis=-1, keepdims=True)  37.1 us
    reduce_sum x4, other arithmetic, backward_part(): jnp.sum(grad_conv * padded_in[lag_index:lag_index + length].astype(jnp.fl...  33.4 us
    psum x1, blocking collectives, per_device(): summed = lax.psum(share_sum, 'rep')  11.9 us
  transfers between devices with their start and end apart: 1, of which 1 were waited for; matrix products, arithmetic and copies ran while one was open for 15% of the time, Pallas kernels for 0%

commit v1 on v0

--- a/solution.py
+++ b/solution.py
@@ -64,22 +64,51 @@
     return (grad_input.astype(jnp.bfloat16), terms)
 
 
+SIDE = 4
+
+
+def shifted(axis_stride, step):
+    pairs = []
+    for source in range(SIDE**3):
+        at = (source // axis_stride) % SIDE
+        pairs.append((source, source + ((at + step) % SIDE - at) * axis_stride))
+    return pairs
+
+
+def gather_stage(block, axis_stride):
+    at = (lax.axis_index("shard") // axis_stride) % SIDE
+    whole = jnp.zeros((SIDE,) + block.shape, block.dtype)
+    whole = lax.dynamic_update_index_in_dim(whole, block, at, 0)
+    for step in range(1, SIDE):
+        came = lax.ppermute(block, "shard", shifted(axis_stride, step))
+        whole = lax.dynamic_update_index_in_dim(whole, came, (at - step) % SIDE, 0)
+    return whole
+
+
+def gather_channels(packed):
+    rows, width = packed.shape
+    whole = gather_stage(packed, 16)
+    whole = gather_stage(whole, 4)
+    whole = gather_stage(whole, 1)
+    return whole.transpose(3, 2, 1, 0, 4).reshape(rows, SIDE**3 * width)
+
+
 def per_device(conv_input, cotangent, kernel, conv_bias, ln_gain, ln_bias):
     taps = kernel.shape[0]
     packed = jnp.concatenate([kernel, conv_bias[None], ln_gain[None], ln_bias[None]], 0)
-    gathered = lax.all_gather(packed, "shard", axis=1, tiled=True)
+    gathered = lax.optimization_barrier(gather_channels(packed))
     activated, normed, inverse, affine, squash = jax.vmap(forward_part, in_axes=(0, None))(
         conv_input, gathered
     )
-    again = lax.all_gather(packed, "shard", axis=1, tiled=True)
     grad_input, terms = jax.vmap(backward_part, in_axes=(0, 0, None, 0, 0, 0, 0))(
-        conv_input, cotangent, again, normed, inverse, affine, squash
+        conv_input, cotangent, gathered, normed, inverse, affine, squash
     )
     terms = jnp.sum(terms, axis=0)
     replicas = lax.axis_size("rep")
     groups = lax.axis_size("shard")
-    share_sum = lax.psum_scatter(terms, "shard", scatter_dimension=1, tiled=True)
-    summed = lax.psum(share_sum, "rep")
+    pieces = terms.reshape(terms.shape[0], groups, -1).transpose(1, 0, 2)
+    share_sum = jnp.sum(lax.all_to_all(pieces, "shard", 0, 0), axis=0)
+    summed = jnp.sum(lax.all_gather(share_sum, "rep", axis=0), axis=0)
     factor = 1.0 / math.sqrt(conv_input.shape[0] * conv_input.shape[1] * replicas * groups)
     grads = summed * factor
     return (activated, grad_input, grads[:taps], grads[taps], grads[taps + 1], grads[taps + 2])

time: 572 us -> 306 us (0.53)
  waiting for transfers between devices: 182 us -> 3.17 us
  blocking collectives: 183 us -> 10 us
  local copies, waits for them, and re-layouts: 13.4 us -> 81.1 us
  starting transfers between devices: 0.04 us -> 27.8 us
  between operations: 14.3 us -> 1.32 us
    unnamed x2 -> x0, waiting for transfers between devices: 182 us -> none
    all_gather x1, blocking collectives: 171 us -> 10 us  [per_device(): summed = jnp.sum(lax.all_gather(share_sum, 'rep', axis=0), axis=0)]
    dynamic_update_slice x0 -> x12, local copies, waits for them, and re-layouts: none -> 34.5 us  [the longest x9 25.9 us: gather_stage(): whole = lax.dynamic_update_index_in_dim(whole, came, (at - step) % SIDE, 0)]
    another operation x1 -> x31, local copies, waits for them, and re-layouts: 4.54 us -> 26.4 us  [backward_part(): jnp.stack(kernel_rows, 0)]
    ppermute x0 -> x9, starting transfers between devices: none -> 18.9 us  [gather_stage(): came = lax.ppermute(block, 'shard', shifted(axis_stride, step))]
    psum x1 -> x0, blocking collectives: 11.9 us -> none  [per_device(): summed = lax.psum(share_sum, 'rep')]
    all_to_all x0 -> x1, starting transfers between devices: none -> 8.98 us  [per_device(): share_sum = jnp.sum(lax.all_to_all(pieces, 'shard', 0, 0), axis=0)]
    concatenate x0 -> x4, local copies, waits for them, and re-layouts: none -> 7.77 us  [backward_part(): jnp.concatenate([jnp.stack(kernel_rows, 0), jnp.sum(grad_conv, axis=0)[No...]
  transfers between devices with their start and end apart: 1 -> 10, of which waited for: 1 -> 2; matrix products, arithmetic and copies ran while one was open for 15% -> 34% of each run, Pallas kernels for 0% -> 0%
where the time goes in v1:
time: 306 us; the launch traced here: 302 us
  other arithmetic  178 us (58%)
  local copies, waits for them, and re-layouts  81.1 us (27%)
  starting transfers between devices  27.8 us (9%)
  blocking collectives  10 us (3%)
  waiting for transfers between devices  3.17 us (1%)
    convert_element_type x1, other arithmetic, backward_part(): return (grad_input.astype(jnp.bfloat16), terms)  88 us
    reduce_sum x1, other arithmetic, forward_part(): row_mean = jnp.mean(conv_out, axis=-1, keepdims=True)  37.1 us
    reduce_sum x4, other arithmetic, backward_part(): jnp.sum(grad_conv * padded_in[lag_index:lag_index + length].astype(jnp.fl...  33.4 us
    another operation x31, local copies, waits for them, and re-layouts, backward_part(): jnp.stack(kernel_rows, 0)  26.4 us
    dynamic_update_slice x9, local copies, waits for them, and re-layouts, gather_stage(): whole = lax.dynamic_update_index_in_dim(whole, came, (at - step) % SIDE, 0)  25.9 us
    ppermute x9, starting transfers between devices, gather_stage(): came = lax.ppermute(block, 'shard', shifted(axis_stride, step))  18.9 us
    all_gather x1, blocking collectives, per_device(): summed = jnp.sum(lax.all_gather(share_sum, 'rep', axis=0), axis=0)  10 us
    reduce_sum x1, other arithmetic, backward_part(): jnp.sum(grad_affine * normed, axis=0)[None]  9.23 us
  transfers between devices with their start and end apart: 10, of which 2 were waited for; matrix products, arithmetic and copies ran while one was open for 34% of the time, Pallas kernels for 0%

profile of v1, /device:TPU:1, one launch (start us, length us, event | category | flops | bytes accessed | tf_op | source)
XLA Modules:
  0.0 301.7 jit_solution(11670533832104359920)
XLA Ops:
  0.6 0.9 pad_maximum_fusion
  1.6 7.8 %collective-permute-start.1 = (bf16[34,96]{1,0:T(8,128)(2,1)S(1)}, bf16[34,96]{1,0:T(8,128)(2,1)S(1)}, u32[]{:S(2)}, u32[]{:S(2)}) collective-permute-start(bf16[34,96]{1,0:T(8,128)(2,1)S(1)} %get-tuple-element.84), channel_id=1, source_target_pairs={{0,32},{1,33},{2,34},{3,35},{4,36},{5,37},{6,38},{7,39},{8,40},{9,... | collective-permute-start | bytes 19592 | tf_op jit(solution)/shard_map/ppermute | solution.py:83
  9.4 1.2 collective-permute-start
  10.6 2.4 collective-permute-start.2
  14.3 2.8 collective-permute-start.5
  19.5 2.3 collective-permute-done.3
  23.7 2.5 collective-permute-start.8
  27.3 1.2 copy.70
  28.5 1.1 broadcast_in_dim.51
  29.5 7.9 %dynamic_update_slice.47 = bf16[4,4,4,34,96]{4,0,1,2,3:T(4,128)(2,1)} dynamic-update-slice(bf16[4,4,4,34,96]{4,0,1,2,3:T(4,128)(2,1)} %broadcast_in_dim.51, bf16[1,4,4,34,96]{4,0,1,2,3:T(2,128)(2,1)S(1)} %copy.70, s32[]{:T(128)S(6)} %select_n.117, s32[]{:T(128)} %constant.144.clone.1, s32[]{:T(128)} %constant.144.clone.1, s32[]{:T(128)} %constant.144.clone.1, s32[]{:T(128)} %constant.144.clone.1) | dynamic-update-slice | bytes 208900 | tf_op jit(solution)/shard_map/jit(dynamic_update_index_in_dim)/dynamic_update_slice | solution.py:81
  37.5 1.1 copy.73
  38.6 1.8 copy.72
  40.4 1.8 copy.71
  42.3 7.9 %dynamic_update_slice.48 = bf16[4,4,4,34,96]{4,0,1,2,3:T(4,128)(2,1)} dynamic-update-slice(bf16[4,4,4,34,96]{4,0,1,2,3:T(4,128)(2,1)} %dynamic_update_slice.47, bf16[1,4,4,34,96]{4,0,1,2,3:T(2,128)(2,1)} %copy.71, s32[]{:T(128)S(6)} %select_n.119, s32[]{:T(128)} %constant.144.clone.1, s32[]{:T(128)} %constant.144.clone.1, s32[]{:T(128)} %constant.144.clone.1, s32[]{:T(128)} %constant.144.clone.1) | dynamic-update-slice | bytes 208900 | tf_op jit(solution)/shard_map/jit(dynamic_update_index_in_dim)/dynamic_update_slice | solution.py:84
  50.2 7.9 %dynamic_update_slice.49 = bf16[4,4,4,34,96]{4,0,1,2,3:T(4,128)(2,1)} dynamic-update-slice(bf16[4,4,4,34,96]{4,0,1,2,3:T(4,128)(2,1)} %dynamic_update_slice.48, bf16[1,4,4,34,96]{4,0,1,2,3:T(2,128)(2,1)} %copy.72, s32[]{:T(128)S(6)} %select_n.121, s32[]{:T(128)} %constant.144.clone.1, s32[]{:T(128)} %constant.144.clone.1, s32[]{:T(128)} %constant.144.clone.1, s32[]{:T(128)} %constant.144.clone.1) | dynamic-update-slice | bytes 208900 | tf_op jit(solution)/shard_map/jit(dynamic_update_index_in_dim)/dynamic_update_slice | solution.py:84
  58.1 7.9 %dynamic_update_slice.50 = bf16[4,4,4,34,96]{4,0,1,2,3:T(4,128)(2,1)} dynamic-update-slice(bf16[4,4,4,34,96]{4,0,1,2,3:T(4,128)(2,1)} %dynamic_update_slice.49, bf16[1,4,4,34,96]{4,0,1,2,3:T(2,128)(2,1)S(1)} %copy.73, s32[]{:T(128)S(6)} %select_n.123, s32[]{:T(128)} %constant.144.clone.1, s32[]{:T(128)} %constant.144.clone.1, s32[]{:T(128)} %constant.144.clone.1, s32[]{:T(128)} %constant.144.clone.1) | dynamic-update-slice | bytes 208900 | tf_op jit(solution)/shard_map/jit(dynamic_update_index_in_dim)/dynamic_update_slice | solution.py:84
  66.0 2.6 reshape.502
  68.6 2.5 slice_convert_fusion.32
  71.2 3.1 %slice_convert_fusion.33 = (f32[1,6144]{1,0:T(1,128)}, f32[1,6144]{1,0:T(1,128)}, f32[1,6144]{1,0:T(1,128)S(1)}, f32[1,6144]{1,0:T(1,128)S(1)}, f32[1,6144]{1,0:...) fusion(bf16[34,6144]{1,0:T(8,128)(2,1)} %reshape.502), kind=kLoop, calls=%fused_computation.262 | loop fusion | flops 116736 | bytes 700416 | tf_op jit(solution)/shard_map/vmap()/convert_element_type | solution.py:25
  74.3 37.1 %fusion.124 = (f32[256]{0:T(256)S(1)}, f32[1,256,6144]{2,1,0:T(8,128)}) fusion(f32[6144]{0:T(1024)S(1)} %bitcast.92, f32[6144]{0:T(1024)S(1)} %bitcast.94, f32[6144]{0:T(1024)} %bitcast.96, f32[6144]{0:T(1024)} %bitcast.98, f32[6144]{0:T(1024)} %bitcast.100, f32[6144]{0:T(1024)} %bitcast.102, f32[6144]{0:T(1024)} %bitcast.104, f32[6144]{0:T(1024)} %bitcast.106, ...), kind=kLoop, calls=%fused_computation.273 | loop fusion | flops 147848960 | bytes 10224640 | tf_op jit(solution)/shard_map/vmap()/reduce_sum | solution.py:21
  111.4 3.7 %multiply_reduce_fusion.2 = f32[256]{0:T(256)S(1)} fusion(f32[1,256,6144]{2,1,0:T(8,128)} %get-tuple-element.45, f32[256]{0:T(256)S(1)} %broadcast_multiply_fusion.3), kind=kLoop, calls=%fused_computation.222 | loop fusion | flops 4718336 | bytes 6293504 | tf_op jit(solution)/shard_map/vmap()/reduce_sum | solution.py:23
  115.1 0.9 copy-done.1
  116.0 9.2 %multiply_reduce_fusion = (f32[6144]{0:T(1024)}, f32[256]{0:T(256)S(1)}, f32[256]{0:T(256)S(1)}, f32[6144]{0:T(1024)}, f32[1,256,6144]{2,1,0:T(8,128)S(1)}, /*index=5*/bf16[1,256,6144]{2,1,0:T(8,128)(2,1)}) fusion(f32[1,256,6144]{2,1,0:T(8,128)S(1)} %copy-done.1, f32[256]{0:T(256)S(1)} %add_rsqrt_fusion, f32[256]{0:T(256)S(1)} %broadcast_multiply_fusion.3, ...), kind=kLoop, calls=%fused_computation.215 | loop fusion | flops 34590208 | bytes 18976768 | tf_op jit(solution)/shard_map/vmap()/reduce_sum | solution.py:59
  125.2 11.9 %fusion.122 = (f32[6144]{0:T(1024)}, f32[6144]{0:T(1024)}, f32[6144]{0:T(1024)}, f32[6144]{0:T(1024)}, f32[6144]{0:T(1024)}, /*index=5*/f32[6144]{0:T(1024)}, f3...) fusion(bf16[1,256,6144]{2,1,0:T(8,128)(2,1)S(1)} %copy-done.2, f32[256]{0:T(256)S(1)} %get-tuple-element.86, ...), kind=kLoop, calls=%fused_computation.214 | loop fusion | flops 53422080 | bytes 22269952 | tf_op jit(solution)/shard_map/vmap()/reduce_sum | solution.py:44
  137.1 4.3 %fusion.89 = (f32[6144]{0:T(1024)}, f32[6144]{0:T(1024)}, f32[6144]{0:T(1024)}, f32[6144]{0:T(1024)}) fusion(f32[1,256,6144]{2,1,0:T(8,128)S(1)} %get-tuple-element.42, bf16[1,256,6144]{2,1,0:T(8,128)(2,1)S(1)} %copy-done.2), kind=kLoop, calls=%fused_computation.181 | loop fusion | flops 18849792 | bytes 9535488 | tf_op jit(solution)/shard_map/vmap()/reduce_sum | solution.py:44
  141.4 8.5 %fusion.98 = (f32[6144]{0:T(1024)}, f32[6144]{0:T(1024)}, f32[6144]{0:T(1024)}, f32[6144]{0:T(1024)}, f32[6144]{0:T(1024)}, /*index=5*/f32[6144]{0:T(1024)}, f32[6144]{0:T(1024)}, f32[6144]{0:T(1024)}, f32[6144]{0:T(1024)}) fusion(f32[1,256,6144]{2,1,0:T(8,128)S(1)} %get-tuple-element.42, bf16[1,256,6144]{2,1,0:T(8,128)(2,1)S(1)} %copy-done.2), kind=kLoop, calls=%fused_computation.190 | loop fusion | flops 42412032 | bytes 9658368 | tf_op jit(solution)/shard_map/vmap()/reduce_sum | solution.py:44
  149.9 8.8 %fusion.107 = (f32[6144]{0:T(1024)}, f32[6144]{0:T(1024)}, f32[6144]{0:T(1024)}, f32[6144]{0:T(1024)}, f32[6144]{0:T(1024)}, /*index=5*/f32[6144]{0:T(1024)}, f3...) fusion(f32[1,256,6144]{2,1,0:T(8,128)S(1)} %get-tuple-element.42, bf16[1,256,6144]{2,1,0:T(8,128)(2,1)S(1)} %copy-done.2), kind=kLoop, calls=%fused_computation.199 | loop fusion | flops 43978752 | bytes 9682944 | tf_op jit(solution)/shard_map/vmap()/reduce_sum | solution.py:44
  158.8 1.0 stack.124
  159.8 0.8 concatenate.17
  160.6 0.8 stack.123
  161.5 0.8 stack.122
  162.3 0.8 stack.121
  163.2 0.8 stack.120
  164.0 0.8 stack.119
  164.9 0.8 stack.118
  165.7 0.8 stack.117
  166.6 0.8 stack.116
  167.5 0.8 concatenate.18
  168.3 0.8 stack.97
  169.2 0.8 stack.96
  170.0 0.8 stack.95
  170.9 0.8 stack.94
  171.7 0.8 stack.106
  172.6 0.8 stack.105
  173.4 0.8 stack.104
  174.3 0.8 stack.103
  175.2 0.8 stack.102
  176.0 0.8 stack.101
  176.9 0.8 stack.100
  177.7 0.8 stack.99
  178.6 0.8 stack.98
  179.4 0.8 stack.115
  180.3 0.8 stack.114
  181.1 0.8 stack.113
  182.0 0.8 stack.112
  182.8 0.8 stack.111
  183.7 0.8 stack.110
  184.6 0.8 stack.109
  185.4 0.8 stack.108
  186.3 0.8 stack.107
  188.0 5.2 %concatenate.19 = f32[34,64,96]{2,0,1:T(8,128)} concatenate(f32[1,64,96]{2,0,1:T(1,128)S(1)} %stack.94, f32[1,64,96]{2,0,1:T(1,128)S(1)} %stack.95, f32[1,64,96]{2,0,1:T(1,128)S(1)} %stack.96, f32[1,64,96]{2,0,1:T(1,128)S(1)} %stack.97, f32[1,64,96]{2,0,1:T(1,128)S(1)} %stack.98, f32[1,64,96]{2,0,1:T(1,128)S(1)} %stack.99, f32[1,64,96]{2,0,1:T(1,128)S(1)} %stack.100, ...), dimensions={0} | concatenate | bytes 1671168 | tf_op jit(solution)/shard_map/vmap()/concatenate | solution.py:55
  193.2 9.0 %all-to-all-start = ((f32[64,34,96]{2,1,0:T(8,128)}), f32[64,34,96]{2,1,0:T(8,128)S(1)}, u32[]{:S(2)}, u32[]{:S(2)}) async-start(f32[64,34,96]{2,1,0:T(8,128)} %bitcast.50), calls=%async_computation | async-start | bytes 2621440 | tf_op jit(solution)/shard_map/all_to_all | solution.py:110
  202.3 88.0 %fusion.54 = bf16[1,256,6144]{2,1,0:T(8,128)(2,1)} fusion(f32[1,256,6144]{2,1,0:T(8,128)} %copy-done, f32[6144]{0:T(1024)S(1)} %bitcast.93, f32[6144]{0:T(1024)S(1)} %bitcast.95, f32[6144]{0:T(1024)S(1)} %bitcast.97, f32[6144]{0:T(1024)S(1)} %bitcast.99, f32[6144]{0:T(1024)S(1)} %bitcast.101, f32[6144]{0:T(1024)S(1)} %bitcast.103, f32[6144]{0:T(1024)S(1)} %bitcast.105, ...), kind=kLoop, calls=%fused_computation.146 | loop fusion | flops 97517568 | bytes 10199040 | tf_op jit(solution)/shard_map/vmap()/convert_element_type | solution.py:64
  290.5 10.0 %all-gather.1 = f32[4,34,96]{2,1,0:T(8,128)S(1)} all-gather(f32[1,34,96]{2,1,0:T(8,128)S(1)} %bitcast.130), channel_id=2, replica_groups=mesh['rep'=4,'shard'=64] {'rep'}, dimensions={0}, use_global_device_ids=true | all-gather | bytes 65280 | tf_op jit(solution)/shard_map/all_gather | solution.py:111
  (73 shorter events, 8.9 us)
Async XLA Ops:
  0.6 73.6 %copy-start.2 = (bf16[1,256,6144]{2,1,0:T(8,128)(2,1)S(1)}, bf16[1,256,6144]{2,1,0:T(8,128)(2,1)}, u32[]{:S(2)}) copy-start(bf16[1,256,6144]{2,1,0:T(8,128)(2,1)} %param.6) | copy-start | bytes 9437188
  1.6 11.6 %collective-permute-start.1 = (bf16[34,96]{1,0:T(8,128)(2,1)S(1)}, bf16[34,96]{1,0:T(8,128)(2,1)S(1)}, u32[]{:S(2)}, u32[]{:S(2)}) collective-permute-start(bf16[34,96]{1,0:T(8,128)(2,1)S(1)} %get-tuple-element.84), channel_id=1, source_target_pairs={{0,32},{1,33},{2,34},{3,35},{4,36},{5,37},{6,38},{7,39},{8,40},{9,... | collective-permute-start | bytes 19592 | tf_op jit(solution)/shard_map/ppermute | solution.py:83
  9.4 4.6 %collective-permute-start = (bf16[34,96]{1,0:T(8,128)(2,1)S(1)}, bf16[34,96]{1,0:T(8,128)(2,1)S(1)}, u32[]{:S(2)}, u32[]{:S(2)}) collective-permute-start(bf16[34,96]{1,0:T(8,128)(2,1)S(1)} %get-tuple-element.84), channel_id=1, source_target_pairs={{0,16},{1,17},{2,18},{3,19},{4,20},{5,21},{6,22},{7,23},{8,24},{9,... | collective-permute-start | bytes 19592 | tf_op jit(solution)/shard_map/ppermute | solution.py:83
  10.6 3.5 %collective-permute-start.2 = (bf16[34,96]{1,0:T(8,128)(2,1)S(1)}, bf16[34,96]{1,0:T(8,128)(2,1)S(1)}, u32[]{:S(2)}, u32[]{:S(2)}) collective-permute-start(bf16[34,96]{1,0:T(8,128)(2,1)S(1)} %get-tuple-element.84), channel_id=1, source_target_pairs={{0,48},{1,49},{2,50},{3,51},{4,52},{5,53},{6,54},{7,55},{8,56},{9,... | collective-permute-start | bytes 19592 | tf_op jit(solution)/shard_map/ppermute | solution.py:83
  14.3 8.7 %collective-permute-start.5 = (bf16[4,34,96]{2,0,1:T(4,128)(2,1)S(1)}, bf16[4,34,96]{2,0,1:T(4,128)(2,1)S(1)}, u32[]{:S(2)}, u32[]{:S(2)}) collective-permute-start(bf16[4,34,96]{2,0,1:T(4,128)(2,1)S(1)} %dynamic_update_slice.42), channel_id=1, source_target_pairs={{0,12},{1,13},{2,14},{3,15},{4,0},{5,1},{6,2},{7,3},{8,4},{9,5},{1... | collective-permute-start | bytes 78344 | tf_op jit(solution)/shard_map/ppermute | solution.py:83
  17.2 5.3 %collective-permute-start.4 = (bf16[4,34,96]{2,0,1:T(4,128)(2,1)S(1)}, bf16[4,34,96]{2,0,1:T(4,128)(2,1)S(1)}, u32[]{:S(2)}, u32[]{:S(2)}) collective-permute-start(bf16[4,34,96]{2,0,1:T(4,128)(2,1)S(1)} %dynamic_update_slice.42), channel_id=1, source_target_pairs={{0,8},{1,9},{2,10},{3,11},{4,12},{5,13},{6,14},{7,15},{8,0},{9,1},... | collective-permute-start | bytes 78344 | tf_op jit(solution)/shard_map/ppermute | solution.py:83
  17.5 4.3 %collective-permute-start.3 = (bf16[4,34,96]{2,0,1:T(4,128)(2,1)S(1)}, bf16[4,34,96]{2,0,1:T(4,128)(2,1)S(1)}, u32[]{:S(2)}, u32[]{:S(2)}) collective-permute-start(bf16[4,34,96]{2,0,1:T(4,128)(2,1)S(1)} %dynamic_update_slice.42), channel_id=1, source_target_pairs={{0,4},{1,5},{2,6},{3,7},{4,8},{5,9},{6,10},{7,11},{8,12},{9,13},{1... | collective-permute-start | bytes 78344 | tf_op jit(solution)/shard_map/ppermute | solution.py:83
  23.7 13.8 %collective-permute-start.8 = (bf16[4,4,34,96]{3,1,2,0:T(4,128)(2,1)}, bf16[4,4,34,96]{3,1,2,0:T(4,128)(2,1)}, u32[]{:S(2)}, u32[]{:S(2)}) collective-permute-start(bf16[4,4,34,96]{3,1,2,0:T(4,128)(2,1)} %bitcast_dynamic-update-slice_fusion), channel_id=1, source_target_pairs={{0,3},{1,0},{2,1},{3,2},{4,7},{5,4},{6,5},{7,6},{8,11},{9,8},{10,9... | collective-permute-start | bytes 313352 | tf_op jit(solution)/shard_map/ppermute | solution.py:83
  26.2 12.4 %collective-permute-start.7 = (bf16[4,4,34,96]{3,1,2,0:T(4,128)(2,1)}, bf16[4,4,34,96]{3,1,2,0:T(4,128)(2,1)}, u32[]{:S(2)}, u32[]{:S(2)}) collective-permute-start(bf16[4,4,34,96]{3,1,2,0:T(4,128)(2,1)} %bitcast_dynamic-update-slice_fusion), channel_id=1, source_target_pairs={{0,2},{1,3},{2,0},{3,1},{4,6},{5,7},{6,4},{7,5},{8,10},{9,11},{10,... | collective-permute-start | bytes 313352 | tf_op jit(solution)/shard_map/ppermute | solution.py:83
  26.7 13.7 %collective-permute-start.6 = (bf16[4,4,34,96]{3,1,2,0:T(4,128)(2,1)}, bf16[4,4,34,96]{3,1,2,0:T(4,128)(2,1)}, u32[]{:S(2)}, u32[]{:S(2)}) collective-permute-start(bf16[4,4,34,96]{3,1,2,0:T(4,128)(2,1)} %bitcast_dynamic-update-slice_fusion), channel_id=1, source_target_pairs={{0,1},{1,2},{2,3},{3,0},{4,5},{5,6},{6,7},{7,4},{8,9},{9,10},{10,1... | collective-permute-start | bytes 313352 | tf_op jit(solution)/shard_map/ppermute | solution.py:83
  111.4 4.6 %copy-start.1 = (f32[1,256,6144]{2,1,0:T(8,128)S(1)}, f32[1,256,6144]{2,1,0:T(8,128)}, u32[]{:S(2)}) copy-start(f32[1,256,6144]{2,1,0:T(8,128)} %get-tuple-element.45) | copy-start | bytes 18874372
  116.0 9.2 %copy-start.18 = (f32[1,6144]{1,0:T(1,128)S(1)}, f32[1,6144]{1,0:T(1,128)}, u32[]{:S(2)}) copy-start(f32[1,6144]{1,0:T(1,128)} %get-tuple-element.47) | copy-start | bytes 73732
  137.1 12.8 %copy-start = (f32[1,256,6144]{2,1,0:T(8,128)}, f32[1,256,6144]{2,1,0:T(8,128)S(1)}, u32[]{:S(2)}) copy-start(f32[1,256,6144]{2,1,0:T(8,128)S(1)} %get-tuple-element.42) | copy-start | bytes 18874372
  158.7 43.5 %copy-start.3 = (f32[1,6144]{1,0:T(1,128)S(1)}, f32[1,6144]{1,0:T(1,128)}, u32[]{:S(2)}) copy-start(f32[1,6144]{1,0:T(1,128)} %get-tuple-element.51) | copy-start | bytes 73732
  158.7 43.5 %copy-start.4 = (f32[1,6144]{1,0:T(1,128)S(1)}, f32[1,6144]{1,0:T(1,128)}, u32[]{:S(2)}) copy-start(f32[1,6144]{1,0:T(1,128)} %get-tuple-element.52) | copy-start | bytes 73732
  158.7 43.5 %copy-start.5 = (f32[1,6144]{1,0:T(1,128)S(1)}, f32[1,6144]{1,0:T(1,128)}, u32[]{:S(2)}) copy-start(f32[1,6144]{1,0:T(1,128)} %get-tuple-element.53) | copy-start | bytes 73732
  158.7 43.5 %copy-start.6 = (f32[1,6144]{1,0:T(1,128)S(1)}, f32[1,6144]{1,0:T(1,128)}, u32[]{:S(2)}) copy-start(f32[1,6144]{1,0:T(1,128)} %get-tuple-element.54) | copy-start | bytes 73732
  158.7 43.5 %copy-start.7 = (f32[1,6144]{1,0:T(1,128)S(1)}, f32[1,6144]{1,0:T(1,128)}, u32[]{:S(2)}) copy-start(f32[1,6144]{1,0:T(1,128)} %get-tuple-element.55) | copy-start | bytes 73732
  158.7 43.5 %copy-start.8 = (f32[1,6144]{1,0:T(1,128)S(1)}, f32[1,6144]{1,0:T(1,128)}, u32[]{:S(2)}) copy-start(f32[1,6144]{1,0:T(1,128)} %get-tuple-element.56) | copy-start | bytes 73732
  158.7 43.5 %copy-start.9 = (f32[1,6144]{1,0:T(1,128)S(1)}, f32[1,6144]{1,0:T(1,128)}, u32[]{:S(2)}) copy-start(f32[1,6144]{1,0:T(1,128)} %get-tuple-element.57) | copy-start | bytes 73732
  158.7 43.5 %copy-start.10 = (f32[1,6144]{1,0:T(1,128)S(1)}, f32[1,6144]{1,0:T(1,128)}, u32[]{:S(2)}) copy-start(f32[1,6144]{1,0:T(1,128)} %get-tuple-element.58) | copy-start | bytes 73732
  158.7 43.5 %copy-start.11 = (f32[1,6144]{1,0:T(1,128)S(1)}, f32[1,6144]{1,0:T(1,128)}, u32[]{:S(2)}) copy-start(f32[1,6144]{1,0:T(1,128)} %get-tuple-element.59) | copy-start | bytes 73732
  158.7 43.5 %copy-start.12 = (f32[1,6144]{1,0:T(1,128)S(1)}, f32[1,6144]{1,0:T(1,128)}, u32[]{:S(2)}) copy-start(f32[1,6144]{1,0:T(1,128)} %get-tuple-element.60) | copy-start | bytes 73732
  158.7 43.5 %copy-start.13 = (f32[1,6144]{1,0:T(1,128)S(1)}, f32[1,6144]{1,0:T(1,128)}, u32[]{:S(2)}) copy-start(f32[1,6144]{1,0:T(1,128)} %get-tuple-element.61) | copy-start | bytes 73732
  158.8 43.5 %copy-start.14 = (f32[1,6144]{1,0:T(1,128)S(1)}, f32[1,6144]{1,0:T(1,128)}, u32[]{:S(2)}) copy-start(f32[1,6144]{1,0:T(1,128)} %get-tuple-element.62) | copy-start | bytes 73732
  158.8 43.5 %copy-start.15 = (f32[1,6144]{1,0:T(1,128)S(1)}, f32[1,6144]{1,0:T(1,128)}, u32[]{:S(2)}) copy-start(f32[1,6144]{1,0:T(1,128)} %get-tuple-element.63) | copy-start | bytes 73732
  158.8 43.5 %copy-start.16 = (f32[1,6144]{1,0:T(1,128)S(1)}, f32[1,6144]{1,0:T(1,128)}, u32[]{:S(2)}) copy-start(f32[1,6144]{1,0:T(1,128)} %get-tuple-element.64) | copy-start | bytes 73732
  158.8 43.5 %copy-start.17 = (f32[1,6144]{1,0:T(1,128)S(1)}, f32[1,6144]{1,0:T(1,128)}, u32[]{:S(2)}) copy-start(f32[1,6144]{1,0:T(1,128)} %get-tuple-element.65) | copy-start | bytes 73732
  193.2 97.2 %all-to-all-start = ((f32[64,34,96]{2,1,0:T(8,128)}), f32[64,34,96]{2,1,0:T(8,128)S(1)}, u32[]{:S(2)}, u32[]{:S(2)}) async-start(f32[64,34,96]{2,1,0:T(8,128)} %bitcast.50), calls=%async_computation | async-start | bytes 2621440 | tf_op jit(solution)/shard_map/all_to_all | solution.py:110

commit v2 on v0

v2 whole, which is shorter than its diff:
```python
import functools
import math

import jax
import jax.numpy as jnp
from jax import lax
from jax.experimental import pallas as pl
from jax.experimental.pallas import tpu as pltpu
from jax.sharding import PartitionSpec as P

SIDE = 4
LANES = 128
SUB = 8
PAD = 16
F32 = jnp.float32


def shifted(axis_stride, step):
    pairs = []
    for source in range(SIDE**3):
        at = (source // axis_stride) % SIDE
        pairs.append((source, source + ((at + step) % SIDE - at) * axis_stride))
    return pairs


def gather_stage(block, axis_stride):
    at = (lax.axis_index("shard") // axis_stride) % SIDE
    came = [block] + [
        lax.ppermute(block, "shard", shifted(axis_stride, step)) for step in range(1, SIDE)
    ]
    return [lax.select_n((at - slot) % SIDE, *came) for slot in range(SIDE)]


def gather_channels(packed):
    group = jnp.concatenate(gather_stage(packed, 1), axis=1)
    column = jnp.stack(gather_stage(group, 16), 0)
    return jnp.stack(gather_stage(column, 4), 1).reshape((SIDE * SIDE,) + group.shape)


def bcast_row(ref, row):
    return jnp.broadcast_to(ref[pl.ds(row, 1), :], (SUB, LANES))


def forward_and_kernel_grad(
    taps, x_hbm, ct_hbm, p_ref, act_hbm, gc_hbm, gr_ref,
    xb, cb, ab, xs, cv, gn, gc, pf, st, s1, s2, row_a, row_b, x_sem, c_sem, a_sem, g_sem,
):
    frames, width = xb.shape
    tiles = width // LANES
    rows = frames // SUB
    chunks = x_sem.shape[0]
    per_chunk = tiles // chunks
    per_group = p_ref.shape[2] // LANES
    block = 8

    def lanes_of(tile):
        return pl.ds(pl.multiple_of(tile * LANES, LANES), LANES)

    def chunk_lanes(chunk):
        wide = per_chunk * LANES
        return pl.ds(pl.multiple_of(chunk * wide, wide), wide)

    def x_copy(chunk):
        return pltpu.make_async_copy(
            x_hbm.at[:, chunk_lanes(chunk)], xb.at[:, chunk_lanes(chunk)], x_sem.at[chunk]
        )

    def c_copy(chunk):
        return pltpu.make_async_copy(
            ct_hbm.at[:, chunk_lanes(chunk)], cb.at[:, chunk_lanes(chunk)], c_sem.at[chunk]
        )

    def a_copy(chunk):
        return pltpu.make_async_copy(
            ab.at[:, chunk_lanes(chunk)], act_hbm.at[:, chunk_lanes(chunk)], a_sem.at[chunk]
        )

    def g_copy(chunk):
        at = pl.ds(chunk * per_chunk, per_chunk)
        return pltpu.make_async_copy(gc.at[at], gc_hbm.at[at], g_sem.at[chunk])

    for chunk in range(chunks):
        x_copy(chunk).start()
    for chunk in range(chunks):
        c_copy(chunk).start()

    def load_params(tile):
        group = tile // per_group
        inside = tile - group * per_group
        lanes = pl.ds(pl.multiple_of(inside * LANES, LANES), LANES)
        pf[...] = p_ref[group, :, lanes].astype(F32)

    zero = jnp.zeros((SUB, LANES), F32)
    s1[...] = jnp.zeros_like(s1)
    s2[...] = jnp.zeros_like(s2)

    def conv_tile(tile, _):
        load_params(tile)
        for edge in (0, SUB, PAD + frames, PAD + frames + SUB):
            xs[tile, pl.ds(edge, SUB), :] = zero
            gc[tile, pl.ds(edge, SUB), :] = zero
        xs[tile, pl.ds(PAD, frames), :] = xb[:, lanes_of(tile)].astype(F32)
        weights = [bcast_row(pf, j) for j in range(taps)]
        bias = bcast_row(pf, taps)
        for r0 in range(0, rows, block):
            acc = [bias] * block
            for phase in range(SUB):
                depth = len(range(phase, taps, SUB))
                for i in range(block + depth - 1):
                    value = xs[tile, pl.ds(SUB * (r0 + i) + phase + 1, SUB), :]
                    for q in range(depth):
                        if 0 <= i - q < block:
                            acc[i - q] = acc[i - q] + value * weights[phase + SUB * q]
            for b in range(block):
                at = pl.ds(SUB * (r0 + b), SUB)
                cv[tile, at, :] = acc[b]
                s1[at, :] += acc[b]
        return 0

    def conv_chunk(chunk, _):
        x_copy(chunk).wait()
        lax.fori_loop(chunk * per_chunk, (chunk + 1) * per_chunk, conv_tile, 0)
        return 0

    lax.fori_loop(0, chunks, conv_chunk, 0)

    row_a[...] = jnp.broadcast_to(
        jnp.sum(s1[...], axis=1, keepdims=True) * (1.0 / width), s1.shape
    )

    def var_tile(tile, _):
        for r in range(rows):
            at = pl.ds(SUB * r, SUB)
            off = cv[tile, at, :] - row_a[at, :]
            s2[at, :] += off * off
        return 0

    lax.fori_loop(0, tiles, var_tile, 0)
    row_b[...] = jnp.broadcast_to(
        lax.rsqrt(jnp.sum(s2[...], axis=1, keepdims=True) * (1.0 / width) + 1e-05), s2.shape
    )
    s1[...] = jnp.zeros_like(s1)
    s2[...] = jnp.zeros_like(s2)

    def act_tile(tile, _):
        load_params(tile)
        gain = bcast_row(pf, taps + 1)
        shift = bcast_row(pf, taps + 2)
        sum_gain, sum_shift = zero, zero
        for r0 in range(0, rows, 4):
            outs = []
            span = pl.ds(SUB * r0, SUB * 4)
            upstream = cb[span, lanes_of(tile)].astype(F32)
            for b in range(4):
                at = pl.ds(SUB * (r0 + b), SUB)
                normed = (cv[tile, at, :] - row_a[at, :]) * row_b[at, :]
                affine = gain * normed + shift
                squash = 0.5 * jnp.tanh(0.5 * affine) + 0.5
                act = affine * squash
                outs.append(act)
                ga = upstream[SUB * b : SUB * (b + 1)] * (squash * (1.0 + (affine - act)))
                sum_gain = sum_gain + ga * normed
                sum_shift = sum_shift + ga
                scaled = ga * gain
                cv[tile, at, :] = normed
                gn[tile, at, :] = scaled
                s1[at, :] += scaled
                s2[at, :] += scaled * normed
            ab[span, lanes_of(tile)] = jnp.concatenate(outs, 0).astype(ab.dtype)
        st[tile, pl.ds(taps + 1, 1), :] = jnp.sum(sum_gain, axis=0, keepdims=True)
        st[tile, pl.ds(taps + 2, 1), :] = jnp.sum(sum_shift, axis=0, keepdims=True)
        return 0

    def act_chunk(chunk, _):
        c_copy(chunk).wait()
        lax.fori_loop(chunk * per_chunk, (chunk + 1) * per_chunk, act_tile, 0)
        a_copy(chunk).start()
        return 0

    lax.fori_loop(0, chunks, act_chunk, 0)

    mean_gn = jnp.sum(s1[...], axis=1, keepdims=True) * (1.0 / width)
    mean_gnn = jnp.sum(s2[...], axis=1, keepdims=True) * (1.0 / width)
    s1[...] = jnp.broadcast_to(mean_gn, s1.shape)
    s2[...] = jnp.broadcast_to(mean_gnn, s2.shape)

    def grad_tile(tile, _):
        acc = [zero] * taps
        total = zero
        for r0 in range(0, rows, block):
            held = []
            for b in range(block):
                at = pl.ds(SUB * (r0 + b), SUB)
                grad = row_b[at, :] * (
                    gn[tile, at, :] - s1[at, :] - cv[tile, at, :] * s2[at, :]
                )
                gc[tile, pl.ds(PAD + SUB * (r0 + b), SUB), :] = grad
                total = total + grad
                held.append(grad)
            for phase in range(SUB):
                depth = len(range(phase, taps, SUB))
                for i in range(block + depth - 1):
                    value = xs[tile, pl.ds(SUB * (r0 + i) + phase + 1, SUB), :]
                    for q in range(depth):
                        if 0 <= i - q < block:
                            acc[phase + SUB * q] = acc[phase + SUB * q] + value * held[i - q]
        for j in range(taps):
            st[tile, pl.ds(j, 1), :] = jnp.sum(acc[j], axis=0, keepdims=True)
        st[tile, pl.ds(taps, 1), :] = jnp.sum(total, axis=0, keepdims=True)
        return 0

    def grad_chunk(chunk, _):
        lax.fori_loop(chunk * per_chunk, (chunk + 1) * per_chunk, grad_tile, 0)
        g_copy(chunk).start()
        return 0

    lax.fori_loop(0, chunks, grad_chunk, 0)

    def out_group(group, _):
        whole = jnp.concatenate(
            [st[group * per_group + u, :, :] for u in range(per_group)], axis=1
        )
        part = per_group * LANES // SIDE
        for a in range(SIDE):
            gr_ref[group * SIDE + a, :, :] = whole[:, a * part : (a + 1) * part]
        return 0

    lax.fori_loop(0, tiles // per_group, out_group, 0)
    for chunk in range(chunks):
        a_copy(chunk).wait()
        g_copy(chunk).wait()


def input_grad(taps, gc_hbm, p_ref, gi_hbm, gc, gb, pf, g_sem, o_sem):
    frames, width = gb.shape
    tiles = width // LANES
    rows = frames // SUB
    chunks = g_sem.shape[0]
    per_chunk = tiles // chunks
    per_group = p_ref.shape[2] // LANES
    block = 8

    def g_copy(chunk):
        at = pl.ds(chunk * per_chunk, per_chunk)
        return pltpu.make_async_copy(gc_hbm.at[at], gc.at[at], g_sem.at[chunk])

    def o_copy(chunk):
        wide = per_chunk * LANES
        at = pl.ds(pl.multiple_of(chunk * wide, wide), wide)
        return pltpu.make_async_copy(gb.at[:, at], gi_hbm.at[:, at], o_sem.at[chunk])

    for chunk in range(chunks):
        g_copy(chunk).start()

    def tile_step(tile, _):
        group = tile // per_group
        inside = tile - group * per_group
        lanes = pl.ds(pl.multiple_of(inside * LANES, LANES), LANES)
        pf[...] = p_ref[group, :, lanes].astype(F32)
        weights = [bcast_row(pf, taps - 1 - j) for j in range(taps)]
        for r0 in range(0, rows, block):
            acc = [None] * block
            for phase in range(SUB):
                depth = len(range(phase, taps, SUB))
                for i in range(block + depth - 1):
                    value = gc[tile, pl.ds(SUB * (r0 + i) + phase + 1, SUB), :]
                    for q in range(depth):
                        b = i - q
                        if 0 <= b < block:
                            term = value * weights[phase + SUB * q]
                            acc[b] = term if acc[b] is None else acc[b] + term
            at = pl.ds(pl.multiple_of(tile * LANES, LANES), LANES)
            gb[pl.ds(SUB * r0, SUB * block), at] = jnp.concatenate(acc, 0).astype(gb.dtype)
        return 0

    def chunk_step(chunk, _):
        g_copy(chunk).wait()
        lax.fori_loop(chunk * per_chunk, (chunk + 1) * per_chunk, tile_step, 0)
        o_copy(chunk).start()
        return 0

    lax.fori_loop(0, chunks, chunk_step, 0)
    for chunk in range(chunks):
        o_copy(chunk).wait()


ANY = pl.BlockSpec(memory_space=pl.ANY)
HELD = pl.BlockSpec(memory_space=pltpu.VMEM)


def run_first(x, cotangent, params, taps):
    frames, width = x.shape
    tiles = width // LANES
    chunks = 8
    rows = params.shape[1]
    padded = frames + 2 * PAD
    whole = (tiles, frames, LANES)
    return pl.pallas_call(
        functools.partial(forward_and_kernel_grad, taps),
        out_shape=(
            jax.ShapeDtypeStruct((frames, width), jnp.bfloat16),
            jax.ShapeDtypeStruct((tiles, padded, LANES), F32),
            jax.ShapeDtypeStruct((SIDE**3, rows, width // SIDE**3), F32),
        ),
        in_specs=[ANY, ANY, HELD],
        out_specs=(ANY, ANY, HELD),
        scratch_shapes=[
            pltpu.VMEM((frames, width), jnp.bfloat16),
            pltpu.VMEM((frames, width), jnp.bfloat16),
            pltpu.VMEM((frames, width), jnp.bfloat16),
            pltpu.VMEM((tiles, padded, LANES), F32),
            pltpu.VMEM(whole, F32),
            pltpu.VMEM(whole, F32),
            pltpu.VMEM((tiles, padded, LANES), F32),
            pltpu.VMEM((rows, LANES), F32),
            pltpu.VMEM((tiles, rows, LANES), F32),
            pltpu.VMEM((frames, LANES), F32),
            pltpu.VMEM((frames, LANES), F32),
            pltpu.VMEM((frames, LANES), F32),
            pltpu.VMEM((frames, LANES), F32),
            pltpu.SemaphoreType.DMA((chunks,)),
            pltpu.SemaphoreType.DMA((chunks,)),
            pltpu.SemaphoreType.DMA((chunks,)),
            pltpu.SemaphoreType.DMA((chunks,)),
        ],
        compiler_params=pltpu.CompilerParams(vmem_limit_bytes=56 << 20),
        cost_estimate=pl.CostEstimate(
            flops=4 * taps * frames * width, bytes_accessed=20 * frames * width, transcendentals=0
        ),
        name="forward_and_kernel_grad",
    )(x, cotangent, params)


def run_second(grad_conv, params, taps, frames, width):
    tiles = width // LANES
    chunks = 8
    return pl.pallas_call(
        functools.partial(input_grad, taps),
        out_shape=jax.ShapeDtypeStruct((frames, width), jnp.bfloat16),
        in_specs=[ANY, HELD],
        out_specs=ANY,
        scratch_shapes=[
            pltpu.VMEM(grad_conv.shape, F32),
            pltpu.VMEM((frames, width), jnp.bfloat16),
            pltpu.VMEM((params.shape[1], LANES), F32),
            pltpu.SemaphoreType.DMA((chunks,)),
            pltpu.SemaphoreType.DMA((chunks,)),
        ],
        compiler_params=pltpu.CompilerParams(vmem_limit_bytes=56 << 20),
        cost_estimate=pl.CostEstimate(
            flops=2 * taps * frames * width, bytes_accessed=6 * frames * width, transcendentals=0
        ),
        name="input_grad",
    )(grad_conv, params)


def per_device(conv_input, cotangent, kernel, conv_bias, ln_gain, ln_bias):
    taps = kernel.shape[0]
    clips, frames, width = conv_input.shape
    packed = jnp.concatenate([kernel, conv_bias[None], ln_gain[None], ln_bias[None]], 0)
    params = gather_channels(packed)
    activated, grad_conv, pieces = run_first(conv_input[0], cotangent[0], params, taps)
    came = lax.all_to_all(pieces, "shard", 0, 0)
    grad_input = run_second(grad_conv, params, taps, frames, width)
    share_sum = jnp.sum(came, axis=0)
    summed = jnp.sum(lax.all_gather(share_sum, "rep", axis=0), axis=0)
    count = clips * frames * lax.axis_size("rep") * lax.axis_size("shard")
    grads = summed * (1.0 / math.sqrt(count))
    return (
        activated[None], grad_input[None],
        grads[:taps], grads[taps], grads[taps + 1], grads[taps + 2],
    )


def solution(mesh):
    data = P(("rep", "shard"), None, None)
    wide = P(None, "shard")
    narrow = P("shard")
    return jax.shard_map(
        per_device,
        mesh=mesh,
        in_specs=(data, data, wide, narrow, narrow, narrow),
        out_specs=(data, data, wide, narrow, narrow, narrow),
        check_vma=False,
    )
```

time: 572 us -> 129 us (0.23)
  other arithmetic: 179 us -> 2.88 us
  blocking collectives: 183 us -> 15 us
  waiting for transfers between devices: 182 us -> 21.3 us
  Pallas kernels: 0 us -> 60.1 us
  starting transfers between devices: 0.04 us -> 26.2 us
  between operations: 14.3 us -> 0.71 us
  local copies, waits for them, and re-layouts: 13.4 us -> 1.98 us
    unnamed x2 -> x0, waiting for transfers between devices: 182 us -> none
    all_gather x1, blocking collectives: 171 us -> 15 us  [per_device(): summed = jnp.sum(lax.all_gather(share_sum, 'rep', axis=0), axis=0)]
    convert_element_type x3 -> x0, other arithmetic: 93.6 us -> none  [the longest x1 88 us: backward_part(): return (grad_input.astype(jnp.bfloat16), terms)]
    reduce_sum x8 -> x2, other arithmetic: 84.3 us -> 0.14 us  [the longest x1 0.12 us: per_device(): share_sum = jnp.sum(came, axis=0)]
    pallas_call x0 -> x2, Pallas kernels: none -> 60.1 us  [the longest x1 43.4 us: run_first(): pl.pallas_call(functools.partial(forward_and_kernel_grad, taps), out_shap...]
    ppermute x0 -> x9, starting transfers between devices: none -> 19 us  [gather_stage(): lax.ppermute(block, 'shard', shifted(axis_stride, step))]
    psum x1 -> x0, blocking collectives: 11.9 us -> none  [per_device(): summed = lax.psum(share_sum, 'rep')]
    ppermute x0 -> x9, waiting for transfers between devices: none -> 11.3 us  [gather_stage(): lax.ppermute(block, 'shard', shifted(axis_stride, step))]
  transfers between devices with their start and end apart: 1 -> 10, of which waited for: 1 -> 8; matrix products, arithmetic and copies ran while one was open for 15% -> 0% of each run, Pallas kernels for 0% -> 13%
where the time goes in v2:
time: 129 us; the launch traced here: 128 us
  Pallas kernels  60.1 us (47%)
  starting transfers between devices  26.2 us (20%)
  waiting for transfers between devices  21.3 us (17%)
  blocking collectives  15 us (12%)
  other arithmetic  2.88 us (2%)
  local copies, waits for them, and re-layouts  1.98 us (2%)
    pallas_call x1, Pallas kernels, run_first(): pl.pallas_call(functools.partial(forward_and_kernel_grad, taps), out_shap...  43.4 us
    ppermute x9, starting transfers between devices, gather_stage(): lax.ppermute(block, 'shard', shifted(axis_stride, step))  19 us
    pallas_call x1, Pallas kernels, run_second(): pl.pallas_call(functools.partial(input_grad, taps), out_shape=jax.ShapeDt...  16.7 us
    all_gather x1, blocking collectives, per_device(): summed = jnp.sum(lax.all_gather(share_sum, 'rep', axis=0), axis=0)  15 us
    ppermute x9, waiting for transfers between devices, gather_stage(): lax.ppermute(block, 'shard', shifted(axis_stride, step))  11.3 us
    all_to_all x1, waiting for transfers between devices, per_device(): came = lax.all_to_all(pieces, 'shard', 0, 0)  10 us
    all_to_all x1, starting transfers between devices, per_device(): came = lax.all_to_all(pieces, 'shard', 0, 0)  7.21 us
  transfers between devices with their start and end apart: 10, of which 8 were waited for; matrix products, arithmetic and copies ran while one was open for 0% of the time, Pallas kernels for 13%

profile of v2, /device:TPU:1, one launch (start us, length us, event | category | flops | bytes accessed | tf_op | source)
XLA Modules:
  0.0 128.2 jit_solution(51458575978133140)
XLA Ops:
  0.6 0.8 pad_maximum_fusion.3
  1.4 3.7 %collective-permute-start.1 = (bf16[34,96]{1,0:T(8,128)(2,1)S(1)}, bf16[34,96]{1,0:T(8,128)(2,1)S(1)}, u32[]{:S(2)}, u32[]{:S(2)}) collective-permute-start(bf16[34,96]{1,0:T(8,128)(2,1)S(1)} %pad_maximum_fusion.3), channel_id=1, source_target_pairs={{0,2},{1,3},{2,0},{3,1},{4,6},{5,7},{6,4},{7,5},{8,10},{9,11},{10,... | collective-permute-start | bytes 19592 | tf_op jit(solution)/shard_map/ppermute | solution.py:29
  5.1 0.9 collective-permute-start.2
  5.9 0.6 collective-permute-start
  6.5 0.0 collective-permute-done.1
  6.5 1.1 collective-permute-done.2
  7.7 2.0 %collective-permute-done = bf16[34,96]{1,0:T(8,128)(2,1)S(1)} collective-permute-done((bf16[34,96]{1,0:T(8,128)(2,1)S(1)}, bf16[34,96]{1,0:T(8,128)(2,1)S(1)}, u32[]{:S(2)}, u32[]{:S(2)}) %collective-permute-start) | collective-permute-done | bytes 6560 | tf_op jit(solution)/shard_map/ppermute | solution.py:29
  9.6 0.8 select_select_fusion.2
  10.4 0.8 select_select_fusion.3
  11.2 0.1 pad_maximum_fusion.2
  11.3 7.0 %collective-permute-start.4 = (bf16[34,384]{1,0:T(8,128)(2,1)S(1)}, bf16[34,384]{1,0:T(8,128)(2,1)S(1)}, u32[]{:S(2)}, u32[]{:S(2)}) collective-permute-start(bf16[34,384]{1,0:T(8,128)(2,1)S(1)} %pad_maximum_fusion.2), channel_id=1, source_target_pairs={{0,32},{1,33},{2,34},{3,35},{4,36},{5,37},{6,38},{7,39},{8,40},{9,... | collective-permute-start | bytes 78344 | tf_op jit(solution)/shard_map/ppermute | solution.py:29
  18.3 0.0 collective-permute-start.5
  18.3 2.4 %collective-permute-start.3 = (bf16[34,384]{1,0:T(8,128)(2,1)S(1)}, bf16[34,384]{1,0:T(8,128)(2,1)S(1)}, u32[]{:S(2)}, u32[]{:S(2)}) collective-permute-start(bf16[34,384]{1,0:T(8,128)(2,1)S(1)} %pad_maximum_fusion.2), channel_id=1, source_target_pairs={{0,16},{1,17},{2,18},{3,19},{4,20},{5,21},{6,22},{7,23},{8,24},{9,... | collective-permute-start | bytes 78344 | tf_op jit(solution)/shard_map/ppermute | solution.py:29
  20.6 0.0 collective-permute-done.4
  20.6 1.6 %collective-permute-done.5 = bf16[34,384]{1,0:T(8,128)(2,1)S(1)} collective-permute-done((bf16[34,384]{1,0:T(8,128)(2,1)S(1)}, bf16[34,384]{1,0:T(8,128)(2,1)S(1)}, u32[]{:S(2)}, u32[]{:S(2)}) %collective-permute-start.5) | collective-permute-done | bytes 26144 | tf_op jit(solution)/shard_map/ppermute | solution.py:29
  22.2 1.0 collective-permute-done.3
  23.2 0.1 select_bitcast_fusion.7
  23.4 3.0 %collective-permute-start.7 = (bf16[4,34,384]{2,1,0:T(8,128)(2,1)S(1)}, bf16[4,34,384]{2,1,0:T(8,128)(2,1)S(1)}, u32[]{:S(2)}, u32[]{:S(2)}) collective-permute-start(bf16[4,34,384]{2,1,0:T(8,128)(2,1)S(1)} %pad_maximum_fusion.1), channel_id=1, source_target_pairs={{0,8},{1,9},{2,10},{3,11},{4,12},{5,13},{6,14},{7,15},{8,0},{9,1},... | collective-permute-start | bytes 313352 | tf_op jit(solution)/shard_map/ppermute | solution.py:29
  26.4 0.8 collective-permute-start.8
  27.2 0.7 collective-permute-start.6
  27.9 0.9 collective-permute-done.7
  28.7 1.7 %collective-permute-done.8 = bf16[4,34,384]{2,1,0:T(8,128)(2,1)S(1)} collective-permute-done((bf16[4,34,384]{2,1,0:T(8,128)(2,1)S(1)}, bf16[4,34,384]{2,1,0:T(8,128)(2,1)S(1)}, u32[]{:S(2)}, u32[]{:S(2)}) %collective-permute-start.8) | collective-permute-done | bytes 104480 | tf_op jit(solution)/shard_map/ppermute | solution.py:29
  30.4 3.1 %collective-permute-done.6 = bf16[4,34,384]{2,1,0:T(8,128)(2,1)S(1)} collective-permute-done((bf16[4,34,384]{2,1,0:T(8,128)(2,1)S(1)}, bf16[4,34,384]{2,1,0:T(8,128)(2,1)S(1)}, u32[]{:S(2)}, u32[]{:S(2)}) %collective-permute-start.6) | collective-permute-done | bytes 104480 | tf_op jit(solution)/shard_map/ppermute | solution.py:29
  33.4 0.1 select_bitcast_fusion.2
  33.5 0.1 select_bitcast_fusion.3
  33.6 0.1 pad_maximum_fusion
  33.7 0.9 copy.13
  34.5 43.4 %forward_and_kernel_grad.1 = (bf16[256,6144]{1,0:T(8,128)(2,1)}, f32[48,288,128]{2,1,0:T(8,128)}, f32[64,34,96]{2,1,0:T(8,128)}) custom-call(bf16[256,6144]{1,0:T(8,128)(2,1)} %bitcast.33, bf16[256,6144]{1,0:T(8,128)(2,1)} %bitcast.34, bf16[16,34,384]{2,1,0:T(8,128)(2,1)} %bitcast.31), custom_call_target="tpu_custom_call" | custom-call | flops 195035136 | bytes 31457280 | tf_op jit(solution)/shard_map/forward_and_kernel_grad/pallas_call | solution.py:298
  77.9 7.2 %all-to-all-start = ((f32[64,34,96]{2,1,0:T(8,128)}), f32[64,34,96]{2,1,0:T(8,128)S(1)}, u32[]{:S(2)}, u32[]{:S(2)}) async-start(f32[64,34,96]{2,1,0:T(8,128)} %get-tuple-element.11), calls=%async_computation | async-start | bytes 2621440 | tf_op jit(solution)/shard_map/all_to_all | solution.py:363
  85.1 16.7 %input_grad.1 = bf16[256,6144]{1,0:T(8,128)(2,1)} custom-call(f32[48,288,128]{2,1,0:T(8,128)} %get-tuple-element.10.gc_hbm, bf16[16,34,384]{2,1,0:T(8,128)(2,1)} %bitcast.32), custom_call_target="tpu_custom_call" | custom-call | flops 97517568 | bytes 9437184 | tf_op jit(solution)/shard_map/input_grad/pallas_call | solution.py:337
  101.9 10.0 %all-to-all-done = f32[64,34,96]{2,1,0:T(8,128)S(1)} async-done(((f32[64,34,96]{2,1,0:T(8,128)}), f32[64,34,96]{2,1,0:T(8,128)S(1)}, u32[]{:S(2)}, u32[]{:S(2)}) %all-to-all-start) | async-done | bytes 835616 | tf_op jit(solution)/shard_map/all_to_all | solution.py:363
  111.9 0.1 reduce_sum.18
  112.0 15.0 %all-gather.1 = f32[4,34,96]{2,1,0:T(8,128)S(1)} all-gather(f32[1,34,96]{2,1,0:T(8,128)S(1)} %bitcast.36), channel_id=2, replica_groups=mesh['rep'=4,'shard'=64] {'rep'}, dimensions={0}, use_global_device_ids=true | all-gather | bytes 65280 | tf_op jit(solution)/shard_map/all_gather | solution.py:366
  127.1 0.5 slice_bitcast_fusion
  127.6 0.6 slice.16
  (3 shorter events, 0.0 us)
Async XLA Ops:
  1.4 5.1 %collective-permute-start.1 = (bf16[34,96]{1,0:T(8,128)(2,1)S(1)}, bf16[34,96]{1,0:T(8,128)(2,1)S(1)}, u32[]{:S(2)}, u32[]{:S(2)}) collective-permute-start(bf16[34,96]{1,0:T(8,128)(2,1)S(1)} %pad_maximum_fusion.3), channel_id=1, source_target_pairs={{0,2},{1,3},{2,0},{3,1},{4,6},{5,7},{6,4},{7,5},{8,10},{9,11},{10,... | collective-permute-start | bytes 19592 | tf_op jit(solution)/shard_map/ppermute | solution.py:29
  5.1 2.6 %collective-permute-start.2 = (bf16[34,96]{1,0:T(8,128)(2,1)S(1)}, bf16[34,96]{1,0:T(8,128)(2,1)S(1)}, u32[]{:S(2)}, u32[]{:S(2)}) collective-permute-start(bf16[34,96]{1,0:T(8,128)(2,1)S(1)} %pad_maximum_fusion.3), channel_id=1, source_target_pairs={{0,3},{1,0},{2,1},{3,2},{4,7},{5,4},{6,5},{7,6},{8,11},{9,8},{10,9... | collective-permute-start | bytes 19592 | tf_op jit(solution)/shard_map/ppermute | solution.py:29
  5.9 3.7 %collective-permute-start = (bf16[34,96]{1,0:T(8,128)(2,1)S(1)}, bf16[34,96]{1,0:T(8,128)(2,1)S(1)}, u32[]{:S(2)}, u32[]{:S(2)}) collective-permute-start(bf16[34,96]{1,0:T(8,128)(2,1)S(1)} %pad_maximum_fusion.3), channel_id=1, source_target_pairs={{0,1},{1,2},{2,3},{3,0},{4,5},{5,6},{6,7},{7,4},{8,9},{9,10},{10,1... | collective-permute-start | bytes 19592 | tf_op jit(solution)/shard_map/ppermute | solution.py:29
  11.3 9.4 %collective-permute-start.4 = (bf16[34,384]{1,0:T(8,128)(2,1)S(1)}, bf16[34,384]{1,0:T(8,128)(2,1)S(1)}, u32[]{:S(2)}, u32[]{:S(2)}) collective-permute-start(bf16[34,384]{1,0:T(8,128)(2,1)S(1)} %pad_maximum_fusion.2), channel_id=1, source_target_pairs={{0,32},{1,33},{2,34},{3,35},{4,36},{5,37},{6,38},{7,39},{8,40},{9,... | collective-permute-start | bytes 78344 | tf_op jit(solution)/shard_map/ppermute | solution.py:29
  18.3 3.9 %collective-permute-start.5 = (bf16[34,384]{1,0:T(8,128)(2,1)S(1)}, bf16[34,384]{1,0:T(8,128)(2,1)S(1)}, u32[]{:S(2)}, u32[]{:S(2)}) collective-permute-start(bf16[34,384]{1,0:T(8,128)(2,1)S(1)} %pad_maximum_fusion.2), channel_id=1, source_target_pairs={{0,48},{1,49},{2,50},{3,51},{4,52},{5,53},{6,54},{7,55},{8,56},{9,... | collective-permute-start | bytes 78344 | tf_op jit(solution)/shard_map/ppermute | solution.py:29
  18.3 5.0 %collective-permute-start.3 = (bf16[34,384]{1,0:T(8,128)(2,1)S(1)}, bf16[34,384]{1,0:T(8,128)(2,1)S(1)}, u32[]{:S(2)}, u32[]{:S(2)}) collective-permute-start(bf16[34,384]{1,0:T(8,128)(2,1)S(1)} %pad_maximum_fusion.2), channel_id=1, source_target_pairs={{0,16},{1,17},{2,18},{3,19},{4,20},{5,21},{6,22},{7,23},{8,24},{9,... | collective-permute-start | bytes 78344 | tf_op jit(solution)/shard_map/ppermute | solution.py:29
  23.4 5.3 %collective-permute-start.7 = (bf16[4,34,384]{2,1,0:T(8,128)(2,1)S(1)}, bf16[4,34,384]{2,1,0:T(8,128)(2,1)S(1)}, u32[]{:S(2)}, u32[]{:S(2)}) collective-permute-start(bf16[4,34,384]{2,1,0:T(8,128)(2,1)S(1)} %pad_maximum_fusion.1), channel_id=1, source_target_pairs={{0,8},{1,9},{2,10},{3,11},{4,12},{5,13},{6,14},{7,15},{8,0},{9,1},... | collective-permute-start | bytes 313352 | tf_op jit(solution)/shard_map/ppermute | solution.py:29
  26.4 4.0 %collective-permute-start.8 = (bf16[4,34,384]{2,1,0:T(8,128)(2,1)S(1)}, bf16[4,34,384]{2,1,0:T(8,128)(2,1)S(1)}, u32[]{:S(2)}, u32[]{:S(2)}) collective-permute-start(bf16[4,34,384]{2,1,0:T(8,128)(2,1)S(1)} %pad_maximum_fusion.1), channel_id=1, source_target_pairs={{0,12},{1,13},{2,14},{3,15},{4,0},{5,1},{6,2},{7,3},{8,4},{9,5},{1... | collective-permute-start | bytes 313352 | tf_op jit(solution)/shard_map/ppermute | solution.py:29
  27.2 6.3 %collective-permute-start.6 = (bf16[4,34,384]{2,1,0:T(8,128)(2,1)S(1)}, bf16[4,34,384]{2,1,0:T(8,128)(2,1)S(1)}, u32[]{:S(2)}, u32[]{:S(2)}) collective-permute-start(bf16[4,34,384]{2,1,0:T(8,128)(2,1)S(1)} %pad_maximum_fusion.1), channel_id=1, source_target_pairs={{0,4},{1,5},{2,6},{3,7},{4,8},{5,9},{6,10},{7,11},{8,12},{9,13},{1... | collective-permute-start | bytes 313352 | tf_op jit(solution)/shard_map/ppermute | solution.py:29
  77.9 34.0 %all-to-all-start = ((f32[64,34,96]{2,1,0:T(8,128)}), f32[64,34,96]{2,1,0:T(8,128)S(1)}, u32[]{:S(2)}, u32[]{:S(2)}) async-start(f32[64,34,96]{2,1,0:T(8,128)} %get-tuple-element.11), calls=%async_computation | async-start | bytes 2621440 | tf_op jit(solution)/shard_map/all_to_all | solution.py:363

commit v3 on v2

--- a/solution.py
+++ b/solution.py
@@ -13,6 +13,7 @@
 SUB = 8
 PAD = 16
 F32 = jnp.float32
+MAIN = 32
 
 
 def shifted(axis_stride, step):
@@ -28,13 +29,20 @@
     came = [block] + [
         lax.ppermute(block, "shard", shifted(axis_stride, step)) for step in range(1, SIDE)
     ]
-    return [lax.select_n((at - slot) % SIDE, *came) for slot in range(SIDE)]
+    return came, [lax.select_n((at - slot) % SIDE, *came) for slot in range(SIDE)]
 
 
 def gather_channels(packed):
-    group = jnp.concatenate(gather_stage(packed, 1), axis=1)
-    column = jnp.stack(gather_stage(group, 16), 0)
-    return jnp.stack(gather_stage(column, 4), 1).reshape((SIDE * SIDE,) + group.shape)
+    group = jnp.concatenate(gather_stage(packed, 1)[1], axis=1)
+    column = jnp.stack(gather_stage(group, 16)[0], 0)
+    return gather_stage(column, 4)[0]
+
+
+def place_params(came_refs, at_z, at_y, p_ref):
+    for y, came in enumerate(came_refs):
+        for z in range(SIDE):
+            group = lax.rem(at_z - z + SIDE, SIDE) * SIDE + lax.rem(at_y - y + SIDE, SIDE)
+            p_ref[group] = came[z]
 
 
 def bcast_row(ref, row):
@@ -42,8 +50,8 @@
 
 
 def forward_and_kernel_grad(
-    taps, x_hbm, ct_hbm, p_ref, act_hbm, gc_hbm, gr_ref,
-    xb, cb, ab, xs, cv, gn, gc, pf, st, s1, s2, row_a, row_b, x_sem, c_sem, a_sem, g_sem,
+    taps, at_ref, x_hbm, ct_hbm, p0, p1, p2, p3, act_hbm, gc_hbm, gr_ref, p_hbm,
+    xb, cb, ab, xs, cv, gn, gc, pf, st, s1, s2, row_a, row_b, p_ref, x_sem, c_sem, a_sem, g_sem, p_sem,
 ):
     frames, width = xb.shape
     tiles = width // LANES
@@ -83,6 +91,10 @@
         x_copy(chunk).start()
     for chunk in range(chunks):
         c_copy(chunk).start()
+    place_params((p0, p1, p2, p3), at_ref[0], at_ref[1], p_ref)
+    p_copy = pltpu.make_async_copy(p_ref, p_hbm, p_sem)
+    p_copy.start()
+    st[...] = jnp.zeros_like(st)
 
     def load_params(tile):
         group = tile // per_group
@@ -222,16 +234,23 @@
         )
         part = per_group * LANES // SIDE
         for a in range(SIDE):
-            gr_ref[group * SIDE + a, :, :] = whole[:, a * part : (a + 1) * part]
+            piece = whole[:, a * part : (a + 1) * part]
+            spill = piece[MAIN : MAIN + SUB]
+            width_left = LANES - part
+            side = [spill[:, c : c + width_left] for c in range(0, part, width_left)]
+            side.append(jnp.zeros((SUB, width_left), F32))
+            both = jnp.concatenate([piece[:MAIN], jnp.concatenate(side, 0)], axis=1)
+            gr_ref[group * SIDE + a] = both
         return 0
 
     lax.fori_loop(0, tiles // per_group, out_group, 0)
     for chunk in range(chunks):
         a_copy(chunk).wait()
         g_copy(chunk).wait()
-
-
-def input_grad(taps, gc_hbm, p_ref, gi_hbm, gc, gb, pf, g_sem, o_sem):
+    p_copy.wait()
+
+
+def input_grad(taps, gc_hbm, p_ref, gi_hbm, zero_ref, gc, gb, pf, g_sem, o_sem):
     frames, width = gb.shape
     tiles = width // LANES
     rows = frames // SUB
@@ -251,6 +270,7 @@
 
     for chunk in range(chunks):
         g_copy(chunk).start()
+    zero_ref[...] = jnp.zeros_like(zero_ref)
 
     def tile_step(tile, _):
         group = tile // per_group
@@ -284,15 +304,34 @@
         o_copy(chunk).wait()
 
 
+def sum_pieces(came_ref, zero_ref, sum_ref):
+    total = zero_ref[...]
+    for source in range(came_ref.shape[0]):
+        total = total + came_ref[source]
+    sum_ref[...] = total
+
+
+def finish(scale, part, own, first, second, third, kernel_ref, bias_ref, gain_ref, shift_ref):
+    total = ((own[...] + first[...]) + (second[...] + third[...])) * scale
+    taps = kernel_ref.shape[0]
+    kernel_ref[...] = total[:taps, :part]
+    bias_ref[...] = total[taps : taps + 1, :part]
+    for row, ref in ((0, gain_ref), (1, shift_ref)):
+        ref[...] = jnp.concatenate(
+            [total[SUB * c + row : SUB * c + row + 1, part:] for c in range(3)], axis=1
+        )
+
+
 ANY = pl.BlockSpec(memory_space=pl.ANY)
 HELD = pl.BlockSpec(memory_space=pltpu.VMEM)
 
 
-def run_first(x, cotangent, params, taps):
+def run_first(x, cotangent, place, params, taps):
     frames, width = x.shape
     tiles = width // LANES
     chunks = 8
-    rows = params.shape[1]
+    rows = params[0].shape[1]
+    groups = (SIDE * SIDE,) + params[0].shape[1:]
     padded = frames + 2 * PAD
     whole = (tiles, frames, LANES)
     return pl.pallas_call(
@@ -300,10 +339,11 @@
         out_shape=(
             jax.ShapeDtypeStruct((frames, width), jnp.bfloat16),
             jax.ShapeDtypeStruct((tiles, padded, LANES), F32),
-            jax.ShapeDtypeStruct((SIDE**3, rows, width // SIDE**3), F32),
+            jax.ShapeDtypeStruct((SIDE**3, MAIN, LANES), F32),
+            jax.ShapeDtypeStruct(groups, params[0].dtype),
         ),
-        in_specs=[ANY, ANY, HELD],
-        out_specs=(ANY, ANY, HELD),
+        in_specs=[pl.BlockSpec(memory_space=pltpu.SMEM), ANY, ANY] + [HELD] * SIDE,
+        out_specs=(ANY, ANY, HELD, ANY),
         scratch_shapes=[
             pltpu.VMEM((frames, width), jnp.bfloat16),
             pltpu.VMEM((frames, width), jnp.bfloat16),
@@ -313,22 +353,24 @@
             pltpu.VMEM(whole, F32),
             pltpu.VMEM((tiles, padded, LANES), F32),
             pltpu.VMEM((rows, LANES), F32),
-            pltpu.VMEM((tiles, rows, LANES), F32),
+            pltpu.VMEM((tiles, MAIN + SUB, LANES), F32),
             pltpu.VMEM((frames, LANES), F32),
             pltpu.VMEM((frames, LANES), F32),
             pltpu.VMEM((frames, LANES), F32),
             pltpu.VMEM((frames, LANES), F32),
-            pltpu.SemaphoreType.DMA((chunks,)),
-            pltpu.SemaphoreType.DMA((chunks,)),
-            pltpu.SemaphoreType.DMA((chunks,)),
-            pltpu.SemaphoreType.DMA((chunks,)),
+            pltpu.VMEM(groups, params[0].dtype),
+            pltpu.SemaphoreType.DMA((chunks,)),
+            pltpu.SemaphoreType.DMA((chunks,)),
+            pltpu.SemaphoreType.DMA((chunks,)),
+            pltpu.SemaphoreType.DMA((chunks,)),
+            pltpu.SemaphoreType.DMA,
         ],
-        compiler_params=pltpu.CompilerParams(vmem_limit_bytes=56 << 20),
+        compiler_params=pltpu.CompilerParams(vmem_limit_bytes=52 << 20),
         cost_estimate=pl.CostEstimate(
             flops=4 * taps * frames * width, bytes_accessed=20 * frames * width, transcendentals=0
         ),
         name="forward_and_kernel_grad",
-    )(x, cotangent, params)
+    )(place, x, cotangent, *params)
 
 
 def run_second(grad_conv, params, taps, frames, width):
@@ -336,9 +378,12 @@
     chunks = 8
     return pl.pallas_call(
         functools.partial(input_grad, taps),
-        out_shape=jax.ShapeDtypeStruct((frames, width), jnp.bfloat16),
+        out_shape=(
+            jax.ShapeDtypeStruct((frames, width), jnp.bfloat16),
+            jax.ShapeDtypeStruct((MAIN, LANES), F32),
+        ),
         in_specs=[ANY, HELD],
-        out_specs=ANY,
+        out_specs=(ANY, HELD),
         scratch_shapes=[
             pltpu.VMEM(grad_conv.shape, F32),
             pltpu.VMEM((frames, width), jnp.bfloat16),
@@ -346,7 +391,7 @@
             pltpu.SemaphoreType.DMA((chunks,)),
             pltpu.SemaphoreType.DMA((chunks,)),
         ],
-        compiler_params=pltpu.CompilerParams(vmem_limit_bytes=56 << 20),
+        compiler_params=pltpu.CompilerParams(vmem_limit_bytes=52 << 20),
         cost_estimate=pl.CostEstimate(
             flops=2 * taps * frames * width, bytes_accessed=6 * frames * width, transcendentals=0
         ),
@@ -359,17 +404,34 @@
     clips, frames, width = conv_input.shape
     packed = jnp.concatenate([kernel, conv_bias[None], ln_gain[None], ln_bias[None]], 0)
     params = gather_channels(packed)
-    activated, grad_conv, pieces = run_first(conv_input[0], cotangent[0], params, taps)
+    me = lax.axis_index("shard")
+    place = jnp.stack([me // (SIDE * SIDE), (me // SIDE) % SIDE])
+    activated, grad_conv, pieces, groups = run_first(
+        conv_input[0], cotangent[0], place, params, taps
+    )
     came = lax.all_to_all(pieces, "shard", 0, 0)
-    grad_input = run_second(grad_conv, params, taps, frames, width)
-    share_sum = jnp.sum(came, axis=0)
-    summed = jnp.sum(lax.all_gather(share_sum, "rep", axis=0), axis=0)
+    grad_input, zeros = run_second(grad_conv, groups, taps, frames, width)
+    own = pl.pallas_call(
+        sum_pieces,
+        out_shape=jax.ShapeDtypeStruct(zeros.shape, F32),
+        in_specs=[HELD, HELD],
+        out_specs=HELD,
+        compiler_params=pltpu.CompilerParams(vmem_limit_bytes=8 << 20),
+        name="sum_pieces",
+    )(came, zeros)
+    others = [lax.ppermute(own, "rep", [(i, i ^ step) for i in range(4)]) for step in (1, 2, 3)]
     count = clips * frames * lax.axis_size("rep") * lax.axis_size("shard")
-    grads = summed * (1.0 / math.sqrt(count))
-    return (
-        activated[None], grad_input[None],
-        grads[:taps], grads[taps], grads[taps + 1], grads[taps + 2],
-    )
+    part = packed.shape[1]
+    row = jax.ShapeDtypeStruct((1, part), F32)
+    grads = pl.pallas_call(
+        functools.partial(finish, 1.0 / math.sqrt(count), part),
+        out_shape=(jax.ShapeDtypeStruct((taps, part), F32), row, row, row),
+        in_specs=[HELD] * 4,
+        out_specs=(HELD,) * 4,
+        compiler_params=pltpu.CompilerParams(vmem_limit_bytes=8 << 20),
+        name="finish",
+    )(own, *others)
+    return (activated[None], grad_input[None], grads[0]) + tuple(g[0] for g in grads[1:])
 
 
 def solution(mesh):

time: 129 us -> 119 us (0.922)
  blocking collectives: 15 us -> 0 us
  starting transfers between devices: 26.2 us -> 31.8 us
  local copies, waits for them, and re-layouts: 1.98 us -> 0 us
  waiting for transfers between devices: 21.3 us -> 23.2 us
    all_gather x1 -> x0, blocking collectives: 15 us -> none  [per_device(): summed = jnp.sum(lax.all_gather(share_sum, 'rep', axis=0), axis=0)]
    ppermute x0 -> x3, starting transfers between devices: none -> 5.02 us  [per_device(): lax.ppermute(own, 'rep', [(i, i ^ step) for i in range(4)])]
    all_to_all x1, waiting for transfers between devices: 10 us -> 12 us  [per_device(): came = lax.all_to_all(pieces, 'shard', 0, 0)]
    ppermute x9, waiting for transfers between devices: 11.3 us -> 9.75 us  [gather_stage(): lax.ppermute(block, 'shard', shifted(axis_stride, step))]
    ppermute x0 -> x3, waiting for transfers between devices: none -> 1.42 us  [per_device(): lax.ppermute(own, 'rep', [(i, i ^ step) for i in range(4)])]
    pallas_call x1 -> x3, Pallas kernels: 16.7 us -> 16.4 us  [the longest x1 15.7 us: run_second(): pl.pallas_call(functools.partial(input_grad, taps), out_shape=(jax.ShapeD...]
  transfers between devices with their start and end apart: 10 -> 13, of which waited for: 8 -> 8; matrix products, arithmetic and copies ran while one was open for 0% -> 0% of each run, Pallas kernels for 13% -> 13%
where the time goes in v3:
time: 119 us; the launch traced here: 118 us
  Pallas kernels  60.1 us (51%)
  starting transfers between devices  31.8 us (27%)
  waiting for transfers between devices  23.2 us (19%)
  other arithmetic  2.57 us (2%)
    pallas_call x1, Pallas kernels, run_first(): pl.pallas_call(functools.partial(forward_and_kernel_grad, taps), out_shap...  43.6 us
    ppermute x9, starting transfers between devices, gather_stage(): lax.ppermute(block, 'shard', shifted(axis_stride, step))  19.5 us
    pallas_call x1, Pallas kernels, run_second(): pl.pallas_call(functools.partial(input_grad, taps), out_shape=(jax.ShapeD...  15.7 us
    all_to_all x1, waiting for transfers between devices, per_device(): came = lax.all_to_all(pieces, 'shard', 0, 0)  12 us
    ppermute x9, waiting for transfers between devices, gather_stage(): lax.ppermute(block, 'shard', shifted(axis_stride, step))  9.75 us
    all_to_all x1, starting transfers between devices, per_device(): came = lax.all_to_all(pieces, 'shard', 0, 0)  7.19 us
    ppermute x3, starting transfers between devices, per_device(): lax.ppermute(own, 'rep', [(i, i ^ step) for i in range(4)])  5.02 us
  transfers between devices with their start and end apart: 13, of which 8 were waited for; matrix products, arithmetic and copies ran while one was open for 0% of the time, Pallas kernels for 13%

profile of v3, /device:TPU:1, one launch (start us, length us, event | category | flops | bytes accessed | tf_op | source)
XLA Modules:
  0.0 118.3 jit_solution(14837924420027558759)
XLA Ops:
  0.6 0.8 pad_maximum_fusion.2
  1.4 3.7 %collective-permute-start.1 = (bf16[34,96]{1,0:T(8,128)(2,1)S(1)}, bf16[34,96]{1,0:T(8,128)(2,1)S(1)}, u32[]{:S(2)}, u32[]{:S(2)}) collective-permute-start(bf16[34,96]{1,0:T(8,128)(2,1)S(1)} %pad_maximum_fusion.2), channel_id=1, source_target_pairs={{0,2},{1,3},{2,0},{3,1},{4,6},{5,7},{6,4},{7,5},{8,10},{9,11},{10,... | collective-permute-start | bytes 19592 | tf_op jit(solution)/shard_map/ppermute | solution.py:30
  5.1 0.9 collective-permute-start.2
  5.9 0.6 collective-permute-start
  6.5 0.0 collective-permute-done.1
  6.5 1.1 collective-permute-done.2
  7.7 2.0 %collective-permute-done = bf16[34,96]{1,0:T(8,128)(2,1)S(1)} collective-permute-done((bf16[34,96]{1,0:T(8,128)(2,1)S(1)}, bf16[34,96]{1,0:T(8,128)(2,1)S(1)}, u32[]{:S(2)}, u32[]{:S(2)}) %collective-permute-start) | collective-permute-done | bytes 6560 | tf_op jit(solution)/shard_map/ppermute | solution.py:30
  9.6 0.8 select_select_fusion.2
  10.4 0.8 select_select_fusion.3
  11.2 0.1 pad_maximum_fusion.1
  11.3 7.0 %collective-permute-start.4 = (bf16[34,384]{1,0:T(8,128)(2,1)S(1)}, bf16[34,384]{1,0:T(8,128)(2,1)S(1)}, u32[]{:S(2)}, u32[]{:S(2)}) collective-permute-start(bf16[34,384]{1,0:T(8,128)(2,1)S(1)} %pad_maximum_fusion.1), channel_id=1, source_target_pairs={{0,32},{1,33},{2,34},{3,35},{4,36},{5,37},{6,38},{7,39},{8,40},{9,... | collective-permute-start | bytes 78344 | tf_op jit(solution)/shard_map/ppermute | solution.py:30
  18.3 1.2 %collective-permute-start.3 = (bf16[34,384]{1,0:T(8,128)(2,1)S(1)}, bf16[34,384]{1,0:T(8,128)(2,1)S(1)}, u32[]{:S(2)}, u32[]{:S(2)}) collective-permute-start(bf16[34,384]{1,0:T(8,128)(2,1)S(1)} %pad_maximum_fusion.1), channel_id=1, source_target_pairs={{0,16},{1,17},{2,18},{3,19},{4,20},{5,21},{6,22},{7,23},{8,24},{9,... | collective-permute-start | bytes 78344 | tf_op jit(solution)/shard_map/ppermute | solution.py:30
  19.5 2.4 %collective-permute-start.5 = (bf16[34,384]{1,0:T(8,128)(2,1)S(1)}, bf16[34,384]{1,0:T(8,128)(2,1)S(1)}, u32[]{:S(2)}, u32[]{:S(2)}) collective-permute-start(bf16[34,384]{1,0:T(8,128)(2,1)S(1)} %pad_maximum_fusion.1), channel_id=1, source_target_pairs={{0,48},{1,49},{2,50},{3,51},{4,52},{5,53},{6,54},{7,55},{8,56},{9,... | collective-permute-start | bytes 78344 | tf_op jit(solution)/shard_map/ppermute | solution.py:30
  21.9 0.1 fusion
  21.9 0.0 collective-permute-done.4
  22.0 1.2 collective-permute-done.3
  23.1 0.0 collective-permute-done.5
  23.2 2.8 %collective-permute-start.8 = (bf16[4,34,384]{2,1,0:T(8,128)(2,1)S(1)}, bf16[4,34,384]{2,1,0:T(8,128)(2,1)S(1)}, u32[]{:S(2)}, u32[]{:S(2)}) collective-permute-start(bf16[4,34,384]{2,1,0:T(8,128)(2,1)S(1)} %pad_maximum_fusion.p0), channel_id=1, source_target_pairs={{0,12},{1,13},{2,14},{3,15},{4,0},{5,1},{6,2},{7,3},{8,4},{9,5},{1... | collective-permute-start | bytes 313352 | tf_op jit(solution)/shard_map/ppermute | solution.py:30
  26.0 0.3 collective-permute-start.7
  26.3 0.7 collective-permute-start.6
  27.0 0.1 pad_add_fusion.at_ref
  27.1 2.0 %collective-permute-done.8.p3 = bf16[4,34,384]{2,1,0:T(8,128)(2,1)S(1)} collective-permute-done((bf16[4,34,384]{2,1,0:T(8,128)(2,1)S(1)}, bf16[4,34,384]{2,1,0:T(8,128)(2,1)S(1)}, u32[]{:S(2)}, u32[]{:S(2)}) %collective-permute-start.8) | collective-permute-done | bytes 104480 | tf_op jit(solution)/shard_map/ppermute | solution.py:30
  29.1 2.2 %collective-permute-done.7.p2 = bf16[4,34,384]{2,1,0:T(8,128)(2,1)S(1)} collective-permute-done((bf16[4,34,384]{2,1,0:T(8,128)(2,1)S(1)}, bf16[4,34,384]{2,1,0:T(8,128)(2,1)S(1)}, u32[]{:S(2)}, u32[]{:S(2)}) %collective-permute-start.7) | collective-permute-done | bytes 104480 | tf_op jit(solution)/shard_map/ppermute | solution.py:30
  31.3 1.2 %collective-permute-done.6.p1 = bf16[4,34,384]{2,1,0:T(8,128)(2,1)S(1)} collective-permute-done((bf16[4,34,384]{2,1,0:T(8,128)(2,1)S(1)}, bf16[4,34,384]{2,1,0:T(8,128)(2,1)S(1)}, u32[]{:S(2)}, u32[]{:S(2)}) %collective-permute-start.6) | collective-permute-done | bytes 104480 | tf_op jit(solution)/shard_map/ppermute | solution.py:30
  32.5 43.6 %forward_and_kernel_grad.1 = (bf16[256,6144]{1,0:T(8,128)(2,1)}, f32[48,288,128]{2,1,0:T(8,128)}, f32[64,32,128]{2,1,0:T(8,128)}, bf16[16,34,384]{2,1,0:T(8,128)(2,1)S(1)}) custom-call(s32[2]{0:T(128)S(1)} %pad_add_fusion.at_ref, bf16[256,6144]{1,0:T(8,128)(2,1)} %bitcast.17, bf16[256,6144]{1,0:T(8,128)(2,1)} %bitcast.18, ...), custom_call_target="tpu_custom_call" | custom-call | flops 195035136 | bytes 31457280 | tf_op jit(solution)/shard_map/forward_and_kernel_grad/pallas_call | solution.py:337
  76.2 7.2 %all-to-all-start = ((f32[64,32,128]{2,1,0:T(8,128)}), f32[64,32,128]{2,1,0:T(8,128)S(1)}, u32[]{:S(2)}, u32[]{:S(2)}) async-start(f32[64,32,128]{2,1,0:T(8,128)} %get-tuple-element.20), calls=%async_computation | async-start | bytes 2097152 | tf_op jit(solution)/shard_map/all_to_all | solution.py:412
  83.4 15.7 %input_grad.1 = (bf16[256,6144]{1,0:T(8,128)(2,1)}, f32[32,128]{1,0:T(8,128)S(1)}) custom-call(f32[48,288,128]{2,1,0:T(8,128)} %get-tuple-element.17.gc_hbm, bf16[16,34,384]{2,1,0:T(8,128)(2,1)S(1)} %get-tuple-element.18.p_ref), custom_call_target="tpu_custom_call" | custom-call | flops 97517568 | bytes 9437184 | tf_op jit(solution)/shard_map/input_grad/pallas_call | solution.py:379
  99.1 12.0 %all-to-all-done.came_ref = f32[64,32,128]{2,1,0:T(8,128)S(1)} async-done(((f32[64,32,128]{2,1,0:T(8,128)}), f32[64,32,128]{2,1,0:T(8,128)S(1)}, u32[]{:S(2)}, u32[]{:S(2)}) %all-to-all-start) | async-done | bytes 1048608 | tf_op jit(solution)/shard_map/all_to_all | solution.py:412
  111.1 0.1 sum_pieces.1.own
  111.2 1.3 %collective-permute-start.11 = (f32[32,128]{1,0:T(8,128)S(1)}, f32[32,128]{1,0:T(8,128)S(1)}, u32[]{:S(2)}, u32[]{:S(2)}) collective-permute-start(f32[32,128]{1,0:T(8,128)S(1)} %sum_pieces.1.own), channel_id=1, source_target_pairs={{0,192},{64,128},{128,64},{192,0},{1,193},{65,129},{129,65},{193,1... | collective-permute-start | bytes 49160 | tf_op jit(solution)/shard_map/ppermute | solution.py:422
  112.5 3.7 %collective-permute-start.10 = (f32[32,128]{1,0:T(8,128)S(1)}, f32[32,128]{1,0:T(8,128)S(1)}, u32[]{:S(2)}, u32[]{:S(2)}) collective-permute-start(f32[32,128]{1,0:T(8,128)S(1)} %sum_pieces.1.own), channel_id=1, source_target_pairs={{0,128},{64,192},{128,0},{192,64},{1,129},{65,193},{129,1},{193,65... | collective-permute-start | bytes 49160 | tf_op jit(solution)/shard_map/ppermute | solution.py:422
  116.2 0.0 collective-permute-start.9
  116.2 0.0 collective-permute-done.11.third
  116.2 1.4 %collective-permute-done.10.second = f32[32,128]{1,0:T(8,128)S(1)} collective-permute-done((f32[32,128]{1,0:T(8,128)S(1)}, f32[32,128]{1,0:T(8,128)S(1)}, u32[]{:S(2)}, u32[]{:S(2)}) %collective-permute-start.10) | collective-permute-done | bytes 16416 | tf_op jit(solution)/shard_map/ppermute | solution.py:422
  117.6 0.0 collective-permute-done.9.first
  117.7 0.6 finish.1
  (1 shorter events, 0.0 us)
Async XLA Ops:
  1.4 5.1 %collective-permute-start.1 = (bf16[34,96]{1,0:T(8,128)(2,1)S(1)}, bf16[34,96]{1,0:T(8,128)(2,1)S(1)}, u32[]{:S(2)}, u32[]{:S(2)}) collective-permute-start(bf16[34,96]{1,0:T(8,128)(2,1)S(1)} %pad_maximum_fusion.2), channel_id=1, source_target_pairs={{0,2},{1,3},{2,0},{3,1},{4,6},{5,7},{6,4},{7,5},{8,10},{9,11},{10,... | collective-permute-start | bytes 19592 | tf_op jit(solution)/shard_map/ppermute | solution.py:30
  5.1 2.6 %collective-permute-start.2 = (bf16[34,96]{1,0:T(8,128)(2,1)S(1)}, bf16[34,96]{1,0:T(8,128)(2,1)S(1)}, u32[]{:S(2)}, u32[]{:S(2)}) collective-permute-start(bf16[34,96]{1,0:T(8,128)(2,1)S(1)} %pad_maximum_fusion.2), channel_id=1, source_target_pairs={{0,3},{1,0},{2,1},{3,2},{4,7},{5,4},{6,5},{7,6},{8,11},{9,8},{10,9... | collective-permute-start | bytes 19592 | tf_op jit(solution)/shard_map/ppermute | solution.py:30
  5.9 3.7 %collective-permute-start = (bf16[34,96]{1,0:T(8,128)(2,1)S(1)}, bf16[34,96]{1,0:T(8,128)(2,1)S(1)}, u32[]{:S(2)}, u32[]{:S(2)}) collective-permute-start(bf16[34,96]{1,0:T(8,128)(2,1)S(1)} %pad_maximum_fusion.2), channel_id=1, source_target_pairs={{0,1},{1,2},{2,3},{3,0},{4,5},{5,6},{6,7},{7,4},{8,9},{9,10},{10,1... | collective-permute-start | bytes 19592 | tf_op jit(solution)/shard_map/ppermute | solution.py:30
  11.3 10.7 %collective-permute-start.4 = (bf16[34,384]{1,0:T(8,128)(2,1)S(1)}, bf16[34,384]{1,0:T(8,128)(2,1)S(1)}, u32[]{:S(2)}, u32[]{:S(2)}) collective-permute-start(bf16[34,384]{1,0:T(8,128)(2,1)S(1)} %pad_maximum_fusion.1), channel_id=1, source_target_pairs={{0,32},{1,33},{2,34},{3,35},{4,36},{5,37},{6,38},{7,39},{8,40},{9,... | collective-permute-start | bytes 78344 | tf_op jit(solution)/shard_map/ppermute | solution.py:30
  18.3 4.9 %collective-permute-start.3 = (bf16[34,384]{1,0:T(8,128)(2,1)S(1)}, bf16[34,384]{1,0:T(8,128)(2,1)S(1)}, u32[]{:S(2)}, u32[]{:S(2)}) collective-permute-start(bf16[34,384]{1,0:T(8,128)(2,1)S(1)} %pad_maximum_fusion.1), channel_id=1, source_target_pairs={{0,16},{1,17},{2,18},{3,19},{4,20},{5,21},{6,22},{7,23},{8,24},{9,... | collective-permute-start | bytes 78344 | tf_op jit(solution)/shard_map/ppermute | solution.py:30
  19.5 3.7 %collective-permute-start.5 = (bf16[34,384]{1,0:T(8,128)(2,1)S(1)}, bf16[34,384]{1,0:T(8,128)(2,1)S(1)}, u32[]{:S(2)}, u32[]{:S(2)}) collective-permute-start(bf16[34,384]{1,0:T(8,128)(2,1)S(1)} %pad_maximum_fusion.1), channel_id=1, source_target_pairs={{0,48},{1,49},{2,50},{3,51},{4,52},{5,53},{6,54},{7,55},{8,56},{9,... | collective-permute-start | bytes 78344 | tf_op jit(solution)/shard_map/ppermute | solution.py:30
  23.2 6.0 %collective-permute-start.8 = (bf16[4,34,384]{2,1,0:T(8,128)(2,1)S(1)}, bf16[4,34,384]{2,1,0:T(8,128)(2,1)S(1)}, u32[]{:S(2)}, u32[]{:S(2)}) collective-permute-start(bf16[4,34,384]{2,1,0:T(8,128)(2,1)S(1)} %pad_maximum_fusion.p0), channel_id=1, source_target_pairs={{0,12},{1,13},{2,14},{3,15},{4,0},{5,1},{6,2},{7,3},{8,4},{9,5},{1... | collective-permute-start | bytes 313352 | tf_op jit(solution)/shard_map/ppermute | solution.py:30
  26.0 5.3 %collective-permute-start.7 = (bf16[4,34,384]{2,1,0:T(8,128)(2,1)S(1)}, bf16[4,34,384]{2,1,0:T(8,128)(2,1)S(1)}, u32[]{:S(2)}, u32[]{:S(2)}) collective-permute-start(bf16[4,34,384]{2,1,0:T(8,128)(2,1)S(1)} %pad_maximum_fusion.p0), channel_id=1, source_target_pairs={{0,8},{1,9},{2,10},{3,11},{4,12},{5,13},{6,14},{7,15},{8,0},{9,1},... | collective-permute-start | bytes 313352 | tf_op jit(solution)/shard_map/ppermute | solution.py:30
  26.3 6.2 %collective-permute-start.6 = (bf16[4,34,384]{2,1,0:T(8,128)(2,1)S(1)}, bf16[4,34,384]{2,1,0:T(8,128)(2,1)S(1)}, u32[]{:S(2)}, u32[]{:S(2)}) collective-permute-start(bf16[4,34,384]{2,1,0:T(8,128)(2,1)S(1)} %pad_maximum_fusion.p0), channel_id=1, source_target_pairs={{0,4},{1,5},{2,6},{3,7},{4,8},{5,9},{6,10},{7,11},{8,12},{9,13},{1... | collective-permute-start | bytes 313352 | tf_op jit(solution)/shard_map/ppermute | solution.py:30
  76.2 34.9 %all-to-all-start = ((f32[64,32,128]{2,1,0:T(8,128)}), f32[64,32,128]{2,1,0:T(8,128)S(1)}, u32[]{:S(2)}, u32[]{:S(2)}) async-start(f32[64,32,128]{2,1,0:T(8,128)} %get-tuple-element.20), calls=%async_computation | async-start | bytes 2097152 | tf_op jit(solution)/shard_map/all_to_all | solution.py:412
  111.2 5.0 %collective-permute-start.11 = (f32[32,128]{1,0:T(8,128)S(1)}, f32[32,128]{1,0:T(8,128)S(1)}, u32[]{:S(2)}, u32[]{:S(2)}) collective-permute-start(f32[32,128]{1,0:T(8,128)S(1)} %sum_pieces.1.own), channel_id=1, source_target_pairs={{0,192},{64,128},{128,64},{192,0},{1,193},{65,129},{129,65},{193,1... | collective-permute-start | bytes 49160 | tf_op jit(solution)/shard_map/ppermute | solution.py:422
  112.5 5.2 %collective-permute-start.10 = (f32[32,128]{1,0:T(8,128)S(1)}, f32[32,128]{1,0:T(8,128)S(1)}, u32[]{:S(2)}, u32[]{:S(2)}) collective-permute-start(f32[32,128]{1,0:T(8,128)S(1)} %sum_pieces.1.own), channel_id=1, source_target_pairs={{0,128},{64,192},{128,0},{192,64},{1,129},{65,193},{129,1},{193,65... | collective-permute-start | bytes 49160 | tf_op jit(solution)/shard_map/ppermute | solution.py:422
  116.2 1.4 %collective-permute-start.9 = (f32[32,128]{1,0:T(8,128)S(1)}, f32[32,128]{1,0:T(8,128)S(1)}, u32[]{:S(2)}, u32[]{:S(2)}) collective-permute-start(f32[32,128]{1,0:T(8,128)S(1)} %sum_pieces.1.own), channel_id=1, source_target_pairs={{0,64},{64,0},{128,192},{192,128},{1,65},{65,1},{129,193},{193,129... | collective-permute-start | bytes 49160 | tf_op jit(solution)/shard_map/ppermute | solution.py:422

commit v4 on v3

--- a/solution.py
+++ b/solution.py
@@ -13,7 +13,10 @@
 SUB = 8
 PAD = 16
 F32 = jnp.float32
+CHUNK_TILES = 3
+EARLY = 5
 MAIN = 32
+HALF = MAIN // 2
 
 
 def shifted(axis_stride, step):
@@ -50,7 +53,7 @@
 
 
 def forward_and_kernel_grad(
-    taps, at_ref, x_hbm, ct_hbm, p0, p1, p2, p3, act_hbm, gc_hbm, gr_ref, p_hbm,
+    taps, at_ref, x_hbm, ct_hbm, p0, p1, p2, p3, act_hbm, gc_hbm, keep_ref, send_ref, p_hbm,
     xb, cb, ab, xs, cv, gn, gc, pf, st, s1, s2, row_a, row_b, p_ref, x_sem, c_sem, a_sem, g_sem, p_sem,
 ):
     frames, width = xb.shape
@@ -240,7 +243,9 @@
             side = [spill[:, c : c + width_left] for c in range(0, part, width_left)]
             side.append(jnp.zeros((SUB, width_left), F32))
             both = jnp.concatenate([piece[:MAIN], jnp.concatenate(side, 0)], axis=1)
-            gr_ref[group * SIDE + a] = both
+            low, high = both[:HALF], both[HALF:]
+            keep_ref[group * SIDE + a] = jnp.where(at_ref[2] == 0, low, high)
+            send_ref[group * SIDE + a] = jnp.where(at_ref[2] == 0, high, low)
         return 0
 
     lax.fori_loop(0, tiles // per_group, out_group, 0)
@@ -250,12 +255,10 @@
     p_copy.wait()
 
 
-def input_grad(taps, gc_hbm, p_ref, gi_hbm, zero_ref, gc, gb, pf, g_sem, o_sem):
-    frames, width = gb.shape
-    tiles = width // LANES
-    rows = frames // SUB
-    chunks = g_sem.shape[0]
-    per_chunk = tiles // chunks
+def input_grad(taps, chunks, gc_hbm, p_ref, *refs):
+    gi_hbm, zero_ref, gc, gb, pf, g_sem, o_sem = refs[-7:]
+    rows = gb.shape[0] // SUB
+    per_chunk = CHUNK_TILES
     per_group = p_ref.shape[2] // LANES
     block = 8
 
@@ -268,7 +271,7 @@
         at = pl.ds(pl.multiple_of(chunk * wide, wide), wide)
         return pltpu.make_async_copy(gb.at[:, at], gi_hbm.at[:, at], o_sem.at[chunk])
 
-    for chunk in range(chunks):
+    for chunk in range(*chunks):
         g_copy(chunk).start()
     zero_ref[...] = jnp.zeros_like(zero_ref)
 
@@ -299,9 +302,13 @@
         o_copy(chunk).start()
         return 0
 
-    lax.fori_loop(0, chunks, chunk_step, 0)
-    for chunk in range(chunks):
+    lax.fori_loop(*chunks, chunk_step, 0)
+    for chunk in range(*chunks):
         o_copy(chunk).wait()
+
+
+def add_came(keep_ref, came_ref, zero_ref, sum_ref):
+    sum_ref[...] = keep_ref[...] + (came_ref[...] + zero_ref[...][None])
 
 
 def sum_pieces(came_ref, zero_ref, sum_ref):
@@ -311,8 +318,11 @@
     sum_ref[...] = total
 
 
-def finish(scale, part, own, first, second, third, kernel_ref, bias_ref, gain_ref, shift_ref):
-    total = ((own[...] + first[...]) + (second[...] + third[...])) * scale
+def finish(scale, part, core_ref, own, core, chip, both, kernel_ref, bias_ref, gain_ref, shift_ref):
+    mine = (own[...] + chip[...]) * scale
+    other = (core[...] + both[...]) * scale
+    first = core_ref[0] == 0
+    total = jnp.concatenate([jnp.where(first, mine, other), jnp.where(first, other, mine)], 0)
     taps = kernel_ref.shape[0]
     kernel_ref[...] = total[:taps, :part]
     bias_ref[...] = total[taps : taps + 1, :part]
@@ -339,11 +349,12 @@
         out_shape=(
             jax.ShapeDtypeStruct((frames, width), jnp.bfloat16),
             jax.ShapeDtypeStruct((tiles, padded, LANES), F32),
-            jax.ShapeDtypeStruct((SIDE**3, MAIN, LANES), F32),
+            jax.ShapeDtypeStruct((SIDE**3, HALF, LANES), F32),
+            jax.ShapeDtypeStruct((SIDE**3, HALF, LANES), F32),
             jax.ShapeDtypeStruct(groups, params[0].dtype),
         ),
         in_specs=[pl.BlockSpec(memory_space=pltpu.SMEM), ANY, ANY] + [HELD] * SIDE,
-        out_specs=(ANY, ANY, HELD, ANY),
+        out_specs=(ANY, ANY, HELD, HELD, ANY),
         scratch_shapes=[
             pltpu.VMEM((frames, width), jnp.bfloat16),
             pltpu.VMEM((frames, width), jnp.bfloat16),
@@ -373,30 +384,51 @@
     )(place, x, cotangent, *params)
 
 
-def run_second(grad_conv, params, taps, frames, width):
+def run_second(grad_conv, params, taps, frames, width, chunks, begun=None):
     tiles = width // LANES
-    chunks = 8
+    share = (chunks[1] - chunks[0]) * CHUNK_TILES / tiles
+    count = tiles // CHUNK_TILES
     return pl.pallas_call(
-        functools.partial(input_grad, taps),
+        functools.partial(input_grad, taps, chunks),
         out_shape=(
             jax.ShapeDtypeStruct((frames, width), jnp.bfloat16),
-            jax.ShapeDtypeStruct((MAIN, LANES), F32),
+            jax.ShapeDtypeStruct((HALF, LANES), F32),
         ),
-        in_specs=[ANY, HELD],
+        in_specs=[ANY, HELD] + ([] if begun is None else [ANY]),
         out_specs=(ANY, HELD),
         scratch_shapes=[
             pltpu.VMEM(grad_conv.shape, F32),
             pltpu.VMEM((frames, width), jnp.bfloat16),
             pltpu.VMEM((params.shape[1], LANES), F32),
-            pltpu.SemaphoreType.DMA((chunks,)),
-            pltpu.SemaphoreType.DMA((chunks,)),
+            pltpu.SemaphoreType.DMA((count,)),
+            pltpu.SemaphoreType.DMA((count,)),
         ],
+        input_output_aliases={} if begun is None else {2: 0},
         compiler_params=pltpu.CompilerParams(vmem_limit_bytes=52 << 20),
         cost_estimate=pl.CostEstimate(
-            flops=2 * taps * frames * width, bytes_accessed=6 * frames * width, transcendentals=0
+            flops=int(2 * taps * frames * width * share),
+            bytes_accessed=int(6 * frames * width * share),
+            transcendentals=0,
         ),
         name="input_grad",
-    )(grad_conv, params)
+    )(grad_conv, params, *([] if begun is None else [begun]))
+
+
+def small(body, out_shape, name, *operands, scalars=0):
+    scalar = pl.BlockSpec(memory_space=pltpu.SMEM)
+    many = isinstance(out_shape, tuple)
+    return pl.pallas_call(
+        body,
+        out_shape=out_shape,
+        in_specs=[scalar] * scalars + [HELD] * (len(operands) - scalars),
+        out_specs=(HELD,) * len(out_shape) if many else HELD,
+        compiler_params=pltpu.CompilerParams(vmem_limit_bytes=8 << 20),
+        name=name,
+    )(*operands)
+
+
+def over_rep(block, step):
+    return lax.ppermute(block, "rep", [(i, i ^ step) for i in range(4)])
 
 
 def per_device(conv_input, cotangent, kernel, conv_bias, ln_gain, ln_bias):
@@ -404,33 +436,27 @@
     clips, frames, width = conv_input.shape
     packed = jnp.concatenate([kernel, conv_bias[None], ln_gain[None], ln_bias[None]], 0)
     params = gather_channels(packed)
-    me = lax.axis_index("shard")
-    place = jnp.stack([me // (SIDE * SIDE), (me // SIDE) % SIDE])
-    activated, grad_conv, pieces, groups = run_first(
+    me, core = lax.axis_index("shard"), lax.axis_index("rep") % 2
+    place = jnp.stack([me // (SIDE * SIDE), (me // SIDE) % SIDE, core])
+    activated, grad_conv, keep, send, groups = run_first(
         conv_input[0], cotangent[0], place, params, taps
     )
+    came = over_rep(send, 1)
+    part_of = functools.partial(run_second, grad_conv, groups, taps, frames, width)
+    begun, zeros = part_of((0, EARLY))
+    pieces = small(add_came, jax.ShapeDtypeStruct(keep.shape, F32), "add_came", keep, came, zeros)
     came = lax.all_to_all(pieces, "shard", 0, 0)
-    grad_input, zeros = run_second(grad_conv, groups, taps, frames, width)
-    own = pl.pallas_call(
-        sum_pieces,
-        out_shape=jax.ShapeDtypeStruct(zeros.shape, F32),
-        in_specs=[HELD, HELD],
-        out_specs=HELD,
-        compiler_params=pltpu.CompilerParams(vmem_limit_bytes=8 << 20),
-        name="sum_pieces",
-    )(came, zeros)
-    others = [lax.ppermute(own, "rep", [(i, i ^ step) for i in range(4)]) for step in (1, 2, 3)]
+    grad_input, zeros = part_of((EARLY, width // LANES // CHUNK_TILES), begun)
+    own = small(sum_pieces, jax.ShapeDtypeStruct(zeros.shape, F32), "sum_pieces", came, zeros)
+    others = [over_rep(own, step) for step in (1, 2, 3)]
     count = clips * frames * lax.axis_size("rep") * lax.axis_size("shard")
     part = packed.shape[1]
     row = jax.ShapeDtypeStruct((1, part), F32)
-    grads = pl.pallas_call(
+    grads = small(
         functools.partial(finish, 1.0 / math.sqrt(count), part),
-        out_shape=(jax.ShapeDtypeStruct((taps, part), F32), row, row, row),
-        in_specs=[HELD] * 4,
-        out_specs=(HELD,) * 4,
-        compiler_params=pltpu.CompilerParams(vmem_limit_bytes=8 << 20),
-        name="finish",
-    )(own, *others)
+        (jax.ShapeDtypeStruct((taps, part), F32), row, row, row),
+        "finish", core[None], own, *others, scalars=1,
+    )
     return (activated[None], grad_input[None], grads[0]) + tuple(g[0] for g in grads[1:])
 
 

time: 119 us -> 120 us (level)
  waiting for transfers between devices: 23.2 us -> 18.3 us
  starting transfers between devices: 31.8 us -> 35.2 us
  Pallas kernels: 60.1 us -> 62.7 us
    all_to_all x1, waiting for transfers between devices: 12 us -> 6.45 us  [per_device(): came = lax.all_to_all(pieces, 'shard', 0, 0)]
    ppermute x3 -> x4, starting transfers between devices: 5.02 us -> 9.62 us  [over_rep(): return lax.ppermute(block, 'rep', [(i, i ^ step) for i in range(4)])]
    pallas_call x3 -> x5, Pallas kernels: 16.4 us -> 19.2 us  [the longest x2 17.7 us: run_second(): pl.pallas_call(functools.partial(input_grad, taps, chunks), out_shape=(ja...]
  transfers between devices with their start and end apart: 13 -> 14, of which waited for: 8 -> 9; matrix products, arithmetic and copies ran while one was open for 0% -> 0% of each run, Pallas kernels for 13% -> 15%
where the time goes in v4:
time: 120 us; the launch traced here: 119 us
  Pallas kernels  62.7 us (52%)
  starting transfers between devices  35.2 us (29%)
  waiting for transfers between devices  18.3 us (15%)
  other arithmetic  2.57 us (2%)
    pallas_call x1, Pallas kernels, run_first(): pl.pallas_call(functools.partial(forward_and_kernel_grad, taps), out_shap...  43.4 us
    ppermute x9, starting transfers between devices, gather_stage(): lax.ppermute(block, 'shard', shifted(axis_stride, step))  19.5 us
    pallas_call x2, Pallas kernels, run_second(): pl.pallas_call(functools.partial(input_grad, taps, chunks), out_shape=(ja...  17.7 us
    ppermute x9, waiting for transfers between devices, gather_stage(): lax.ppermute(block, 'shard', shifted(axis_stride, step))  9.75 us
    ppermute x4, starting transfers between devices, over_rep(): return lax.ppermute(block, 'rep', [(i, i ^ step) for i in range(4)])  9.62 us
    all_to_all x1, waiting for transfers between devices, per_device(): came = lax.all_to_all(pieces, 'shard', 0, 0)  6.45 us
    all_to_all x1, starting transfers between devices, per_device(): came = lax.all_to_all(pieces, 'shard', 0, 0)  6.03 us
  transfers between devices with their start and end apart: 14, of which 9 were waited for; matrix products, arithmetic and copies ran while one was open for 0% of the time, Pallas kernels for 15%

profile of v4, /device:TPU:1, one launch (start us, length us, event | category | flops | bytes accessed | tf_op | source)
XLA Modules:
  0.0 119.4 jit_solution(17656714935640276629)
XLA Ops:
  0.6 0.8 pad_maximum_fusion.2
  1.4 3.7 %collective-permute-start.1 = (bf16[34,96]{1,0:T(8,128)(2,1)S(1)}, bf16[34,96]{1,0:T(8,128)(2,1)S(1)}, u32[]{:S(2)}, u32[]{:S(2)}) collective-permute-start(bf16[34,96]{1,0:T(8,128)(2,1)S(1)} %pad_maximum_fusion.2), channel_id=1, source_target_pairs={{0,2},{1,3},{2,0},{3,1},{4,6},{5,7},{6,4},{7,5},{8,10},{9,11},{10,... | collective-permute-start | bytes 19592 | tf_op jit(solution)/shard_map/ppermute | solution.py:33
  5.1 0.9 collective-permute-start.2
  5.9 0.6 collective-permute-start
  6.5 0.0 collective-permute-done.1
  6.5 1.1 collective-permute-done.2
  7.7 2.0 %collective-permute-done = bf16[34,96]{1,0:T(8,128)(2,1)S(1)} collective-permute-done((bf16[34,96]{1,0:T(8,128)(2,1)S(1)}, bf16[34,96]{1,0:T(8,128)(2,1)S(1)}, u32[]{:S(2)}, u32[]{:S(2)}) %collective-permute-start) | collective-permute-done | bytes 6560 | tf_op jit(solution)/shard_map/ppermute | solution.py:33
  9.6 0.8 select_select_fusion.2
  10.4 0.8 select_select_fusion.3
  11.2 0.1 pad_maximum_fusion.1
  11.3 7.0 %collective-permute-start.4 = (bf16[34,384]{1,0:T(8,128)(2,1)S(1)}, bf16[34,384]{1,0:T(8,128)(2,1)S(1)}, u32[]{:S(2)}, u32[]{:S(2)}) collective-permute-start(bf16[34,384]{1,0:T(8,128)(2,1)S(1)} %pad_maximum_fusion.1), channel_id=1, source_target_pairs={{0,32},{1,33},{2,34},{3,35},{4,36},{5,37},{6,38},{7,39},{8,40},{9,... | collective-permute-start | bytes 78344 | tf_op jit(solution)/shard_map/ppermute | solution.py:33
  18.3 1.2 collective-permute-start.3
  19.5 2.4 %collective-permute-start.5 = (bf16[34,384]{1,0:T(8,128)(2,1)S(1)}, bf16[34,384]{1,0:T(8,128)(2,1)S(1)}, u32[]{:S(2)}, u32[]{:S(2)}) collective-permute-start(bf16[34,384]{1,0:T(8,128)(2,1)S(1)} %pad_maximum_fusion.1), channel_id=1, source_target_pairs={{0,48},{1,49},{2,50},{3,51},{4,52},{5,53},{6,54},{7,55},{8,56},{9,... | collective-permute-start | bytes 78344 | tf_op jit(solution)/shard_map/ppermute | solution.py:33
  21.9 0.1 fusion
  21.9 0.0 collective-permute-done.4
  22.0 1.2 collective-permute-done.3
  23.1 0.0 collective-permute-done.5
  23.2 2.8 %collective-permute-start.8 = (bf16[4,34,384]{2,1,0:T(8,128)(2,1)S(1)}, bf16[4,34,384]{2,1,0:T(8,128)(2,1)S(1)}, u32[]{:S(2)}, u32[]{:S(2)}) collective-permute-start(bf16[4,34,384]{2,1,0:T(8,128)(2,1)S(1)} %pad_maximum_fusion.p0), channel_id=1, source_target_pairs={{0,12},{1,13},{2,14},{3,15},{4,0},{5,1},{6,2},{7,3},{8,4},{9,5},{1... | collective-permute-start | bytes 313352 | tf_op jit(solution)/shard_map/ppermute | solution.py:33
  26.0 0.3 collective-permute-start.7
  26.3 0.7 collective-permute-start.6
  27.0 0.1 pad_add_fusion.at_ref
  27.1 2.0 %collective-permute-done.8.p3 = bf16[4,34,384]{2,1,0:T(8,128)(2,1)S(1)} collective-permute-done((bf16[4,34,384]{2,1,0:T(8,128)(2,1)S(1)}, bf16[4,34,384]{2,1,0:T(8,128)(2,1)S(1)}, u32[]{:S(2)}, u32[]{:S(2)}) %collective-permute-start.8) | collective-permute-done | bytes 104480 | tf_op jit(solution)/shard_map/ppermute | solution.py:33
  29.1 2.2 %collective-permute-done.7.p2 = bf16[4,34,384]{2,1,0:T(8,128)(2,1)S(1)} collective-permute-done((bf16[4,34,384]{2,1,0:T(8,128)(2,1)S(1)}, bf16[4,34,384]{2,1,0:T(8,128)(2,1)S(1)}, u32[]{:S(2)}, u32[]{:S(2)}) %collective-permute-start.7) | collective-permute-done | bytes 104480 | tf_op jit(solution)/shard_map/ppermute | solution.py:33
  31.3 1.2 %collective-permute-done.6.p1 = bf16[4,34,384]{2,1,0:T(8,128)(2,1)S(1)} collective-permute-done((bf16[4,34,384]{2,1,0:T(8,128)(2,1)S(1)}, bf16[4,34,384]{2,1,0:T(8,128)(2,1)S(1)}, u32[]{:S(2)}, u32[]{:S(2)}) %collective-permute-start.6) | collective-permute-done | bytes 104480 | tf_op jit(solution)/shard_map/ppermute | solution.py:33
  32.5 43.4 %forward_and_kernel_grad.1 = (bf16[256,6144]{1,0:T(8,128)(2,1)}, f32[48,288,128]{2,1,0:T(8,128)}, f32[64,16,128]{2,1,0:T(8,128)S(1)}, f32[64,16,128]{2,1,0:T(8,128)}, bf16[16,34,384]{2,1,0:T(8,128)(2,1)S(1)}) custom-call(s32[3]{0:T(128)S(1)} %pad_add_fusion.at_ref, bf16[256,6144]{1,0:T(8,128)(2,1)} %bitcast.18, bf16[256,6144]{1,0:T(8,128)(2,1)} %bitcast.19, ...), custom_call_target="tpu_custom_call" | custom-call | flops 195035136 | bytes 31457280 | tf_op jit(solution)/shard_map/forward_and_kernel_grad/pallas_call | solution.py:347
  76.0 5.6 %collective-permute-start.9 = (f32[64,16,128]{2,1,0:T(8,128)}, f32[64,16,128]{2,1,0:T(8,128)S(1)}, u32[]{:S(2)}, u32[]{:S(2)}) collective-permute-start(f32[64,16,128]{2,1,0:T(8,128)} %get-tuple-element.25), channel_id=1, source_target_pairs={{0,64},{64,0},{128,192},{192,128},{1,65},{65,1},{129,193},{193,129... | collective-permute-start | bytes 1572872 | tf_op jit(solution)/shard_map/ppermute | solution.py:431
  81.6 6.3 %input_grad.2 = (bf16[256,6144]{1,0:T(8,128)(2,1)}, f32[16,128]{1,0:T(8,128)S(1)}) custom-call(f32[48,288,128]{2,1,0:T(8,128)} %get-tuple-element.20.gc_hbm, bf16[16,34,384]{2,1,0:T(8,128)(2,1)S(1)} %get-tuple-element.21.p_ref), custom_call_target="tpu_custom_call" | custom-call | flops 30474240 | bytes 2949120 | tf_op jit(solution)/shard_map/input_grad/pallas_call | solution.py:391
  87.8 0.0 collective-permute-done.9.came_ref
  87.8 0.8 add_came.1
  88.7 6.0 %all-to-all-start = ((f32[64,16,128]{2,1,0:T(8,128)}), f32[64,16,128]{2,1,0:T(8,128)S(1)}, u32[]{:S(2)}, u32[]{:S(2)}) async-start(f32[64,16,128]{2,1,0:T(8,128)} %add_came.1), calls=%async_computation | async-start | bytes 1048576 | tf_op jit(solution)/shard_map/all_to_all | solution.py:448
  94.7 11.4 %input_grad.3 = (bf16[256,6144]{1,0:T(8,128)(2,1)}, f32[16,128]{1,0:T(8,128)S(1)}) custom-call(f32[48,288,128]{2,1,0:T(8,128)} %get-tuple-element.20.gc_hbm, bf16[16,34,384]{2,1,0:T(8,128)(2,1)S(1)} %get-tuple-element.21.p_ref, bf16[256,6144]{1,0:T(8,128)(2,1)} %get-tuple-element.22.refs_0_), custom_call_target="tpu_custom_call", output_to_operand_aliasing={{0}: (2, {})} | custom-call | flops 67043328 | bytes 6488064 | tf_op jit(solution)/shard_map/input_grad/pallas_call | solution.py:391
  106.1 6.5 %all-to-all-done.came_ref = f32[64,16,128]{2,1,0:T(8,128)S(1)} async-done(((f32[64,16,128]{2,1,0:T(8,128)}), f32[64,16,128]{2,1,0:T(8,128)S(1)}, u32[]{:S(2)}, u32[]{:S(2)}) %all-to-all-start) | async-done | bytes 524320 | tf_op jit(solution)/shard_map/all_to_all | solution.py:448
  112.6 0.1 sum_pieces.1.own
  112.7 3.3 %collective-permute-start.12 = (f32[16,128]{1,0:T(8,128)S(1)}, f32[16,128]{1,0:T(8,128)S(1)}, u32[]{:S(2)}, u32[]{:S(2)}) collective-permute-start(f32[16,128]{1,0:T(8,128)S(1)} %sum_pieces.1.own), channel_id=1, source_target_pairs={{0,192},{64,128},{128,64},{192,0},{1,193},{65,129},{129,65},{193,1... | collective-permute-start | bytes 24584 | tf_op jit(solution)/shard_map/ppermute | solution.py:431
  115.9 0.8 collective-permute-start.11
  116.7 0.0 collective-permute-start.10
  116.7 0.6 collective-permute-done.12.both
  117.3 1.5 %collective-permute-done.11.chip = f32[16,128]{1,0:T(8,128)S(1)} collective-permute-done((f32[16,128]{1,0:T(8,128)S(1)}, f32[16,128]{1,0:T(8,128)S(1)}, u32[]{:S(2)}, u32[]{:S(2)}) %collective-permute-start.11) | collective-permute-done | bytes 8224 | tf_op jit(solution)/shard_map/ppermute | solution.py:431
  118.8 0.0 collective-permute-done.10.core
  118.8 0.6 finish.1
  (1 shorter events, 0.0 us)
Async XLA Ops:
  1.4 5.1 %collective-permute-start.1 = (bf16[34,96]{1,0:T(8,128)(2,1)S(1)}, bf16[34,96]{1,0:T(8,128)(2,1)S(1)}, u32[]{:S(2)}, u32[]{:S(2)}) collective-permute-start(bf16[34,96]{1,0:T(8,128)(2,1)S(1)} %pad_maximum_fusion.2), channel_id=1, source_target_pairs={{0,2},{1,3},{2,0},{3,1},{4,6},{5,7},{6,4},{7,5},{8,10},{9,11},{10,... | collective-permute-start | bytes 19592 | tf_op jit(solution)/shard_map/ppermute | solution.py:33
  5.1 2.6 %collective-permute-start.2 = (bf16[34,96]{1,0:T(8,128)(2,1)S(1)}, bf16[34,96]{1,0:T(8,128)(2,1)S(1)}, u32[]{:S(2)}, u32[]{:S(2)}) collective-permute-start(bf16[34,96]{1,0:T(8,128)(2,1)S(1)} %pad_maximum_fusion.2), channel_id=1, source_target_pairs={{0,3},{1,0},{2,1},{3,2},{4,7},{5,4},{6,5},{7,6},{8,11},{9,8},{10,9... | collective-permute-start | bytes 19592 | tf_op jit(solution)/shard_map/ppermute | solution.py:33
  5.9 3.7 %collective-permute-start = (bf16[34,96]{1,0:T(8,128)(2,1)S(1)}, bf16[34,96]{1,0:T(8,128)(2,1)S(1)}, u32[]{:S(2)}, u32[]{:S(2)}) collective-permute-start(bf16[34,96]{1,0:T(8,128)(2,1)S(1)} %pad_maximum_fusion.2), channel_id=1, source_target_pairs={{0,1},{1,2},{2,3},{3,0},{4,5},{5,6},{6,7},{7,4},{8,9},{9,10},{10,1... | collective-permute-start | bytes 19592 | tf_op jit(solution)/shard_map/ppermute | solution.py:33
  11.3 10.7 %collective-permute-start.4 = (bf16[34,384]{1,0:T(8,128)(2,1)S(1)}, bf16[34,384]{1,0:T(8,128)(2,1)S(1)}, u32[]{:S(2)}, u32[]{:S(2)}) collective-permute-start(bf16[34,384]{1,0:T(8,128)(2,1)S(1)} %pad_maximum_fusion.1), channel_id=1, source_target_pairs={{0,32},{1,33},{2,34},{3,35},{4,36},{5,37},{6,38},{7,39},{8,40},{9,... | collective-permute-start | bytes 78344 | tf_op jit(solution)/shard_map/ppermute | solution.py:33
  18.3 4.9 %collective-permute-start.3 = (bf16[34,384]{1,0:T(8,128)(2,1)S(1)}, bf16[34,384]{1,0:T(8,128)(2,1)S(1)}, u32[]{:S(2)}, u32[]{:S(2)}) collective-permute-start(bf16[34,384]{1,0:T(8,128)(2,1)S(1)} %pad_maximum_fusion.1), channel_id=1, source_target_pairs={{0,16},{1,17},{2,18},{3,19},{4,20},{5,21},{6,22},{7,23},{8,24},{9,... | collective-permute-start | bytes 78344 | tf_op jit(solution)/shard_map/ppermute | solution.py:33
  19.5 3.7 %collective-permute-start.5 = (bf16[34,384]{1,0:T(8,128)(2,1)S(1)}, bf16[34,384]{1,0:T(8,128)(2,1)S(1)}, u32[]{:S(2)}, u32[]{:S(2)}) collective-permute-start(bf16[34,384]{1,0:T(8,128)(2,1)S(1)} %pad_maximum_fusion.1), channel_id=1, source_target_pairs={{0,48},{1,49},{2,50},{3,51},{4,52},{5,53},{6,54},{7,55},{8,56},{9,... | collective-permute-start | bytes 78344 | tf_op jit(solution)/shard_map/ppermute | solution.py:33
  23.2 6.0 %collective-permute-start.8 = (bf16[4,34,384]{2,1,0:T(8,128)(2,1)S(1)}, bf16[4,34,384]{2,1,0:T(8,128)(2,1)S(1)}, u32[]{:S(2)}, u32[]{:S(2)}) collective-permute-start(bf16[4,34,384]{2,1,0:T(8,128)(2,1)S(1)} %pad_maximum_fusion.p0), channel_id=1, source_target_pairs={{0,12},{1,13},{2,14},{3,15},{4,0},{5,1},{6,2},{7,3},{8,4},{9,5},{1... | collective-permute-start | bytes 313352 | tf_op jit(solution)/shard_map/ppermute | solution.py:33
  26.0 5.3 %collective-permute-start.7 = (bf16[4,34,384]{2,1,0:T(8,128)(2,1)S(1)}, bf16[4,34,384]{2,1,0:T(8,128)(2,1)S(1)}, u32[]{:S(2)}, u32[]{:S(2)}) collective-permute-start(bf16[4,34,384]{2,1,0:T(8,128)(2,1)S(1)} %pad_maximum_fusion.p0), channel_id=1, source_target_pairs={{0,8},{1,9},{2,10},{3,11},{4,12},{5,13},{6,14},{7,15},{8,0},{9,1},... | collective-permute-start | bytes 313352 | tf_op jit(solution)/shard_map/ppermute | solution.py:33
  26.3 6.2 %collective-permute-start.6 = (bf16[4,34,384]{2,1,0:T(8,128)(2,1)S(1)}, bf16[4,34,384]{2,1,0:T(8,128)(2,1)S(1)}, u32[]{:S(2)}, u32[]{:S(2)}) collective-permute-start(bf16[4,34,384]{2,1,0:T(8,128)(2,1)S(1)} %pad_maximum_fusion.p0), channel_id=1, source_target_pairs={{0,4},{1,5},{2,6},{3,7},{4,8},{5,9},{6,10},{7,11},{8,12},{9,13},{1... | collective-permute-start | bytes 313352 | tf_op jit(solution)/shard_map/ppermute | solution.py:33
  76.0 11.9 %collective-permute-start.9 = (f32[64,16,128]{2,1,0:T(8,128)}, f32[64,16,128]{2,1,0:T(8,128)S(1)}, u32[]{:S(2)}, u32[]{:S(2)}) collective-permute-start(f32[64,16,128]{2,1,0:T(8,128)} %get-tuple-element.25), channel_id=1, source_target_pairs={{0,64},{64,0},{128,192},{192,128},{1,65},{65,1},{129,193},{193,129... | collective-permute-start | bytes 1572872 | tf_op jit(solution)/shard_map/ppermute | solution.py:431
  88.7 23.9 %all-to-all-start = ((f32[64,16,128]{2,1,0:T(8,128)}), f32[64,16,128]{2,1,0:T(8,128)S(1)}, u32[]{:S(2)}, u32[]{:S(2)}) async-start(f32[64,16,128]{2,1,0:T(8,128)} %add_came.1), calls=%async_computation | async-start | bytes 1048576 | tf_op jit(solution)/shard_map/all_to_all | solution.py:448
  112.7 4.6 %collective-permute-start.12 = (f32[16,128]{1,0:T(8,128)S(1)}, f32[16,128]{1,0:T(8,128)S(1)}, u32[]{:S(2)}, u32[]{:S(2)}) collective-permute-start(f32[16,128]{1,0:T(8,128)S(1)} %sum_pieces.1.own), channel_id=1, source_target_pairs={{0,192},{64,128},{128,64},{192,0},{1,193},{65,129},{129,65},{193,1... | collective-permute-start | bytes 24584 | tf_op jit(solution)/shard_map/ppermute | solution.py:431
  115.9 2.9 %collective-permute-start.11 = (f32[16,128]{1,0:T(8,128)S(1)}, f32[16,128]{1,0:T(8,128)S(1)}, u32[]{:S(2)}, u32[]{:S(2)}) collective-permute-start(f32[16,128]{1,0:T(8,128)S(1)} %sum_pieces.1.own), channel_id=1, source_target_pairs={{0,128},{64,192},{128,0},{192,64},{1,129},{65,193},{129,1},{193,65... | collective-permute-start | bytes 24584 | tf_op jit(solution)/shard_map/ppermute | solution.py:431
  116.7 2.1 %collective-permute-start.10 = (f32[16,128]{1,0:T(8,128)S(1)}, f32[16,128]{1,0:T(8,128)S(1)}, u32[]{:S(2)}, u32[]{:S(2)}) collective-permute-start(f32[16,128]{1,0:T(8,128)S(1)} %sum_pieces.1.own), channel_id=1, source_target_pairs={{0,64},{64,0},{128,192},{192,128},{1,65},{65,1},{129,193},{193,129... | collective-permute-start | bytes 24584 | tf_op jit(solution)/shard_map/ppermute | solution.py:431

commit v5 on v4

--- a/solution.py
+++ b/solution.py
@@ -14,9 +14,8 @@
 PAD = 16
 F32 = jnp.float32
 CHUNK_TILES = 3
-EARLY = 5
+EARLY = 12
 MAIN = 32
-HALF = MAIN // 2
 
 
 def shifted(axis_stride, step):
@@ -53,7 +52,7 @@
 
 
 def forward_and_kernel_grad(
-    taps, at_ref, x_hbm, ct_hbm, p0, p1, p2, p3, act_hbm, gc_hbm, keep_ref, send_ref, p_hbm,
+    taps, at_ref, x_hbm, ct_hbm, p0, p1, p2, p3, act_hbm, gc_hbm, gr_ref, p_hbm,
     xb, cb, ab, xs, cv, gn, gc, pf, st, s1, s2, row_a, row_b, p_ref, x_sem, c_sem, a_sem, g_sem, p_sem,
 ):
     frames, width = xb.shape
@@ -243,9 +242,8 @@
             side = [spill[:, c : c + width_left] for c in range(0, part, width_left)]
             side.append(jnp.zeros((SUB, width_left), F32))
             both = jnp.concatenate([piece[:MAIN], jnp.concatenate(side, 0)], axis=1)
-            low, high = both[:HALF], both[HALF:]
-            keep_ref[group * SIDE + a] = jnp.where(at_ref[2] == 0, low, high)
-            send_ref[group * SIDE + a] = jnp.where(at_ref[2] == 0, high, low)
+            at_yx = lax.rem(group, SIDE) * SIDE + a
+            gr_ref[at_yx * SIDE + group // SIDE] = both
         return 0
 
     lax.fori_loop(0, tiles // per_group, out_group, 0)
@@ -307,22 +305,21 @@
         o_copy(chunk).wait()
 
 
-def add_came(keep_ref, came_ref, zero_ref, sum_ref):
-    sum_ref[...] = keep_ref[...] + (came_ref[...] + zero_ref[...][None])
-
-
-def sum_pieces(came_ref, zero_ref, sum_ref):
-    total = zero_ref[...]
-    for source in range(came_ref.shape[0]):
-        total = total + came_ref[source]
-    sum_ref[...] = total
-
-
-def finish(scale, part, core_ref, own, core, chip, both, kernel_ref, bias_ref, gain_ref, shift_ref):
-    mine = (own[...] + chip[...]) * scale
-    other = (core[...] + both[...]) * scale
-    first = core_ref[0] == 0
-    total = jnp.concatenate([jnp.where(first, mine, other), jnp.where(first, other, mine)], 0)
+def sum_plane(at_ref, came_ref, zero_ref, *sum_refs):
+    for step, sum_ref in enumerate(sum_refs):
+        at = lax.rem(at_ref[0] + step, SIDE)
+        total = zero_ref[...]
+        for source in range(came_ref.shape[0]):
+            total = total + came_ref[source, at]
+        sum_ref[...] = total
+
+
+def sum_column(own, first, second, third, zero_ref, sum_ref):
+    sum_ref[...] = (own[...] + first[...]) + (second[...] + third[...]) + zero_ref[...]
+
+
+def finish(scale, part, own, first, second, third, kernel_ref, bias_ref, gain_ref, shift_ref):
+    total = ((own[...] + first[...]) + (second[...] + third[...])) * scale
     taps = kernel_ref.shape[0]
     kernel_ref[...] = total[:taps, :part]
     bias_ref[...] = total[taps : taps + 1, :part]
@@ -349,12 +346,11 @@
         out_shape=(
             jax.ShapeDtypeStruct((frames, width), jnp.bfloat16),
             jax.ShapeDtypeStruct((tiles, padded, LANES), F32),
-            jax.ShapeDtypeStruct((SIDE**3, HALF, LANES), F32),
-            jax.ShapeDtypeStruct((SIDE**3, HALF, LANES), F32),
+            jax.ShapeDtypeStruct((SIDE**3, MAIN, LANES), F32),
             jax.ShapeDtypeStruct(groups, params[0].dtype),
         ),
         in_specs=[pl.BlockSpec(memory_space=pltpu.SMEM), ANY, ANY] + [HELD] * SIDE,
-        out_specs=(ANY, ANY, HELD, HELD, ANY),
+        out_specs=(ANY, ANY, HELD, ANY),
         scratch_shapes=[
             pltpu.VMEM((frames, width), jnp.bfloat16),
             pltpu.VMEM((frames, width), jnp.bfloat16),
@@ -392,7 +388,7 @@
         functools.partial(input_grad, taps, chunks),
         out_shape=(
             jax.ShapeDtypeStruct((frames, width), jnp.bfloat16),
-            jax.ShapeDtypeStruct((HALF, LANES), F32),
+            jax.ShapeDtypeStruct((MAIN, LANES), F32),
         ),
         in_specs=[ANY, HELD] + ([] if begun is None else [ANY]),
         out_specs=(ANY, HELD),
@@ -436,18 +432,22 @@
     clips, frames, width = conv_input.shape
     packed = jnp.concatenate([kernel, conv_bias[None], ln_gain[None], ln_bias[None]], 0)
     params = gather_channels(packed)
-    me, core = lax.axis_index("shard"), lax.axis_index("rep") % 2
-    place = jnp.stack([me // (SIDE * SIDE), (me // SIDE) % SIDE, core])
-    activated, grad_conv, keep, send, groups = run_first(
+    me = lax.axis_index("shard")
+    place = jnp.stack([me // (SIDE * SIDE), (me // SIDE) % SIDE])
+    activated, grad_conv, pieces, groups = run_first(
         conv_input[0], cotangent[0], place, params, taps
     )
-    came = over_rep(send, 1)
     part_of = functools.partial(run_second, grad_conv, groups, taps, frames, width)
+    planes = [list(range(z * SIDE * SIDE, (z + 1) * SIDE * SIDE)) for z in range(SIDE)]
+    came = lax.all_to_all(
+        pieces.reshape(SIDE * SIDE, SIDE, MAIN, LANES), "shard", 0, 0, axis_index_groups=planes
+    )
     begun, zeros = part_of((0, EARLY))
-    pieces = small(add_came, jax.ShapeDtypeStruct(keep.shape, F32), "add_came", keep, came, zeros)
-    came = lax.all_to_all(pieces, "shard", 0, 0)
+    piece = jax.ShapeDtypeStruct(zeros.shape, F32)
+    sums = small(sum_plane, (piece,) * SIDE, "sum_plane", place, came, zeros, scalars=1)
+    column = [lax.ppermute(sums[s], "shard", shifted(SIDE * SIDE, s)) for s in range(1, SIDE)]
     grad_input, zeros = part_of((EARLY, width // LANES // CHUNK_TILES), begun)
-    own = small(sum_pieces, jax.ShapeDtypeStruct(zeros.shape, F32), "sum_pieces", came, zeros)
+    own = small(sum_column, piece, "sum_column", sums[0], *column, zeros)
     others = [over_rep(own, step) for step in (1, 2, 3)]
     count = clips * frames * lax.axis_size("rep") * lax.axis_size("shard")
     part = packed.shape[1]
@@ -455,7 +455,7 @@
     grads = small(
         functools.partial(finish, 1.0 / math.sqrt(count), part),
         (jax.ShapeDtypeStruct((taps, part), F32), row, row, row),
-        "finish", core[None], own, *others, scalars=1,
+        "finish", own, *others,
     )
     return (activated[None], grad_input[None], grads[0]) + tuple(g[0] for g in grads[1:])
 

time: 120 us -> 116 us (0.967)
  waiting for transfers between devices: 18.3 us -> 11.2 us
  starting transfers between devices: 35.2 us -> 38.8 us
    ppermute x0 -> x3, starting transfers between devices: none -> 7.84 us  [per_device(): lax.ppermute(sums[s], 'shard', shifted(SIDE * SIDE, s))]
    all_to_all x1, waiting for transfers between devices: 6.45 us -> 0.01 us  [per_device(): lax.all_to_all(pieces.reshape(SIDE * SIDE, SIDE, MAIN, LANES), 'shard', 0...]
    all_to_all x1, starting transfers between devices: 6.03 us -> 3.66 us  [per_device(): lax.all_to_all(pieces.reshape(SIDE * SIDE, SIDE, MAIN, LANES), 'shard', 0...]
    ppermute x4 -> x3, starting transfers between devices: 9.62 us -> 7.74 us  [over_rep(): return lax.ppermute(block, 'rep', [(i, i ^ step) for i in range(4)])]
  transfers between devices with their start and end apart: 14 -> 16, of which waited for: 9 -> 7; matrix products, arithmetic and copies ran while one was open for 0% -> 0% of each run, Pallas kernels for 15% -> 15%
where the time goes in v5:
time: 116 us
  Pallas kernels  62.6 us (54%)
  starting transfers between devices  38.8 us (33%)
  waiting for transfers between devices  11.2 us (10%)
  other arithmetic  2.57 us (2%)
    pallas_call x1, Pallas kernels, run_first(): pl.pallas_call(functools.partial(forward_and_kernel_grad, taps), out_shap...  43.7 us
    ppermute x9, starting transfers between devices, gather_stage(): lax.ppermute(block, 'shard', shifted(axis_stride, step))  19.5 us
    pallas_call x2, Pallas kernels, run_second(): pl.pallas_call(functools.partial(input_grad, taps, chunks), out_shape=(ja...  17.7 us
    ppermute x9, waiting for transfers between devices, gather_stage(): lax.ppermute(block, 'shard', shifted(axis_stride, step))  9.75 us
    ppermute x3, starting transfers between devices, per_device(): lax.ppermute(sums[s], 'shard', shifted(SIDE * SIDE, s))  7.84 us
    ppermute x3, starting transfers between devices, over_rep(): return lax.ppermute(block, 'rep', [(i, i ^ step) for i in range(4)])  7.74 us
    all_to_all x1, starting transfers between devices, per_device(): lax.all_to_all(pieces.reshape(SIDE * SIDE, SIDE, MAIN, LANES), 'shard', 0...  3.66 us
  transfers between devices with their start and end apart: 16, of which 7 were waited for; matrix products, arithmetic and copies ran while one was open for 0% of the time, Pallas kernels for 15%

profile of v5, /device:TPU:1, one launch (start us, length us, event | category | flops | bytes accessed | tf_op | source)
XLA Modules:
  0.0 115.9 jit_solution(2601850466528640238)
XLA Ops:
  0.6 0.8 pad_maximum_fusion.2
  1.4 3.7 %collective-permute-start.1 = (bf16[34,96]{1,0:T(8,128)(2,1)S(1)}, bf16[34,96]{1,0:T(8,128)(2,1)S(1)}, u32[]{:S(2)}, u32[]{:S(2)}) collective-permute-start(bf16[34,96]{1,0:T(8,128)(2,1)S(1)} %pad_maximum_fusion.2), channel_id=1, source_target_pairs={{0,2},{1,3},{2,0},{3,1},{4,6},{5,7},{6,4},{7,5},{8,10},{9,11},{10,... | collective-permute-start | bytes 19592 | tf_op jit(solution)/shard_map/ppermute | solution.py:32
  5.1 0.9 collective-permute-start.2
  5.9 0.6 collective-permute-start
  6.5 0.0 collective-permute-done.1
  6.5 1.1 collective-permute-done.2
  7.7 2.0 %collective-permute-done = bf16[34,96]{1,0:T(8,128)(2,1)S(1)} collective-permute-done((bf16[34,96]{1,0:T(8,128)(2,1)S(1)}, bf16[34,96]{1,0:T(8,128)(2,1)S(1)}, u32[]{:S(2)}, u32[]{:S(2)}) %collective-permute-start) | collective-permute-done | bytes 6560 | tf_op jit(solution)/shard_map/ppermute | solution.py:32
  9.6 0.8 select_select_fusion.2
  10.4 0.8 select_select_fusion.3
  11.2 0.1 pad_maximum_fusion.1
  11.3 7.0 %collective-permute-start.4 = (bf16[34,384]{1,0:T(8,128)(2,1)S(1)}, bf16[34,384]{1,0:T(8,128)(2,1)S(1)}, u32[]{:S(2)}, u32[]{:S(2)}) collective-permute-start(bf16[34,384]{1,0:T(8,128)(2,1)S(1)} %pad_maximum_fusion.1), channel_id=1, source_target_pairs={{0,32},{1,33},{2,34},{3,35},{4,36},{5,37},{6,38},{7,39},{8,40},{9,... | collective-permute-start | bytes 78344 | tf_op jit(solution)/shard_map/ppermute | solution.py:32
  18.3 1.2 %collective-permute-start.3 = (bf16[34,384]{1,0:T(8,128)(2,1)S(1)}, bf16[34,384]{1,0:T(8,128)(2,1)S(1)}, u32[]{:S(2)}, u32[]{:S(2)}) collective-permute-start(bf16[34,384]{1,0:T(8,128)(2,1)S(1)} %pad_maximum_fusion.1), channel_id=1, source_target_pairs={{0,16},{1,17},{2,18},{3,19},{4,20},{5,21},{6,22},{7,23},{8,24},{9,... | collective-permute-start | bytes 78344 | tf_op jit(solution)/shard_map/ppermute | solution.py:32
  19.5 2.4 %collective-permute-start.5 = (bf16[34,384]{1,0:T(8,128)(2,1)S(1)}, bf16[34,384]{1,0:T(8,128)(2,1)S(1)}, u32[]{:S(2)}, u32[]{:S(2)}) collective-permute-start(bf16[34,384]{1,0:T(8,128)(2,1)S(1)} %pad_maximum_fusion.1), channel_id=1, source_target_pairs={{0,48},{1,49},{2,50},{3,51},{4,52},{5,53},{6,54},{7,55},{8,56},{9,... | collective-permute-start | bytes 78344 | tf_op jit(solution)/shard_map/ppermute | solution.py:32
  21.9 0.1 fusion
  21.9 0.0 collective-permute-done.4
  22.0 1.2 %collective-permute-done.3 = bf16[34,384]{1,0:T(8,128)(2,1)S(1)} collective-permute-done((bf16[34,384]{1,0:T(8,128)(2,1)S(1)}, bf16[34,384]{1,0:T(8,128)(2,1)S(1)}, u32[]{:S(2)}, u32[]{:S(2)}) %collective-permute-start.3) | collective-permute-done | bytes 26144 | tf_op jit(solution)/shard_map/ppermute | solution.py:32
  23.1 0.0 collective-permute-done.5
  23.2 2.8 %collective-permute-start.8 = (bf16[4,34,384]{2,1,0:T(8,128)(2,1)S(1)}, bf16[4,34,384]{2,1,0:T(8,128)(2,1)S(1)}, u32[]{:S(2)}, u32[]{:S(2)}) collective-permute-start(bf16[4,34,384]{2,1,0:T(8,128)(2,1)S(1)} %pad_maximum_fusion.p0), channel_id=1, source_target_pairs={{0,12},{1,13},{2,14},{3,15},{4,0},{5,1},{6,2},{7,3},{8,4},{9,5},{1... | collective-permute-start | bytes 313352 | tf_op jit(solution)/shard_map/ppermute | solution.py:32
  26.0 0.3 collective-permute-start.7
  26.3 0.7 collective-permute-start.6
  27.0 0.1 pad_add_fusion.at_ref
  27.1 2.0 %collective-permute-done.8.p3 = bf16[4,34,384]{2,1,0:T(8,128)(2,1)S(1)} collective-permute-done((bf16[4,34,384]{2,1,0:T(8,128)(2,1)S(1)}, bf16[4,34,384]{2,1,0:T(8,128)(2,1)S(1)}, u32[]{:S(2)}, u32[]{:S(2)}) %collective-permute-start.8) | collective-permute-done | bytes 104480 | tf_op jit(solution)/shard_map/ppermute | solution.py:32
  29.1 2.2 %collective-permute-done.7.p2 = bf16[4,34,384]{2,1,0:T(8,128)(2,1)S(1)} collective-permute-done((bf16[4,34,384]{2,1,0:T(8,128)(2,1)S(1)}, bf16[4,34,384]{2,1,0:T(8,128)(2,1)S(1)}, u32[]{:S(2)}, u32[]{:S(2)}) %collective-permute-start.7) | collective-permute-done | bytes 104480 | tf_op jit(solution)/shard_map/ppermute | solution.py:32
  31.3 1.2 %collective-permute-done.6.p1 = bf16[4,34,384]{2,1,0:T(8,128)(2,1)S(1)} collective-permute-done((bf16[4,34,384]{2,1,0:T(8,128)(2,1)S(1)}, bf16[4,34,384]{2,1,0:T(8,128)(2,1)S(1)}, u32[]{:S(2)}, u32[]{:S(2)}) %collective-permute-start.6) | collective-permute-done | bytes 104480 | tf_op jit(solution)/shard_map/ppermute | solution.py:32
  32.5 43.7 %forward_and_kernel_grad.1 = (bf16[256,6144]{1,0:T(8,128)(2,1)}, f32[48,288,128]{2,1,0:T(8,128)}, f32[64,32,128]{2,1,0:T(8,128)}, bf16[16,34,384]{2,1,0:T(8,128)(2,1)S(1)}) custom-call(s32[2]{0:T(128)S(1)} %pad_add_fusion.at_ref, bf16[256,6144]{1,0:T(8,128)(2,1)} %bitcast.18, bf16[256,6144]{1,0:T(8,128)(2,1)} %bitcast.19, ...), custom_call_target="tpu_custom_call" | custom-call | flops 195035136 | bytes 31457280 | tf_op jit(solution)/shard_map/forward_and_kernel_grad/pallas_call | solution.py:344
  76.2 3.7 %all-to-all-start = ((f32[16,4,32,128]{3,2,1,0:T(8,128)}), f32[16,4,32,128]{3,2,1,0:T(8,128)S(1)}, u32[]{:S(2)}, u32[]{:S(2)}) async-start(f32[16,4,32,128]{3,2,1,0:T(8,128)} %bitcast.21), calls=%async_computation | async-start | bytes 2097152 | tf_op jit(solution)/shard_map/all_to_all | solution.py:442
  79.9 12.3 %input_grad.2 = (bf16[256,6144]{1,0:T(8,128)(2,1)}, f32[32,128]{1,0:T(8,128)S(1)}) custom-call(f32[48,288,128]{2,1,0:T(8,128)} %get-tuple-element.23.gc_hbm, bf16[16,34,384]{2,1,0:T(8,128)(2,1)S(1)} %get-tuple-element.24.p_ref), custom_call_target="tpu_custom_call" | custom-call | flops 73138176 | bytes 7077888 | tf_op jit(solution)/shard_map/input_grad/pallas_call | solution.py:387
  92.2 0.0 all-to-all-done.came_ref
  92.2 0.6 sum_plane.1
  92.8 1.7 %collective-permute-start.9 = (f32[32,128]{1,0:T(8,128)S(1)}, f32[32,128]{1,0:T(8,128)S(1)}, u32[]{:S(2)}, u32[]{:S(2)}) collective-permute-start(f32[32,128]{1,0:T(8,128)S(1)} %get-tuple-element.30), channel_id=1, source_target_pairs={{0,16},{1,17},{2,18},{3,19},{4,20},{5,21},{6,22},{7,23},{8,24},{9,... | collective-permute-start | bytes 49160 | tf_op jit(solution)/shard_map/ppermute | solution.py:448
  94.4 6.2 %collective-permute-start.10 = (f32[32,128]{1,0:T(8,128)S(1)}, f32[32,128]{1,0:T(8,128)S(1)}, u32[]{:S(2)}, u32[]{:S(2)}) collective-permute-start(f32[32,128]{1,0:T(8,128)S(1)} %get-tuple-element.31), channel_id=1, source_target_pairs={{0,32},{1,33},{2,34},{3,35},{4,36},{5,37},{6,38},{7,39},{8,40},{9,... | collective-permute-start | bytes 49160 | tf_op jit(solution)/shard_map/ppermute | solution.py:448
  100.6 0.0 collective-permute-start.11
  100.6 5.4 %input_grad.3 = (bf16[256,6144]{1,0:T(8,128)(2,1)}, f32[32,128]{1,0:T(8,128)S(1)}) custom-call(f32[48,288,128]{2,1,0:T(8,128)} %get-tuple-element.23.gc_hbm, bf16[16,34,384]{2,1,0:T(8,128)(2,1)S(1)} %get-tuple-element.24.p_ref, bf16[256,6144]{1,0:T(8,128)(2,1)} %get-tuple-element.25.refs_0_), custom_call_target="tpu_custom_call", output_to_operand_aliasing={{0}: (2, {})} | custom-call | flops 24379392 | bytes 2359296 | tf_op jit(solution)/shard_map/input_grad/pallas_call | solution.py:387
  106.0 0.0 collective-permute-done.9.first
  106.0 0.0 collective-permute-done.10.second
  106.1 0.0 collective-permute-done.11.third
  106.1 6.3 %collective-permute-start.14 = (f32[32,128]{1,0:T(8,128)S(1)}, f32[32,128]{1,0:T(8,128)S(1)}, u32[]{:S(2)}, u32[]{:S(2)}) collective-permute-start(f32[32,128]{1,0:T(8,128)S(1)} %sum_column.1.own), channel_id=1, source_target_pairs={{0,192},{64,128},{128,64},{192,0},{1,193},{65,129},{129,65},{193,1... | collective-permute-start | bytes 49160 | tf_op jit(solution)/shard_map/ppermute | solution.py:427
  112.4 1.4 %collective-permute-start.13 = (f32[32,128]{1,0:T(8,128)S(1)}, f32[32,128]{1,0:T(8,128)S(1)}, u32[]{:S(2)}, u32[]{:S(2)}) collective-permute-start(f32[32,128]{1,0:T(8,128)S(1)} %sum_column.1.own), channel_id=1, source_target_pairs={{0,128},{64,192},{128,0},{192,64},{1,129},{65,193},{129,1},{193,65... | collective-permute-start | bytes 49160 | tf_op jit(solution)/shard_map/ppermute | solution.py:427
  113.8 0.0 collective-permute-start.12
  113.8 0.0 collective-permute-done.14.third
  113.8 1.4 %collective-permute-done.13.second = f32[32,128]{1,0:T(8,128)S(1)} collective-permute-done((f32[32,128]{1,0:T(8,128)S(1)}, f32[32,128]{1,0:T(8,128)S(1)}, u32[]{:S(2)}, u32[]{:S(2)}) %collective-permute-start.13) | collective-permute-done | bytes 16416 | tf_op jit(solution)/shard_map/ppermute | solution.py:427
  115.2 0.0 collective-permute-done.12.first
  115.2 0.6 finish.1
  (2 shorter events, 0.0 us)
Async XLA Ops:
  1.4 5.1 %collective-permute-start.1 = (bf16[34,96]{1,0:T(8,128)(2,1)S(1)}, bf16[34,96]{1,0:T(8,128)(2,1)S(1)}, u32[]{:S(2)}, u32[]{:S(2)}) collective-permute-start(bf16[34,96]{1,0:T(8,128)(2,1)S(1)} %pad_maximum_fusion.2), channel_id=1, source_target_pairs={{0,2},{1,3},{2,0},{3,1},{4,6},{5,7},{6,4},{7,5},{8,10},{9,11},{10,... | collective-permute-start | bytes 19592 | tf_op jit(solution)/shard_map/ppermute | solution.py:32
  5.1 2.6 %collective-permute-start.2 = (bf16[34,96]{1,0:T(8,128)(2,1)S(1)}, bf16[34,96]{1,0:T(8,128)(2,1)S(1)}, u32[]{:S(2)}, u32[]{:S(2)}) collective-permute-start(bf16[34,96]{1,0:T(8,128)(2,1)S(1)} %pad_maximum_fusion.2), channel_id=1, source_target_pairs={{0,3},{1,0},{2,1},{3,2},{4,7},{5,4},{6,5},{7,6},{8,11},{9,8},{10,9... | collective-permute-start | bytes 19592 | tf_op jit(solution)/shard_map/ppermute | solution.py:32
  5.9 3.7 %collective-permute-start = (bf16[34,96]{1,0:T(8,128)(2,1)S(1)}, bf16[34,96]{1,0:T(8,128)(2,1)S(1)}, u32[]{:S(2)}, u32[]{:S(2)}) collective-permute-start(bf16[34,96]{1,0:T(8,128)(2,1)S(1)} %pad_maximum_fusion.2), channel_id=1, source_target_pairs={{0,1},{1,2},{2,3},{3,0},{4,5},{5,6},{6,7},{7,4},{8,9},{9,10},{10,1... | collective-permute-start | bytes 19592 | tf_op jit(solution)/shard_map/ppermute | solution.py:32
  11.3 10.7 %collective-permute-start.4 = (bf16[34,384]{1,0:T(8,128)(2,1)S(1)}, bf16[34,384]{1,0:T(8,128)(2,1)S(1)}, u32[]{:S(2)}, u32[]{:S(2)}) collective-permute-start(bf16[34,384]{1,0:T(8,128)(2,1)S(1)} %pad_maximum_fusion.1), channel_id=1, source_target_pairs={{0,32},{1,33},{2,34},{3,35},{4,36},{5,37},{6,38},{7,39},{8,40},{9,... | collective-permute-start | bytes 78344 | tf_op jit(solution)/shard_map/ppermute | solution.py:32
  18.3 4.9 %collective-permute-start.3 = (bf16[34,384]{1,0:T(8,128)(2,1)S(1)}, bf16[34,384]{1,0:T(8,128)(2,1)S(1)}, u32[]{:S(2)}, u32[]{:S(2)}) collective-permute-start(bf16[34,384]{1,0:T(8,128)(2,1)S(1)} %pad_maximum_fusion.1), channel_id=1, source_target_pairs={{0,16},{1,17},{2,18},{3,19},{4,20},{5,21},{6,22},{7,23},{8,24},{9,... | collective-permute-start | bytes 78344 | tf_op jit(solution)/shard_map/ppermute | solution.py:32
  19.5 3.7 %collective-permute-start.5 = (bf16[34,384]{1,0:T(8,128)(2,1)S(1)}, bf16[34,384]{1,0:T(8,128)(2,1)S(1)}, u32[]{:S(2)}, u32[]{:S(2)}) collective-permute-start(bf16[34,384]{1,0:T(8,128)(2,1)S(1)} %pad_maximum_fusion.1), channel_id=1, source_target_pairs={{0,48},{1,49},{2,50},{3,51},{4,52},{5,53},{6,54},{7,55},{8,56},{9,... | collective-permute-start | bytes 78344 | tf_op jit(solution)/shard_map/ppermute | solution.py:32
  23.2 6.0 %collective-permute-start.8 = (bf16[4,34,384]{2,1,0:T(8,128)(2,1)S(1)}, bf16[4,34,384]{2,1,0:T(8,128)(2,1)S(1)}, u32[]{:S(2)}, u32[]{:S(2)}) collective-permute-start(bf16[4,34,384]{2,1,0:T(8,128)(2,1)S(1)} %pad_maximum_fusion.p0), channel_id=1, source_target_pairs={{0,12},{1,13},{2,14},{3,15},{4,0},{5,1},{6,2},{7,3},{8,4},{9,5},{1... | collective-permute-start | bytes 313352 | tf_op jit(solution)/shard_map/ppermute | solution.py:32
  26.0 5.3 %collective-permute-start.7 = (bf16[4,34,384]{2,1,0:T(8,128)(2,1)S(1)}, bf16[4,34,384]{2,1,0:T(8,128)(2,1)S(1)}, u32[]{:S(2)}, u32[]{:S(2)}) collective-permute-start(bf16[4,34,384]{2,1,0:T(8,128)(2,1)S(1)} %pad_maximum_fusion.p0), channel_id=1, source_target_pairs={{0,8},{1,9},{2,10},{3,11},{4,12},{5,13},{6,14},{7,15},{8,0},{9,1},... | collective-permute-start | bytes 313352 | tf_op jit(solution)/shard_map/ppermute | solution.py:32
  26.3 6.2 %collective-permute-start.6 = (bf16[4,34,384]{2,1,0:T(8,128)(2,1)S(1)}, bf16[4,34,384]{2,1,0:T(8,128)(2,1)S(1)}, u32[]{:S(2)}, u32[]{:S(2)}) collective-permute-start(bf16[4,34,384]{2,1,0:T(8,128)(2,1)S(1)} %pad_maximum_fusion.p0), channel_id=1, source_target_pairs={{0,4},{1,5},{2,6},{3,7},{4,8},{5,9},{6,10},{7,11},{8,12},{9,13},{1... | collective-permute-start | bytes 313352 | tf_op jit(solution)/shard_map/ppermute | solution.py:32
  76.2 16.0 %all-to-all-start = ((f32[16,4,32,128]{3,2,1,0:T(8,128)}), f32[16,4,32,128]{3,2,1,0:T(8,128)S(1)}, u32[]{:S(2)}, u32[]{:S(2)}) async-start(f32[16,4,32,128]{3,2,1,0:T(8,128)} %bitcast.21), calls=%async_computation | async-start | bytes 2097152 | tf_op jit(solution)/shard_map/all_to_all | solution.py:442
  92.8 13.3 %collective-permute-start.9 = (f32[32,128]{1,0:T(8,128)S(1)}, f32[32,128]{1,0:T(8,128)S(1)}, u32[]{:S(2)}, u32[]{:S(2)}) collective-permute-start(f32[32,128]{1,0:T(8,128)S(1)} %get-tuple-element.30), channel_id=1, source_target_pairs={{0,16},{1,17},{2,18},{3,19},{4,20},{5,21},{6,22},{7,23},{8,24},{9,... | collective-permute-start | bytes 49160 | tf_op jit(solution)/shard_map/ppermute | solution.py:448
  94.4 11.6 %collective-permute-start.10 = (f32[32,128]{1,0:T(8,128)S(1)}, f32[32,128]{1,0:T(8,128)S(1)}, u32[]{:S(2)}, u32[]{:S(2)}) collective-permute-start(f32[32,128]{1,0:T(8,128)S(1)} %get-tuple-element.31), channel_id=1, source_target_pairs={{0,32},{1,33},{2,34},{3,35},{4,36},{5,37},{6,38},{7,39},{8,40},{9,... | collective-permute-start | bytes 49160 | tf_op jit(solution)/shard_map/ppermute | solution.py:448
  100.6 5.4 %collective-permute-start.11 = (f32[32,128]{1,0:T(8,128)S(1)}, f32[32,128]{1,0:T(8,128)S(1)}, u32[]{:S(2)}, u32[]{:S(2)}) collective-permute-start(f32[32,128]{1,0:T(8,128)S(1)} %get-tuple-element.32), channel_id=1, source_target_pairs={{0,48},{1,49},{2,50},{3,51},{4,52},{5,53},{6,54},{7,55},{8,56},{9,... | collective-permute-start | bytes 49160 | tf_op jit(solution)/shard_map/ppermute | solution.py:448
  106.1 7.7 %collective-permute-start.14 = (f32[32,128]{1,0:T(8,128)S(1)}, f32[32,128]{1,0:T(8,128)S(1)}, u32[]{:S(2)}, u32[]{:S(2)}) collective-permute-start(f32[32,128]{1,0:T(8,128)S(1)} %sum_column.1.own), channel_id=1, source_target_pairs={{0,192},{64,128},{128,64},{192,0},{1,193},{65,129},{129,65},{193,1... | collective-permute-start | bytes 49160 | tf_op jit(solution)/shard_map/ppermute | solution.py:427
  112.4 2.8 %collective-permute-start.13 = (f32[32,128]{1,0:T(8,128)S(1)}, f32[32,128]{1,0:T(8,128)S(1)}, u32[]{:S(2)}, u32[]{:S(2)}) collective-permute-start(f32[32,128]{1,0:T(8,128)S(1)} %sum_column.1.own), channel_id=1, source_target_pairs={{0,128},{64,192},{128,0},{192,64},{1,129},{65,193},{129,1},{193,65... | collective-permute-start | bytes 49160 | tf_op jit(solution)/shard_map/ppermute | solution.py:427
  113.8 1.4 %collective-permute-start.12 = (f32[32,128]{1,0:T(8,128)S(1)}, f32[32,128]{1,0:T(8,128)S(1)}, u32[]{:S(2)}, u32[]{:S(2)}) collective-permute-start(f32[32,128]{1,0:T(8,128)S(1)} %sum_column.1.own), channel_id=1, source_target_pairs={{0,64},{64,0},{128,192},{192,128},{1,65},{65,1},{129,193},{193,129... | collective-permute-start | bytes 49160 | tf_op jit(solution)/shard_map/ppermute | solution.py:427

commit v6 on v5

--- a/solution.py
+++ b/solution.py
@@ -26,25 +26,29 @@
     return pairs
 
 
-def gather_stage(block, axis_stride):
-    at = (lax.axis_index("shard") // axis_stride) % SIDE
-    came = [block] + [
-        lax.ppermute(block, "shard", shifted(axis_stride, step)) for step in range(1, SIDE)
-    ]
-    return came, [lax.select_n((at - slot) % SIDE, *came) for slot in range(SIDE)]
+def plane_groups():
+    plane = SIDE * SIDE
+    return [list(range(z * plane, (z + 1) * plane)) for z in range(SIDE)]
 
 
 def gather_channels(packed):
-    group = jnp.concatenate(gather_stage(packed, 1)[1], axis=1)
-    column = jnp.stack(gather_stage(group, 16)[0], 0)
-    return gather_stage(column, 4)[0]
-
-
-def place_params(came_refs, at_z, at_y, p_ref):
-    for y, came in enumerate(came_refs):
-        for z in range(SIDE):
-            group = lax.rem(at_z - z + SIDE, SIDE) * SIDE + lax.rem(at_y - y + SIDE, SIDE)
-            p_ref[group] = came[z]
+    stride = SIDE * SIDE
+    column = jnp.concatenate(
+        [packed] + [lax.ppermute(packed, "shard", shifted(stride, step)) for step in range(1, SIDE)]
+    )
+    same = jnp.broadcast_to(column[None], (stride,) + column.shape)
+    return lax.all_to_all(same, "shard", 0, 0, axis_index_groups=plane_groups())
+
+
+def place_params(came, at_z, p_ref):
+    rows = p_ref.shape[1]
+    for y in range(SIDE):
+        for slot in range(SIDE):
+            group = lax.rem(at_z - slot + SIDE, SIDE) * SIDE + y
+            at = slice(slot * rows, (slot + 1) * rows)
+            p_ref[group] = jnp.concatenate(
+                [came[y * SIDE + x, at, :] for x in range(SIDE)], axis=1
+            )
 
 
 def bcast_row(ref, row):
@@ -52,8 +56,8 @@
 
 
 def forward_and_kernel_grad(
-    taps, at_ref, x_hbm, ct_hbm, p0, p1, p2, p3, act_hbm, gc_hbm, gr_ref, p_hbm,
-    xb, cb, ab, xs, cv, gn, gc, pf, st, s1, s2, row_a, row_b, p_ref, x_sem, c_sem, a_sem, g_sem, p_sem,
+    taps, at_ref, x_hbm, ct_hbm, came_ref, act_hbm, gc_hbm, gr_ref, p_hbm,
+    xb, cb, ab, xs, xe, xo, xt, fa, fb, fc, cv, gn, gc, pf, st, s1, s2, row_a, row_b, p_ref, x_sem, c_sem, a_sem, g_sem, p_sem,
 ):
     frames, width = xb.shape
     tiles = width // LANES
@@ -93,7 +97,7 @@
         x_copy(chunk).start()
     for chunk in range(chunks):
         c_copy(chunk).start()
-    place_params((p0, p1, p2, p3), at_ref[0], at_ref[1], p_ref)
+    place_params(came_ref, at_ref[0], p_ref)
     p_copy = pltpu.make_async_copy(p_ref, p_hbm, p_sem)
     p_copy.start()
     st[...] = jnp.zeros_like(st)
@@ -108,27 +112,63 @@
     s1[...] = jnp.zeros_like(s1)
     s2[...] = jnp.zeros_like(s2)
 
+    for edge in (0, SUB, PAD + frames, PAD + frames + SUB, PAD + frames + 2 * SUB):
+        xs[pl.ds(edge, SUB), :] = zero
+
     def conv_tile(tile, _):
         load_params(tile)
         for edge in (0, SUB, PAD + frames, PAD + frames + SUB):
-            xs[tile, pl.ds(edge, SUB), :] = zero
             gc[tile, pl.ds(edge, SUB), :] = zero
-        xs[tile, pl.ds(PAD, frames), :] = xb[:, lanes_of(tile)].astype(F32)
-        weights = [bcast_row(pf, j) for j in range(taps)]
+        xs[pl.ds(PAD, frames), :] = xb[:, lanes_of(tile)].astype(F32)
+        half = rows // 2
+        xo[tile, pl.ds(SUB * (half + 2), SUB), :] = zero
+        for r in range(half + 2):
+            at = pl.ds(SUB * r, SUB)
+            even = xs[pl.ds(2 * SUB * r + 1, SUB, stride=2), :]
+            odd = xs[pl.ds(2 * SUB * r + 2, SUB, stride=2), :]
+            xe[tile, at, :] = even
+            xo[tile, at, :] = odd
+            xt[tile, at, :] = even + odd
         bias = bcast_row(pf, taps)
-        for r0 in range(0, rows, block):
-            acc = [bias] * block
-            for phase in range(SUB):
-                depth = len(range(phase, taps, SUB))
-                for i in range(block + depth - 1):
-                    value = xs[tile, pl.ds(SUB * (r0 + i) + phase + 1, SUB), :]
-                    for q in range(depth):
-                        if 0 <= i - q < block:
-                            acc[i - q] = acc[i - q] + value * weights[phase + SUB * q]
-            for b in range(block):
-                at = pl.ds(SUB * (r0 + b), SUB)
-                cv[tile, at, :] = acc[b]
-                s1[at, :] += acc[b]
+
+        def run(source, weights, first, count, start, store):
+            for r0 in range(0, count, block):
+                size = min(block, count - r0)
+                acc = [start] * size
+                for phase in range(SUB):
+                    depth = len(range(phase, len(weights), SUB))
+                    for i in range(size + depth - 1):
+                        value = source[tile, pl.ds(SUB * (r0 + i) + phase + first, SUB), :]
+                        for q in range(depth):
+                            if 0 <= i - q < size:
+                                term = value * weights[phase + SUB * q]
+                                before = acc[i - q]
+                                acc[i - q] = term if before is None else before + term
+                for b in range(size):
+                    store(r0 + b, acc[b])
+
+        w_even = [bcast_row(pf, 2 * e) for e in range(taps // 2 + 1)]
+        w_odd = [bcast_row(pf, 2 * e + 1) for e in range(taps // 2)]
+
+        def keep(ref):
+            def store(r, value):
+                ref[pl.ds(SUB * r, SUB), :] = value
+            return store
+
+        run(xo, w_odd, 0, half + 1, None, keep(fb))
+        run(xe, w_even, 0, half, bias, keep(fa))
+        w_both = [w_even[0]] + [w_even[e] + w_odd[e - 1] for e in range(1, len(w_even))]
+
+        def last(r, value):
+            here = pl.ds(SUB * r, SUB)
+            own, before, after = fa[here, :], fb[here, :], fb[pl.ds(SUB * r + 1, SUB), :]
+            cv[tile, pl.ds(2 * SUB * r, SUB, stride=2), :] = own + before
+            cv[tile, pl.ds(2 * SUB * r + 1, SUB, stride=2), :] = (value - own) - after + (bias + bias)
+
+        run(xt, w_both, 0, half, None, last)
+        for r in range(rows):
+            at = pl.ds(SUB * r, SUB)
+            s1[at, :] += cv[tile, at, :]
         return 0
 
     def conv_chunk(chunk, _):
@@ -199,10 +239,8 @@
     s2[...] = jnp.broadcast_to(mean_gnn, s2.shape)
 
     def grad_tile(tile, _):
-        acc = [zero] * taps
         total = zero
         for r0 in range(0, rows, block):
-            held = []
             for b in range(block):
                 at = pl.ds(SUB * (r0 + b), SUB)
                 grad = row_b[at, :] * (
@@ -210,16 +248,40 @@
                 )
                 gc[tile, pl.ds(PAD + SUB * (r0 + b), SUB), :] = grad
                 total = total + grad
-                held.append(grad)
-            for phase in range(SUB):
-                depth = len(range(phase, taps, SUB))
-                for i in range(block + depth - 1):
-                    value = xs[tile, pl.ds(SUB * (r0 + i) + phase + 1, SUB), :]
-                    for q in range(depth):
-                        if 0 <= i - q < block:
-                            acc[phase + SUB * q] = acc[phase + SUB * q] + value * held[i - q]
-        for j in range(taps):
-            st[tile, pl.ds(j, 1), :] = jnp.sum(acc[j], axis=0, keepdims=True)
+        half = rows // 2
+        for r in range(half):
+            here = pl.ds(SUB * r, SUB)
+            g_even = gc[tile, pl.ds(PAD + 2 * SUB * r, SUB, stride=2), :]
+            g_odd = gc[tile, pl.ds(PAD + 2 * SUB * r + 1, SUB, stride=2), :]
+            fa[here, :] = g_even - g_odd
+            fc[here, :] = g_odd
+        for r in range(half + 1):
+            g_even = gc[tile, pl.ds(PAD + 2 * SUB * r, SUB, stride=2), :]
+            g_before = gc[tile, pl.ds(PAD + 2 * SUB * r - 1, SUB, stride=2), :]
+            fb[pl.ds(SUB * r, SUB), :] = g_even - g_before
+
+        def corr(source, grads, count, size):
+            acc = [zero] * size
+            for r0 in range(0, count, block):
+                many = min(block, count - r0)
+                held = [grads[pl.ds(SUB * (r0 + b), SUB), :] for b in range(many)]
+                for phase in range(SUB):
+                    depth = len(range(phase, size, SUB))
+                    for i in range(many + depth - 1):
+                        value = source[tile, pl.ds(SUB * (r0 + i) + phase, SUB), :]
+                        for q in range(depth):
+                            if 0 <= i - q < many:
+                                acc[phase + SUB * q] = acc[phase + SUB * q] + value * held[i - q]
+            return acc
+
+        d_even = corr(xe, fa, half, taps // 2 + 1)
+        d_both = corr(xt, fc, half, taps // 2 + 1)
+        for e in range(taps // 2 + 1):
+            st[tile, pl.ds(2 * e, 1), :] = jnp.sum(d_even[e] + d_both[e], axis=0, keepdims=True)
+        d_odd = corr(xo, fb, half + 1, taps // 2)
+        for e in range(taps // 2):
+            both = d_odd[e] + d_both[e + 1]
+            st[tile, pl.ds(2 * e + 1, 1), :] = jnp.sum(both, axis=0, keepdims=True)
         st[tile, pl.ds(taps, 1), :] = jnp.sum(total, axis=0, keepdims=True)
         return 0
 
@@ -337,8 +399,8 @@
     frames, width = x.shape
     tiles = width // LANES
     chunks = 8
-    rows = params[0].shape[1]
-    groups = (SIDE * SIDE,) + params[0].shape[1:]
+    rows = params.shape[1] // SIDE
+    groups = (SIDE * SIDE, rows, SIDE * params.shape[2])
     padded = frames + 2 * PAD
     whole = (tiles, frames, LANES)
     return pl.pallas_call(
@@ -347,15 +409,21 @@
             jax.ShapeDtypeStruct((frames, width), jnp.bfloat16),
             jax.ShapeDtypeStruct((tiles, padded, LANES), F32),
             jax.ShapeDtypeStruct((SIDE**3, MAIN, LANES), F32),
-            jax.ShapeDtypeStruct(groups, params[0].dtype),
+            jax.ShapeDtypeStruct(groups, params.dtype),
         ),
-        in_specs=[pl.BlockSpec(memory_space=pltpu.SMEM), ANY, ANY] + [HELD] * SIDE,
+        in_specs=[pl.BlockSpec(memory_space=pltpu.SMEM), ANY, ANY, HELD],
         out_specs=(ANY, ANY, HELD, ANY),
         scratch_shapes=[
             pltpu.VMEM((frames, width), jnp.bfloat16),
             pltpu.VMEM((frames, width), jnp.bfloat16),
             pltpu.VMEM((frames, width), jnp.bfloat16),
-            pltpu.VMEM((tiles, padded, LANES), F32),
+            pltpu.VMEM((padded + SUB, LANES), F32),
+            pltpu.VMEM((tiles, frames // 2 + 3 * SUB, LANES), F32),
+            pltpu.VMEM((tiles, frames // 2 + 3 * SUB, LANES), F32),
+            pltpu.VMEM((tiles, frames // 2 + 3 * SUB, LANES), F32),
+            pltpu.VMEM((frames // 2, LANES), F32),
+            pltpu.VMEM((frames // 2 + SUB, LANES), F32),
+            pltpu.VMEM((frames // 2, LANES), F32),
             pltpu.VMEM(whole, F32),
             pltpu.VMEM(whole, F32),
             pltpu.VMEM((tiles, padded, LANES), F32),
@@ -365,7 +433,7 @@
             pltpu.VMEM((frames, LANES), F32),
             pltpu.VMEM((frames, LANES), F32),
             pltpu.VMEM((frames, LANES), F32),
-            pltpu.VMEM(groups, params[0].dtype),
+            pltpu.VMEM(groups, params.dtype),
             pltpu.SemaphoreType.DMA((chunks,)),
             pltpu.SemaphoreType.DMA((chunks,)),
             pltpu.SemaphoreType.DMA((chunks,)),
@@ -377,7 +445,7 @@
             flops=4 * taps * frames * width, bytes_accessed=20 * frames * width, transcendentals=0
         ),
         name="forward_and_kernel_grad",
-    )(place, x, cotangent, *params)
+    )(place, x, cotangent, params)
 
 
 def run_second(grad_conv, params, taps, frames, width, chunks, begun=None):
@@ -433,14 +501,13 @@
     packed = jnp.concatenate([kernel, conv_bias[None], ln_gain[None], ln_bias[None]], 0)
     params = gather_channels(packed)
     me = lax.axis_index("shard")
-    place = jnp.stack([me // (SIDE * SIDE), (me // SIDE) % SIDE])
+    place = (me // (SIDE * SIDE))[None]
     activated, grad_conv, pieces, groups = run_first(
         conv_input[0], cotangent[0], place, params, taps
     )
     part_of = functools.partial(run_second, grad_conv, groups, taps, frames, width)
-    planes = [list(range(z * SIDE * SIDE, (z + 1) * SIDE * SIDE)) for z in range(SIDE)]
     came = lax.all_to_all(
-        pieces.reshape(SIDE * SIDE, SIDE, MAIN, LANES), "shard", 0, 0, axis_index_groups=planes
+        pieces.reshape(SIDE * SIDE, SIDE, MAIN, LANES), "shard", 0, 0, axis_index_groups=plane_groups()
     )
     begun, zeros = part_of((0, EARLY))
     piece = jax.ShapeDtypeStruct(zeros.shape, F32)

time: 116 us -> 116 us (level)
  waiting for transfers between devices: 11.2 us -> 16.7 us
  starting transfers between devices: 38.8 us -> 34.5 us
  Pallas kernels: 62.6 us -> 59.1 us
  local copies, waits for them, and re-layouts: 0 us -> 3.36 us
  other arithmetic: 2.57 us -> 0.76 us
    all_to_all x0 -> x1, waiting for transfers between devices: none -> 9.64 us  [gather_channels(): return lax.all_to_all(same, 'shard', 0, 0, axis_index_groups=plane_groups())]
    ppermute x9 -> x3, starting transfers between devices: 19.5 us -> 10.2 us  [gather_channels(): lax.ppermute(packed, 'shard', shifted(stride, step))]
    all_to_all x0 -> x1, starting transfers between devices: none -> 6.75 us  [gather_channels(): return lax.all_to_all(same, 'shard', 0, 0, axis_index_groups=plane_groups())]
    ppermute x9 -> x3, waiting for transfers between devices: 9.75 us -> 3.18 us  [gather_channels(): lax.ppermute(packed, 'shard', shifted(stride, step))]
    pallas_call x1, Pallas kernels: 43.7 us -> 40.7 us  [run_first(): pl.pallas_call(functools.partial(forward_and_kernel_grad, taps), out_shap...]
    concatenate x0 -> x1, local copies, waits for them, and re-layouts: none -> 2.49 us  [gather_channels(): jnp.concatenate([packed] + [lax.ppermute(packed, 'shard', shifted(stride,...]
    all_to_all x1, waiting for transfers between devices: 0.01 us -> 1.71 us  [per_device(): lax.all_to_all(pieces.reshape(SIDE * SIDE, SIDE, MAIN, LANES), 'shard', 0...]
    select_n x2 -> x0, other arithmetic: 1.54 us -> none  [gather_stage(): lax.select_n((at - slot) % SIDE, *came)]
  transfers between devices with their start and end apart: 16 -> 11, of which waited for: 7 -> 5; matrix products, arithmetic and copies ran while one was open for 0% -> 0% of each run, Pallas kernels for 15% -> 15%
where the time goes in v6:
time: 116 us; the launch traced here: 115 us
  Pallas kernels  59.1 us (51%)
  starting transfers between devices  34.5 us (30%)
  waiting for transfers between devices  16.7 us (14%)
  local copies, waits for them, and re-layouts  3.36 us (3%)
    pallas_call x1, Pallas kernels, run_first(): pl.pallas_call(functools.partial(forward_and_kernel_grad, taps), out_shap...  40.7 us
    pallas_call x2, Pallas kernels, run_second(): pl.pallas_call(functools.partial(input_grad, taps, chunks), out_shape=(ja...  17.7 us
    ppermute x3, starting transfers between devices, gather_channels(): lax.ppermute(packed, 'shard', shifted(stride, step))  10.2 us
    all_to_all x1, waiting for transfers between devices, gather_channels(): return lax.all_to_all(same, 'shard', 0, 0, axis_index_groups=plane_groups())  9.64 us
    ppermute x3, starting transfers between devices, over_rep(): return lax.ppermute(block, 'rep', [(i, i ^ step) for i in range(4)])  7.01 us
    ppermute x3, starting transfers between devices, per_device(): lax.ppermute(sums[s], 'shard', shifted(SIDE * SIDE, s))  6.86 us
    all_to_all x1, starting transfers between devices, gather_channels(): return lax.all_to_all(same, 'shard', 0, 0, axis_index_groups=plane_groups())  6.75 us
    all_to_all x1, starting transfers between devices, per_device(): lax.all_to_all(pieces.reshape(SIDE * SIDE, SIDE, MAIN, LANES), 'shard', 0...  3.66 us
  transfers between devices with their start and end apart: 11, of which 5 were waited for; matrix products, arithmetic and copies ran while one was open for 0% of the time, Pallas kernels for 15%

profile of v6, /device:TPU:1, one launch (start us, length us, event | category | flops | bytes accessed | tf_op | source)
XLA Modules:
  0.0 115.2 jit_solution(4571664865040207960)
XLA Ops:
  0.6 0.8 pad_maximum_fusion
  1.4 6.9 %collective-permute-start.2 = (bf16[34,96]{1,0:T(8,128)(2,1)S(1)}, bf16[34,96]{1,0:T(8,128)(2,1)S(1)}, u32[]{:S(2)}, u32[]{:S(2)}) collective-permute-start(bf16[34,96]{1,0:T(8,128)(2,1)S(1)} %pad_maximum_fusion), channel_id=1, source_target_pairs={{0,48},{1,49},{2,50},{3,51},{4,52},{5,53},{6,54},{7,55},{8,56},{9,... | collective-permute-start | bytes 19592 | tf_op jit(solution)/shard_map/ppermute | solution.py:37
  8.3 1.0 collective-permute-start.1
  9.3 2.3 %collective-permute-start = (bf16[34,96]{1,0:T(8,128)(2,1)S(1)}, bf16[34,96]{1,0:T(8,128)(2,1)S(1)}, u32[]{:S(2)}, u32[]{:S(2)}) collective-permute-start(bf16[34,96]{1,0:T(8,128)(2,1)S(1)} %pad_maximum_fusion), channel_id=1, source_target_pairs={{0,16},{1,17},{2,18},{3,19},{4,20},{5,21},{6,22},{7,23},{8,24},{9,... | collective-permute-start | bytes 19592 | tf_op jit(solution)/shard_map/ppermute | solution.py:37
  11.6 0.0 collective-permute-done.2
  11.6 3.2 %collective-permute-done.1 = bf16[34,96]{1,0:T(8,128)(2,1)S(1)} collective-permute-done((bf16[34,96]{1,0:T(8,128)(2,1)S(1)}, bf16[34,96]{1,0:T(8,128)(2,1)S(1)}, u32[]{:S(2)}, u32[]{:S(2)}) %collective-permute-start.1) | collective-permute-done | bytes 6560 | tf_op jit(solution)/shard_map/ppermute | solution.py:37
  14.8 0.0 collective-permute-done
  14.8 2.5 %concatenate.8 = bf16[136,96]{1,0:T(8,128)(2,1)S(1)} concatenate(bf16[31,96]{1,0:T(8,128)(2,1)} %param.8, bf16[1,96]{1,0:T(2,128)(2,1)} %bitcast.17, bf16[1,96]{1,0:T(2,128)(2,1)} %bitcast.19, bf16[1,96]{1,0:T(2,128)(2,1)} %bitcast.21, bf16[34,96]{1,0:T(8,128)(2,1)S(1)} %collective-permute-done, bf16[34,96]{1,0:T(8,128)(2,1)S(1)} %collective-permute-done.1, ...), dimensions={0} | concatenate | bytes 52224 | tf_op jit(solution)/shard_map/concatenate | solution.py:36
  17.2 0.9 broadcast_in_dim.28
  18.1 6.8 %all-to-all-start = ((bf16[16,136,96]{2,1,0:T(8,128)(2,1)}), bf16[16,136,96]{2,1,0:T(8,128)(2,1)S(1)}, u32[]{:S(2)}, u32[]{:S(2)}) async-start(bf16[16,136,96]{2,1,0:T(8,128)(2,1)} %broadcast_in_dim.28), calls=%async_computation | async-start | bytes 1114112 | tf_op jit(solution)/shard_map/all_to_all | solution.py:40
  24.9 9.6 %all-to-all-done.came_ref = bf16[16,136,96]{2,1,0:T(8,128)(2,1)S(1)} async-done(((bf16[16,136,96]{2,1,0:T(8,128)(2,1)}), bf16[16,136,96]{2,1,0:T(8,128)(2,1)S(1)}, u32[]{:S(2)}, u32[]{:S(2)}) %all-to-all-start) | async-done | bytes 417824 | tf_op jit(solution)/shard_map/all_to_all | solution.py:40
  34.5 40.7 %forward_and_kernel_grad.1 = (bf16[256,6144]{1,0:T(8,128)(2,1)}, f32[48,288,128]{2,1,0:T(8,128)}, f32[64,32,128]{2,1,0:T(8,128)}, bf16[16,34,384]{2,1,0:T(8,128)(2,1)S(1)}) custom-call(s32[1]{0:T(128)} %bitcast.at_ref, bf16[256,6144]{1,0:T(8,128)(2,1)} %bitcast.12, bf16[256,6144]{1,0:T(8,128)(2,1)} %bitcast.13, bf16[16,136,96]{2,1,0:T(8,128)(2,1)S(1)} %all-to-all-done.came_ref), custom_call_target="tpu_custom_call" | custom-call | flops 195035136 | bytes 31457280 | tf_op jit(solution)/shard_map/forward_and_kernel_grad/pallas_call | solution.py:406
  75.3 3.7 %all-to-all-start.1 = ((f32[16,4,32,128]{3,2,1,0:T(8,128)}), f32[16,4,32,128]{3,2,1,0:T(8,128)S(1)}, u32[]{:S(2)}, u32[]{:S(2)}) async-start(f32[16,4,32,128]{3,2,1,0:T(8,128)} %bitcast.15), calls=%async_computation.1 | async-start | bytes 2097152 | tf_op jit(solution)/shard_map/all_to_all | solution.py:509
  78.9 12.3 %input_grad.2 = (bf16[256,6144]{1,0:T(8,128)(2,1)}, f32[32,128]{1,0:T(8,128)S(1)}) custom-call(f32[48,288,128]{2,1,0:T(8,128)} %get-tuple-element.23.gc_hbm, bf16[16,34,384]{2,1,0:T(8,128)(2,1)S(1)} %get-tuple-element.24.p_ref), custom_call_target="tpu_custom_call" | custom-call | flops 73138176 | bytes 7077888 | tf_op jit(solution)/shard_map/input_grad/pallas_call | solution.py:455
  91.2 1.7 %all-to-all-done.1.came_ref = f32[16,4,32,128]{3,2,1,0:T(8,128)S(1)} async-done(((f32[16,4,32,128]{3,2,1,0:T(8,128)}), f32[16,4,32,128]{3,2,1,0:T(8,128)S(1)}, u32[]{:S(2)}, u32[]{:S(2)}) %all-to-all-start.1) | async-done | bytes 1048608 | tf_op jit(solution)/shard_map/all_to_all | solution.py:509
  92.9 0.1 sum_plane.1
  93.0 0.1 collective-permute-start.3
  93.1 3.3 %collective-permute-start.4 = (f32[32,128]{1,0:T(8,128)S(1)}, f32[32,128]{1,0:T(8,128)S(1)}, u32[]{:S(2)}, u32[]{:S(2)}) collective-permute-start(f32[32,128]{1,0:T(8,128)S(1)} %get-tuple-element.31), channel_id=1, source_target_pairs={{0,32},{1,33},{2,34},{3,35},{4,36},{5,37},{6,38},{7,39},{8,40},{9,... | collective-permute-start | bytes 49160 | tf_op jit(solution)/shard_map/ppermute | solution.py:515
  96.4 3.5 %collective-permute-start.5 = (f32[32,128]{1,0:T(8,128)S(1)}, f32[32,128]{1,0:T(8,128)S(1)}, u32[]{:S(2)}, u32[]{:S(2)}) collective-permute-start(f32[32,128]{1,0:T(8,128)S(1)} %get-tuple-element.32), channel_id=1, source_target_pairs={{0,48},{1,49},{2,50},{3,51},{4,52},{5,53},{6,54},{7,55},{8,56},{9,... | collective-permute-start | bytes 49160 | tf_op jit(solution)/shard_map/ppermute | solution.py:515
  99.9 5.4 %input_grad.3 = (bf16[256,6144]{1,0:T(8,128)(2,1)}, f32[32,128]{1,0:T(8,128)S(1)}) custom-call(f32[48,288,128]{2,1,0:T(8,128)} %get-tuple-element.23.gc_hbm, bf16[16,34,384]{2,1,0:T(8,128)(2,1)S(1)} %get-tuple-element.24.p_ref, bf16[256,6144]{1,0:T(8,128)(2,1)} %get-tuple-element.25.refs_0_), custom_call_target="tpu_custom_call", output_to_operand_aliasing={{0}: (2, {})} | custom-call | flops 24379392 | bytes 2359296 | tf_op jit(solution)/shard_map/input_grad/pallas_call | solution.py:455
  105.3 0.0 collective-permute-done.3.first
  105.3 0.0 collective-permute-done.4.second
  105.3 0.0 collective-permute-done.5.third
  105.3 6.3 %collective-permute-start.8 = (f32[32,128]{1,0:T(8,128)S(1)}, f32[32,128]{1,0:T(8,128)S(1)}, u32[]{:S(2)}, u32[]{:S(2)}) collective-permute-start(f32[32,128]{1,0:T(8,128)S(1)} %sum_column.1.own), channel_id=1, source_target_pairs={{0,192},{64,128},{128,64},{192,0},{1,193},{65,129},{129,65},{193,1... | collective-permute-start | bytes 49160 | tf_op jit(solution)/shard_map/ppermute | solution.py:495
  111.6 0.7 collective-permute-start.7
  112.3 0.0 collective-permute-start.6
  112.3 0.7 collective-permute-done.8.third
  113.0 1.5 %collective-permute-done.7.second = f32[32,128]{1,0:T(8,128)S(1)} collective-permute-done((f32[32,128]{1,0:T(8,128)S(1)}, f32[32,128]{1,0:T(8,128)S(1)}, u32[]{:S(2)}, u32[]{:S(2)}) %collective-permute-start.7) | collective-permute-done | bytes 16416 | tf_op jit(solution)/shard_map/ppermute | solution.py:495
  114.5 0.0 collective-permute-done.6.first
  114.5 0.6 finish.1
  (1 shorter events, 0.0 us)
Async XLA Ops:
  1.4 10.2 %collective-permute-start.2 = (bf16[34,96]{1,0:T(8,128)(2,1)S(1)}, bf16[34,96]{1,0:T(8,128)(2,1)S(1)}, u32[]{:S(2)}, u32[]{:S(2)}) collective-permute-start(bf16[34,96]{1,0:T(8,128)(2,1)S(1)} %pad_maximum_fusion), channel_id=1, source_target_pairs={{0,48},{1,49},{2,50},{3,51},{4,52},{5,53},{6,54},{7,55},{8,56},{9,... | collective-permute-start | bytes 19592 | tf_op jit(solution)/shard_map/ppermute | solution.py:37
  8.3 6.4 %collective-permute-start.1 = (bf16[34,96]{1,0:T(8,128)(2,1)S(1)}, bf16[34,96]{1,0:T(8,128)(2,1)S(1)}, u32[]{:S(2)}, u32[]{:S(2)}) collective-permute-start(bf16[34,96]{1,0:T(8,128)(2,1)S(1)} %pad_maximum_fusion), channel_id=1, source_target_pairs={{0,32},{1,33},{2,34},{3,35},{4,36},{5,37},{6,38},{7,39},{8,40},{9,... | collective-permute-start | bytes 19592 | tf_op jit(solution)/shard_map/ppermute | solution.py:37
  9.3 5.4 %collective-permute-start = (bf16[34,96]{1,0:T(8,128)(2,1)S(1)}, bf16[34,96]{1,0:T(8,128)(2,1)S(1)}, u32[]{:S(2)}, u32[]{:S(2)}) collective-permute-start(bf16[34,96]{1,0:T(8,128)(2,1)S(1)} %pad_maximum_fusion), channel_id=1, source_target_pairs={{0,16},{1,17},{2,18},{3,19},{4,20},{5,21},{6,22},{7,23},{8,24},{9,... | collective-permute-start | bytes 19592 | tf_op jit(solution)/shard_map/ppermute | solution.py:37
  18.1 16.4 %all-to-all-start = ((bf16[16,136,96]{2,1,0:T(8,128)(2,1)}), bf16[16,136,96]{2,1,0:T(8,128)(2,1)S(1)}, u32[]{:S(2)}, u32[]{:S(2)}) async-start(bf16[16,136,96]{2,1,0:T(8,128)(2,1)} %broadcast_in_dim.28), calls=%async_computation | async-start | bytes 1114112 | tf_op jit(solution)/shard_map/all_to_all | solution.py:40
  75.3 17.7 %all-to-all-start.1 = ((f32[16,4,32,128]{3,2,1,0:T(8,128)}), f32[16,4,32,128]{3,2,1,0:T(8,128)S(1)}, u32[]{:S(2)}, u32[]{:S(2)}) async-start(f32[16,4,32,128]{3,2,1,0:T(8,128)} %bitcast.15), calls=%async_computation.1 | async-start | bytes 2097152 | tf_op jit(solution)/shard_map/all_to_all | solution.py:509
  93.0 12.3 %collective-permute-start.3 = (f32[32,128]{1,0:T(8,128)S(1)}, f32[32,128]{1,0:T(8,128)S(1)}, u32[]{:S(2)}, u32[]{:S(2)}) collective-permute-start(f32[32,128]{1,0:T(8,128)S(1)} %get-tuple-element.30), channel_id=1, source_target_pairs={{0,16},{1,17},{2,18},{3,19},{4,20},{5,21},{6,22},{7,23},{8,24},{9,... | collective-permute-start | bytes 49160 | tf_op jit(solution)/shard_map/ppermute | solution.py:515
  93.1 12.2 %collective-permute-start.4 = (f32[32,128]{1,0:T(8,128)S(1)}, f32[32,128]{1,0:T(8,128)S(1)}, u32[]{:S(2)}, u32[]{:S(2)}) collective-permute-start(f32[32,128]{1,0:T(8,128)S(1)} %get-tuple-element.31), channel_id=1, source_target_pairs={{0,32},{1,33},{2,34},{3,35},{4,36},{5,37},{6,38},{7,39},{8,40},{9,... | collective-permute-start | bytes 49160 | tf_op jit(solution)/shard_map/ppermute | solution.py:515
  96.4 8.9 %collective-permute-start.5 = (f32[32,128]{1,0:T(8,128)S(1)}, f32[32,128]{1,0:T(8,128)S(1)}, u32[]{:S(2)}, u32[]{:S(2)}) collective-permute-start(f32[32,128]{1,0:T(8,128)S(1)} %get-tuple-element.32), channel_id=1, source_target_pairs={{0,48},{1,49},{2,50},{3,51},{4,52},{5,53},{6,54},{7,55},{8,56},{9,... | collective-permute-start | bytes 49160 | tf_op jit(solution)/shard_map/ppermute | solution.py:515
  105.3 7.7 %collective-permute-start.8 = (f32[32,128]{1,0:T(8,128)S(1)}, f32[32,128]{1,0:T(8,128)S(1)}, u32[]{:S(2)}, u32[]{:S(2)}) collective-permute-start(f32[32,128]{1,0:T(8,128)S(1)} %sum_column.1.own), channel_id=1, source_target_pairs={{0,192},{64,128},{128,64},{192,0},{1,193},{65,129},{129,65},{193,1... | collective-permute-start | bytes 49160 | tf_op jit(solution)/shard_map/ppermute | solution.py:495
  111.6 2.9 %collective-permute-start.7 = (f32[32,128]{1,0:T(8,128)S(1)}, f32[32,128]{1,0:T(8,128)S(1)}, u32[]{:S(2)}, u32[]{:S(2)}) collective-permute-start(f32[32,128]{1,0:T(8,128)S(1)} %sum_column.1.own), channel_id=1, source_target_pairs={{0,128},{64,192},{128,0},{192,64},{1,129},{65,193},{129,1},{193,65... | collective-permute-start | bytes 49160 | tf_op jit(solution)/shard_map/ppermute | solution.py:495
  112.3 2.2 %collective-permute-start.6 = (f32[32,128]{1,0:T(8,128)S(1)}, f32[32,128]{1,0:T(8,128)S(1)}, u32[]{:S(2)}, u32[]{:S(2)}) collective-permute-start(f32[32,128]{1,0:T(8,128)S(1)} %sum_column.1.own), channel_id=1, source_target_pairs={{0,64},{64,0},{128,192},{192,128},{1,65},{65,1},{129,193},{193,129... | collective-permute-start | bytes 49160 | tf_op jit(solution)/shard_map/ppermute | solution.py:495

commit v7 on v6

--- a/solution.py
+++ b/solution.py
@@ -14,7 +14,7 @@
 PAD = 16
 F32 = jnp.float32
 CHUNK_TILES = 3
-EARLY = 12
+EARLY = 10
 MAIN = 32
 
 
@@ -31,12 +31,21 @@
     return [list(range(z * plane, (z + 1) * plane)) for z in range(SIDE)]
 
 
+def spread(*refs):
+    out_ref = refs[-1]
+    rows = refs[0].shape[0]
+    for to in range(out_ref.shape[0]):
+        for slot, ref in enumerate(refs[:-1]):
+            out_ref[to, slot * rows : (slot + 1) * rows, :] = ref[...]
+
+
 def gather_channels(packed):
     stride = SIDE * SIDE
-    column = jnp.concatenate(
-        [packed] + [lax.ppermute(packed, "shard", shifted(stride, step)) for step in range(1, SIDE)]
-    )
-    same = jnp.broadcast_to(column[None], (stride,) + column.shape)
+    column = [packed] + [
+        lax.ppermute(packed, "shard", shifted(stride, step)) for step in range(1, SIDE)
+    ]
+    shape = jax.ShapeDtypeStruct((stride, SIDE * packed.shape[0], packed.shape[1]), packed.dtype)
+    same = small(spread, shape, "spread", *column)
     return lax.all_to_all(same, "shard", 0, 0, axis_index_groups=plane_groups())
 
 
@@ -367,21 +376,20 @@
         o_copy(chunk).wait()
 
 
-def sum_plane(at_ref, came_ref, zero_ref, *sum_refs):
-    for step, sum_ref in enumerate(sum_refs):
-        at = lax.rem(at_ref[0] + step, SIDE)
+def sum_plane(came_ref, zero_ref, sum_ref):
+    for z in range(SIDE):
         total = zero_ref[...]
         for source in range(came_ref.shape[0]):
-            total = total + came_ref[source, at]
-        sum_ref[...] = total
-
-
-def sum_column(own, first, second, third, zero_ref, sum_ref):
-    sum_ref[...] = (own[...] + first[...]) + (second[...] + third[...]) + zero_ref[...]
-
-
-def finish(scale, part, own, first, second, third, kernel_ref, bias_ref, gain_ref, shift_ref):
-    total = ((own[...] + first[...]) + (second[...] + third[...])) * scale
+            total = total + came_ref[source, z]
+        for rep in range(sum_ref.shape[0] // SIDE):
+            sum_ref[rep * SIDE + z] = total
+
+
+def finish(scale, part, came_ref, zero_ref, kernel_ref, bias_ref, gain_ref, shift_ref):
+    total = zero_ref[...]
+    for source in range(came_ref.shape[0]):
+        total = total + came_ref[source]
+    total = total * scale
     taps = kernel_ref.shape[0]
     kernel_ref[...] = total[:taps, :part]
     bias_ref[...] = total[taps : taps + 1, :part]
@@ -491,14 +499,11 @@
     )(*operands)
 
 
-def over_rep(block, step):
-    return lax.ppermute(block, "rep", [(i, i ^ step) for i in range(4)])
-
-
 def per_device(conv_input, cotangent, kernel, conv_bias, ln_gain, ln_bias):
     taps = kernel.shape[0]
     clips, frames, width = conv_input.shape
     packed = jnp.concatenate([kernel, conv_bias[None], ln_gain[None], ln_bias[None]], 0)
+    packed = jnp.pad(packed, ((0, -packed.shape[0] % SUB), (0, 0)))
     params = gather_channels(packed)
     me = lax.axis_index("shard")
     place = (me // (SIDE * SIDE))[None]
@@ -510,19 +515,22 @@
         pieces.reshape(SIDE * SIDE, SIDE, MAIN, LANES), "shard", 0, 0, axis_index_groups=plane_groups()
     )
     begun, zeros = part_of((0, EARLY))
-    piece = jax.ShapeDtypeStruct(zeros.shape, F32)
-    sums = small(sum_plane, (piece,) * SIDE, "sum_plane", place, came, zeros, scalars=1)
-    column = [lax.ppermute(sums[s], "shard", shifted(SIDE * SIDE, s)) for s in range(1, SIDE)]
+    reps, plane = lax.axis_size("rep"), SIDE * SIDE
+    shape = jax.ShapeDtypeStruct((reps * SIDE,) + zeros.shape, F32)
+    sums = small(sum_plane, shape, "sum_plane", came, zeros)
+    columns = [
+        [rep * SIDE**3 + z * plane + at for rep in range(reps) for z in range(SIDE)]
+        for at in range(plane)
+    ]
+    came = lax.all_to_all(sums, ("rep", "shard"), 0, 0, axis_index_groups=columns)
     grad_input, zeros = part_of((EARLY, width // LANES // CHUNK_TILES), begun)
-    own = small(sum_column, piece, "sum_column", sums[0], *column, zeros)
-    others = [over_rep(own, step) for step in (1, 2, 3)]
     count = clips * frames * lax.axis_size("rep") * lax.axis_size("shard")
-    part = packed.shape[1]
+    part = kernel.shape[1]
     row = jax.ShapeDtypeStruct((1, part), F32)
     grads = small(
         functools.partial(finish, 1.0 / math.sqrt(count), part),
         (jax.ShapeDtypeStruct((taps, part), F32), row, row, row),
-        "finish", own, *others,
+        "finish", came, zeros,
     )
     return (activated[None], grad_input[None], grads[0]) + tuple(g[0] for g in grads[1:])
 

time: 116 us -> 115 us (level)
  waiting for transfers between devices: 16.7 us -> 22.2 us
  starting transfers between devices: 34.5 us -> 29.8 us
  local copies, waits for them, and re-layouts: 3.36 us -> 0 us
  Pallas kernels: 59.1 us -> 60.6 us
    ppermute x6 -> x0, starting transfers between devices: 13.9 us -> none  [the longest x3 7.01 us: over_rep(): return lax.ppermute(block, 'rep', [(i, i ^ step) for i in range(4)])]
    all_to_all x0 -> x1, starting transfers between devices: none -> 9.17 us  [per_device(): lax.all_to_all(sums, ('rep', 'shard'), 0, 0, axis_index_groups=columns)]
    all_to_all x0 -> x1, waiting for transfers between devices: none -> 4.48 us  [per_device(): lax.all_to_all(sums, ('rep', 'shard'), 0, 0, axis_index_groups=columns)]
    concatenate x1 -> x0, local copies, waits for them, and re-layouts: 2.49 us -> none  [gather_channels(): jnp.concatenate([packed] + [lax.ppermute(packed, 'shard', shifted(stride,...]
    ppermute x6 -> x0, waiting for transfers between devices: 2.21 us -> none  [the longest x3 2.2 us: over_rep(): return lax.ppermute(block, 'rep', [(i, i ^ step) for i in range(4)])]
    all_to_all x1, waiting for transfers between devices: 1.71 us -> 3.68 us  [per_device(): lax.all_to_all(pieces.reshape(SIDE * SIDE, SIDE, MAIN, LANES), 'shard', 0...]
    pallas_call x3, Pallas kernels: 0.69 us -> 2.33 us  [small(): pl.pallas_call(body, out_shape=out_shape, in_specs=[scalar] * scalars + [...]
    all_to_all x1, waiting for transfers between devices: 9.64 us -> 10.9 us  [gather_channels(): return lax.all_to_all(same, 'shard', 0, 0, axis_index_groups=plane_groups())]
  transfers between devices with their start and end apart: 11 -> 6, of which waited for: 5 -> 4; matrix products, arithmetic and copies ran while one was open for 0% -> 0% of each run, Pallas kernels for 15% -> 15%
where the time goes in v7:
time: 115 us; the launch traced here: 114 us
  Pallas kernels  60.6 us (53%)
  starting transfers between devices  29.8 us (26%)
  waiting for transfers between devices  22.2 us (19%)
    pallas_call x1, Pallas kernels, run_first(): pl.pallas_call(functools.partial(forward_and_kernel_grad, taps), out_shap...  40.6 us
    pallas_call x2, Pallas kernels, run_second(): pl.pallas_call(functools.partial(input_grad, taps, chunks), out_shape=(ja...  17.7 us
    all_to_all x1, waiting for transfers between devices, gather_channels(): return lax.all_to_all(same, 'shard', 0, 0, axis_index_groups=plane_groups())  10.9 us
    ppermute x3, starting transfers between devices, gather_channels(): lax.ppermute(packed, 'shard', shifted(stride, step))  10.2 us
    all_to_all x1, starting transfers between devices, per_device(): lax.all_to_all(sums, ('rep', 'shard'), 0, 0, axis_index_groups=columns)  9.17 us
    all_to_all x1, starting transfers between devices, gather_channels(): return lax.all_to_all(same, 'shard', 0, 0, axis_index_groups=plane_groups())  6.75 us
    all_to_all x1, waiting for transfers between devices, per_device(): lax.all_to_all(sums, ('rep', 'shard'), 0, 0, axis_index_groups=columns)  4.48 us
    all_to_all x1, waiting for transfers between devices, per_device(): lax.all_to_all(pieces.reshape(SIDE * SIDE, SIDE, MAIN, LANES), 'shard', 0...  3.68 us
  transfers between devices with their start and end apart: 6, of which 4 were waited for; matrix products, arithmetic and copies ran while one was open for 0% of the time, Pallas kernels for 15%

profile of v7, /device:TPU:1, one launch (start us, length us, event | category | flops | bytes accessed | tf_op | source)
XLA Modules:
  0.0 114.1 jit_solution(3924318120658094592)
XLA Ops:
  0.6 0.8 fusion.6.refs_0_
  1.4 6.9 %collective-permute-start.2 = (bf16[40,96]{1,0:T(8,128)(2,1)S(1)}, bf16[40,96]{1,0:T(8,128)(2,1)S(1)}, u32[]{:S(2)}, u32[]{:S(2)}) collective-permute-start(bf16[40,96]{1,0:T(8,128)(2,1)S(1)} %fusion.6.refs_0_), channel_id=1, source_target_pairs={{0,48},{1,49},{2,50},{3,51},{4,52},{5,53},{6,54},{7,55},{8,56},{9,... | collective-permute-start | bytes 23048 | tf_op jit(solution)/shard_map/ppermute | solution.py:45
  8.3 1.0 collective-permute-start.1
  9.3 2.3 %collective-permute-start = (bf16[40,96]{1,0:T(8,128)(2,1)S(1)}, bf16[40,96]{1,0:T(8,128)(2,1)S(1)}, u32[]{:S(2)}, u32[]{:S(2)}) collective-permute-start(bf16[40,96]{1,0:T(8,128)(2,1)S(1)} %fusion.6.refs_0_), channel_id=1, source_target_pairs={{0,16},{1,17},{2,18},{3,19},{4,20},{5,21},{6,22},{7,23},{8,24},{9,... | collective-permute-start | bytes 23048 | tf_op jit(solution)/shard_map/ppermute | solution.py:45
  11.6 0.0 collective-permute-done.2.refs_3_
  11.6 3.2 %collective-permute-done.1.refs_2_ = bf16[40,96]{1,0:T(8,128)(2,1)S(1)} collective-permute-done((bf16[40,96]{1,0:T(8,128)(2,1)S(1)}, bf16[40,96]{1,0:T(8,128)(2,1)S(1)}, u32[]{:S(2)}, u32[]{:S(2)}) %collective-permute-start.1) | collective-permute-done | bytes 7712 | tf_op jit(solution)/shard_map/ppermute | solution.py:45
  14.8 0.0 collective-permute-done.refs_1_
  14.8 0.9 spread.1
  15.7 6.8 %all-to-all-start = ((bf16[16,160,96]{2,1,0:T(8,128)(2,1)}), bf16[16,160,96]{2,1,0:T(8,128)(2,1)S(1)}, u32[]{:S(2)}, u32[]{:S(2)}) async-start(bf16[16,160,96]{2,1,0:T(8,128)(2,1)} %spread.1), calls=%async_computation | async-start | bytes 1310720 | tf_op jit(solution)/shard_map/all_to_all | solution.py:49
  22.5 10.9 %all-to-all-done.came_ref = bf16[16,160,96]{2,1,0:T(8,128)(2,1)S(1)} async-done(((bf16[16,160,96]{2,1,0:T(8,128)(2,1)}), bf16[16,160,96]{2,1,0:T(8,128)(2,1)S(1)}, u32[]{:S(2)}, u32[]{:S(2)}) %all-to-all-start) | async-done | bytes 491552 | tf_op jit(solution)/shard_map/all_to_all | solution.py:49
  33.4 40.6 %forward_and_kernel_grad.1 = (bf16[256,6144]{1,0:T(8,128)(2,1)}, f32[48,288,128]{2,1,0:T(8,128)}, f32[64,32,128]{2,1,0:T(8,128)}, bf16[16,40,384]{2,1,0:T(8,128)(2,1)S(1)}) custom-call(s32[1]{0:T(128)} %bitcast.at_ref, bf16[256,6144]{1,0:T(8,128)(2,1)} %bitcast.12, bf16[256,6144]{1,0:T(8,128)(2,1)} %bitcast.13, bf16[16,160,96]{2,1,0:T(8,128)(2,1)S(1)} %all-to-all-done.came_ref), custom_call_target="tpu_custom_call" | custom-call | flops 195035136 | bytes 31457280 | tf_op jit(solution)/shard_map/forward_and_kernel_grad/pallas_call | solution.py:414
  74.0 3.7 %all-to-all-start.1 = ((f32[16,4,32,128]{3,2,1,0:T(8,128)}), f32[16,4,32,128]{3,2,1,0:T(8,128)S(1)}, u32[]{:S(2)}, u32[]{:S(2)}) async-start(f32[16,4,32,128]{3,2,1,0:T(8,128)} %bitcast.15), calls=%async_computation.1 | async-start | bytes 2097152 | tf_op jit(solution)/shard_map/all_to_all | solution.py:514
  77.7 10.6 %input_grad.2 = (bf16[256,6144]{1,0:T(8,128)(2,1)}, f32[32,128]{1,0:T(8,128)S(1)}) custom-call(f32[48,288,128]{2,1,0:T(8,128)} %get-tuple-element.19.gc_hbm, bf16[16,40,384]{2,1,0:T(8,128)(2,1)S(1)} %get-tuple-element.20.p_ref), custom_call_target="tpu_custom_call" | custom-call | flops 60948480 | bytes 5898240 | tf_op jit(solution)/shard_map/input_grad/pallas_call | solution.py:463
  88.3 3.7 %all-to-all-done.1.came_ref = f32[16,4,32,128]{3,2,1,0:T(8,128)S(1)} async-done(((f32[16,4,32,128]{3,2,1,0:T(8,128)}), f32[16,4,32,128]{3,2,1,0:T(8,128)S(1)}, u32[]{:S(2)}, u32[]{:S(2)}) %all-to-all-start.1) | async-done | bytes 1048608 | tf_op jit(solution)/shard_map/all_to_all | solution.py:514
  91.9 0.8 sum_plane.1
  92.7 9.2 %all-to-all-start.2 = ((f32[16,32,128]{2,1,0:T(8,128)}), f32[16,32,128]{2,1,0:T(8,128)S(1)}, u32[]{:S(2)}, u32[]{:S(2)}) async-start(f32[16,32,128]{2,1,0:T(8,128)} %sum_plane.1), calls=%async_computation.2 | async-start | bytes 524288 | tf_op jit(solution)/shard_map/all_to_all | solution.py:525
  101.9 7.1 %input_grad.3 = (bf16[256,6144]{1,0:T(8,128)(2,1)}, f32[32,128]{1,0:T(8,128)S(1)}) custom-call(f32[48,288,128]{2,1,0:T(8,128)} %get-tuple-element.19.gc_hbm, bf16[16,40,384]{2,1,0:T(8,128)(2,1)S(1)} %get-tuple-element.20.p_ref, bf16[256,6144]{1,0:T(8,128)(2,1)} %get-tuple-element.21.refs_0_), custom_call_target="tpu_custom_call", output_to_operand_aliasing={{0}: (2, {})} | custom-call | flops 36569088 | bytes 3538944 | tf_op jit(solution)/shard_map/input_grad/pallas_call | solution.py:463
  109.0 4.5 %all-to-all-done.2.came_ref = f32[16,32,128]{2,1,0:T(8,128)S(1)} async-done(((f32[16,32,128]{2,1,0:T(8,128)}), f32[16,32,128]{2,1,0:T(8,128)S(1)}, u32[]{:S(2)}, u32[]{:S(2)}) %all-to-all-start.2) | async-done | bytes 262176 | tf_op jit(solution)/shard_map/all_to_all | solution.py:525
  113.5 0.6 finish.1
Async XLA Ops:
  1.4 10.2 %collective-permute-start.2 = (bf16[40,96]{1,0:T(8,128)(2,1)S(1)}, bf16[40,96]{1,0:T(8,128)(2,1)S(1)}, u32[]{:S(2)}, u32[]{:S(2)}) collective-permute-start(bf16[40,96]{1,0:T(8,128)(2,1)S(1)} %fusion.6.refs_0_), channel_id=1, source_target_pairs={{0,48},{1,49},{2,50},{3,51},{4,52},{5,53},{6,54},{7,55},{8,56},{9,... | collective-permute-start | bytes 23048 | tf_op jit(solution)/shard_map/ppermute | solution.py:45
  8.3 6.4 %collective-permute-start.1 = (bf16[40,96]{1,0:T(8,128)(2,1)S(1)}, bf16[40,96]{1,0:T(8,128)(2,1)S(1)}, u32[]{:S(2)}, u32[]{:S(2)}) collective-permute-start(bf16[40,96]{1,0:T(8,128)(2,1)S(1)} %fusion.6.refs_0_), channel_id=1, source_target_pairs={{0,32},{1,33},{2,34},{3,35},{4,36},{5,37},{6,38},{7,39},{8,40},{9,... | collective-permute-start | bytes 23048 | tf_op jit(solution)/shard_map/ppermute | solution.py:45
  9.3 5.4 %collective-permute-start = (bf16[40,96]{1,0:T(8,128)(2,1)S(1)}, bf16[40,96]{1,0:T(8,128)(2,1)S(1)}, u32[]{:S(2)}, u32[]{:S(2)}) collective-permute-start(bf16[40,96]{1,0:T(8,128)(2,1)S(1)} %fusion.6.refs_0_), channel_id=1, source_target_pairs={{0,16},{1,17},{2,18},{3,19},{4,20},{5,21},{6,22},{7,23},{8,24},{9,... | collective-permute-start | bytes 23048 | tf_op jit(solution)/shard_map/ppermute | solution.py:45
  15.7 17.7 %all-to-all-start = ((bf16[16,160,96]{2,1,0:T(8,128)(2,1)}), bf16[16,160,96]{2,1,0:T(8,128)(2,1)S(1)}, u32[]{:S(2)}, u32[]{:S(2)}) async-start(bf16[16,160,96]{2,1,0:T(8,128)(2,1)} %spread.1), calls=%async_computation | async-start | bytes 1310720 | tf_op jit(solution)/shard_map/all_to_all | solution.py:49
  74.0 17.9 %all-to-all-start.1 = ((f32[16,4,32,128]{3,2,1,0:T(8,128)}), f32[16,4,32,128]{3,2,1,0:T(8,128)S(1)}, u32[]{:S(2)}, u32[]{:S(2)}) async-start(f32[16,4,32,128]{3,2,1,0:T(8,128)} %bitcast.15), calls=%async_computation.1 | async-start | bytes 2097152 | tf_op jit(solution)/shard_map/all_to_all | solution.py:514
  92.7 20.8 %all-to-all-start.2 = ((f32[16,32,128]{2,1,0:T(8,128)}), f32[16,32,128]{2,1,0:T(8,128)S(1)}, u32[]{:S(2)}, u32[]{:S(2)}) async-start(f32[16,32,128]{2,1,0:T(8,128)} %sum_plane.1), calls=%async_computation.2 | async-start | bytes 524288 | tf_op jit(solution)/shard_map/all_to_all | solution.py:525

commit v8 on v7

--- a/solution.py
+++ b/solution.py
@@ -141,8 +141,8 @@
         bias = bcast_row(pf, taps)
 
         def run(source, weights, first, count, start, store):
-            for r0 in range(0, count, block):
-                size = min(block, count - r0)
+            for r0 in range(0, count, 16):
+                size = min(16, count - r0)
                 acc = [start] * size
                 for phase in range(SUB):
                     depth = len(range(phase, len(weights), SUB))
@@ -171,13 +171,14 @@
         def last(r, value):
             here = pl.ds(SUB * r, SUB)
             own, before, after = fa[here, :], fb[here, :], fb[pl.ds(SUB * r + 1, SUB), :]
-            cv[tile, pl.ds(2 * SUB * r, SUB, stride=2), :] = own + before
-            cv[tile, pl.ds(2 * SUB * r + 1, SUB, stride=2), :] = (value - own) - after + (bias + bias)
+            even = own + before
+            odd = (value - own) - after + (bias + bias)
+            cv[tile, pl.ds(2 * SUB * r, SUB, stride=2), :] = even
+            cv[tile, pl.ds(2 * SUB * r + 1, SUB, stride=2), :] = odd
+            s2[here, :] += even
+            s2[pl.ds(SUB * (half + r), SUB), :] += odd
 
         run(xt, w_both, 0, half, None, last)
-        for r in range(rows):
-            at = pl.ds(SUB * r, SUB)
-            s1[at, :] += cv[tile, at, :]
         return 0
 
     def conv_chunk(chunk, _):
@@ -186,6 +187,11 @@
         return 0
 
     lax.fori_loop(0, chunks, conv_chunk, 0)
+    for r in range(rows // 2):
+        here = pl.ds(SUB * r, SUB)
+        s1[pl.ds(2 * SUB * r, SUB, stride=2), :] = s2[here, :]
+        s1[pl.ds(2 * SUB * r + 1, SUB, stride=2), :] = s2[pl.ds(frames // 2 + SUB * r, SUB), :]
+    s2[...] = jnp.zeros_like(s2)
 
     row_a[...] = jnp.broadcast_to(
         jnp.sum(s1[...], axis=1, keepdims=True) * (1.0 / width), s1.shape

time: 115 us -> 114 us (level)
  transfers between devices with their start and end apart: 6 -> 6, of which waited for: 4 -> 4; matrix products, arithmetic and copies ran while one was open for 0% -> 0% of each run, Pallas kernels for 15% -> 16%
where the time goes in v8:
time: 114 us
  Pallas kernels  60.2 us (53%)
  starting transfers between devices  29.8 us (26%)
  waiting for transfers between devices  22.2 us (19%)
    pallas_call x1, Pallas kernels, run_first(): pl.pallas_call(functools.partial(forward_and_kernel_grad, taps), out_shap...  40.2 us
    pallas_call x2, Pallas kernels, run_second(): pl.pallas_call(functools.partial(input_grad, taps, chunks), out_shape=(ja...  17.7 us
    all_to_all x1, waiting for transfers between devices, gather_channels(): return lax.all_to_all(same, 'shard', 0, 0, axis_index_groups=plane_groups())  10.9 us
    ppermute x3, starting transfers between devices, gather_channels(): lax.ppermute(packed, 'shard', shifted(stride, step))  10.2 us
    all_to_all x1, starting transfers between devices, per_device(): lax.all_to_all(sums, ('rep', 'shard'), 0, 0, axis_index_groups=columns)  9.17 us
    all_to_all x1, starting transfers between devices, gather_channels(): return lax.all_to_all(same, 'shard', 0, 0, axis_index_groups=plane_groups())  6.75 us
    all_to_all x1, waiting for transfers between devices, per_device(): lax.all_to_all(sums, ('rep', 'shard'), 0, 0, axis_index_groups=columns)  4.48 us
    all_to_all x1, waiting for transfers between devices, per_device(): lax.all_to_all(pieces.reshape(SIDE * SIDE, SIDE, MAIN, LANES), 'shard', 0...  3.68 us
  transfers between devices with their start and end apart: 6, of which 4 were waited for; matrix products, arithmetic and copies ran while one was open for 0% of the time, Pallas kernels for 16%

profile of v8, /device:TPU:1, one launch (start us, length us, event | category | flops | bytes accessed | tf_op | source)
XLA Modules:
  0.0 113.7 jit_solution(9902552674186363328)
XLA Ops:
  0.6 0.8 fusion.6.refs_0_
  1.4 6.9 %collective-permute-start.2 = (bf16[40,96]{1,0:T(8,128)(2,1)S(1)}, bf16[40,96]{1,0:T(8,128)(2,1)S(1)}, u32[]{:S(2)}, u32[]{:S(2)}) collective-permute-start(bf16[40,96]{1,0:T(8,128)(2,1)S(1)} %fusion.6.refs_0_), channel_id=1, source_target_pairs={{0,48},{1,49},{2,50},{3,51},{4,52},{5,53},{6,54},{7,55},{8,56},{9,... | collective-permute-start | bytes 23048 | tf_op jit(solution)/shard_map/ppermute | solution.py:45
  8.3 1.0 collective-permute-start.1
  9.3 2.3 %collective-permute-start = (bf16[40,96]{1,0:T(8,128)(2,1)S(1)}, bf16[40,96]{1,0:T(8,128)(2,1)S(1)}, u32[]{:S(2)}, u32[]{:S(2)}) collective-permute-start(bf16[40,96]{1,0:T(8,128)(2,1)S(1)} %fusion.6.refs_0_), channel_id=1, source_target_pairs={{0,16},{1,17},{2,18},{3,19},{4,20},{5,21},{6,22},{7,23},{8,24},{9,... | collective-permute-start | bytes 23048 | tf_op jit(solution)/shard_map/ppermute | solution.py:45
  11.6 0.0 collective-permute-done.2.refs_3_
  11.6 3.2 %collective-permute-done.1.refs_2_ = bf16[40,96]{1,0:T(8,128)(2,1)S(1)} collective-permute-done((bf16[40,96]{1,0:T(8,128)(2,1)S(1)}, bf16[40,96]{1,0:T(8,128)(2,1)S(1)}, u32[]{:S(2)}, u32[]{:S(2)}) %collective-permute-start.1) | collective-permute-done | bytes 7712 | tf_op jit(solution)/shard_map/ppermute | solution.py:45
  14.8 0.0 collective-permute-done.refs_1_
  14.8 0.9 spread.1
  15.7 6.8 %all-to-all-start = ((bf16[16,160,96]{2,1,0:T(8,128)(2,1)}), bf16[16,160,96]{2,1,0:T(8,128)(2,1)S(1)}, u32[]{:S(2)}, u32[]{:S(2)}) async-start(bf16[16,160,96]{2,1,0:T(8,128)(2,1)} %spread.1), calls=%async_computation | async-start | bytes 1310720 | tf_op jit(solution)/shard_map/all_to_all | solution.py:49
  22.5 10.9 %all-to-all-done.came_ref = bf16[16,160,96]{2,1,0:T(8,128)(2,1)S(1)} async-done(((bf16[16,160,96]{2,1,0:T(8,128)(2,1)}), bf16[16,160,96]{2,1,0:T(8,128)(2,1)S(1)}, u32[]{:S(2)}, u32[]{:S(2)}) %all-to-all-start) | async-done | bytes 491552 | tf_op jit(solution)/shard_map/all_to_all | solution.py:49
  33.4 40.2 %forward_and_kernel_grad.1 = (bf16[256,6144]{1,0:T(8,128)(2,1)}, f32[48,288,128]{2,1,0:T(8,128)}, f32[64,32,128]{2,1,0:T(8,128)}, bf16[16,40,384]{2,1,0:T(8,128)(2,1)S(1)}) custom-call(s32[1]{0:T(128)} %bitcast.at_ref, bf16[256,6144]{1,0:T(8,128)(2,1)} %bitcast.12, bf16[256,6144]{1,0:T(8,128)(2,1)} %bitcast.13, bf16[16,160,96]{2,1,0:T(8,128)(2,1)S(1)} %all-to-all-done.came_ref), custom_call_target="tpu_custom_call" | custom-call | flops 195035136 | bytes 31457280 | tf_op jit(solution)/shard_map/forward_and_kernel_grad/pallas_call | solution.py:420
  73.6 3.7 %all-to-all-start.1 = ((f32[16,4,32,128]{3,2,1,0:T(8,128)}), f32[16,4,32,128]{3,2,1,0:T(8,128)S(1)}, u32[]{:S(2)}, u32[]{:S(2)}) async-start(f32[16,4,32,128]{3,2,1,0:T(8,128)} %bitcast.15), calls=%async_computation.1 | async-start | bytes 2097152 | tf_op jit(solution)/shard_map/all_to_all | solution.py:520
  77.2 10.6 %input_grad.2 = (bf16[256,6144]{1,0:T(8,128)(2,1)}, f32[32,128]{1,0:T(8,128)S(1)}) custom-call(f32[48,288,128]{2,1,0:T(8,128)} %get-tuple-element.19.gc_hbm, bf16[16,40,384]{2,1,0:T(8,128)(2,1)S(1)} %get-tuple-element.20.p_ref), custom_call_target="tpu_custom_call" | custom-call | flops 60948480 | bytes 5898240 | tf_op jit(solution)/shard_map/input_grad/pallas_call | solution.py:469
  87.8 3.7 %all-to-all-done.1.came_ref = f32[16,4,32,128]{3,2,1,0:T(8,128)S(1)} async-done(((f32[16,4,32,128]{3,2,1,0:T(8,128)}), f32[16,4,32,128]{3,2,1,0:T(8,128)S(1)}, u32[]{:S(2)}, u32[]{:S(2)}) %all-to-all-start.1) | async-done | bytes 1048608 | tf_op jit(solution)/shard_map/all_to_all | solution.py:520
  91.5 0.8 sum_plane.1
  92.2 9.2 %all-to-all-start.2 = ((f32[16,32,128]{2,1,0:T(8,128)}), f32[16,32,128]{2,1,0:T(8,128)S(1)}, u32[]{:S(2)}, u32[]{:S(2)}) async-start(f32[16,32,128]{2,1,0:T(8,128)} %sum_plane.1), calls=%async_computation.2 | async-start | bytes 524288 | tf_op jit(solution)/shard_map/all_to_all | solution.py:531
  101.4 7.1 %input_grad.3 = (bf16[256,6144]{1,0:T(8,128)(2,1)}, f32[32,128]{1,0:T(8,128)S(1)}) custom-call(f32[48,288,128]{2,1,0:T(8,128)} %get-tuple-element.19.gc_hbm, bf16[16,40,384]{2,1,0:T(8,128)(2,1)S(1)} %get-tuple-element.20.p_ref, bf16[256,6144]{1,0:T(8,128)(2,1)} %get-tuple-element.21.refs_0_), custom_call_target="tpu_custom_call", output_to_operand_aliasing={{0}: (2, {})} | custom-call | flops 36569088 | bytes 3538944 | tf_op jit(solution)/shard_map/input_grad/pallas_call | solution.py:469
  108.5 4.5 %all-to-all-done.2.came_ref = f32[16,32,128]{2,1,0:T(8,128)S(1)} async-done(((f32[16,32,128]{2,1,0:T(8,128)}), f32[16,32,128]{2,1,0:T(8,128)S(1)}, u32[]{:S(2)}, u32[]{:S(2)}) %all-to-all-start.2) | async-done | bytes 262176 | tf_op jit(solution)/shard_map/all_to_all | solution.py:531
  113.0 0.6 finish.1
Async XLA Ops:
  1.4 10.2 %collective-permute-start.2 = (bf16[40,96]{1,0:T(8,128)(2,1)S(1)}, bf16[40,96]{1,0:T(8,128)(2,1)S(1)}, u32[]{:S(2)}, u32[]{:S(2)}) collective-permute-start(bf16[40,96]{1,0:T(8,128)(2,1)S(1)} %fusion.6.refs_0_), channel_id=1, source_target_pairs={{0,48},{1,49},{2,50},{3,51},{4,52},{5,53},{6,54},{7,55},{8,56},{9,... | collective-permute-start | bytes 23048 | tf_op jit(solution)/shard_map/ppermute | solution.py:45
  8.3 6.4 %collective-permute-start.1 = (bf16[40,96]{1,0:T(8,128)(2,1)S(1)}, bf16[40,96]{1,0:T(8,128)(2,1)S(1)}, u32[]{:S(2)}, u32[]{:S(2)}) collective-permute-start(bf16[40,96]{1,0:T(8,128)(2,1)S(1)} %fusion.6.refs_0_), channel_id=1, source_target_pairs={{0,32},{1,33},{2,34},{3,35},{4,36},{5,37},{6,38},{7,39},{8,40},{9,... | collective-permute-start | bytes 23048 | tf_op jit(solution)/shard_map/ppermute | solution.py:45
  9.3 5.4 %collective-permute-start = (bf16[40,96]{1,0:T(8,128)(2,1)S(1)}, bf16[40,96]{1,0:T(8,128)(2,1)S(1)}, u32[]{:S(2)}, u32[]{:S(2)}) collective-permute-start(bf16[40,96]{1,0:T(8,128)(2,1)S(1)} %fusion.6.refs_0_), channel_id=1, source_target_pairs={{0,16},{1,17},{2,18},{3,19},{4,20},{5,21},{6,22},{7,23},{8,24},{9,... | collective-permute-start | bytes 23048 | tf_op jit(solution)/shard_map/ppermute | solution.py:45
  15.7 17.7 %all-to-all-start = ((bf16[16,160,96]{2,1,0:T(8,128)(2,1)}), bf16[16,160,96]{2,1,0:T(8,128)(2,1)S(1)}, u32[]{:S(2)}, u32[]{:S(2)}) async-start(bf16[16,160,96]{2,1,0:T(8,128)(2,1)} %spread.1), calls=%async_computation | async-start | bytes 1310720 | tf_op jit(solution)/shard_map/all_to_all | solution.py:49
  73.6 17.9 %all-to-all-start.1 = ((f32[16,4,32,128]{3,2,1,0:T(8,128)}), f32[16,4,32,128]{3,2,1,0:T(8,128)S(1)}, u32[]{:S(2)}, u32[]{:S(2)}) async-start(f32[16,4,32,128]{3,2,1,0:T(8,128)} %bitcast.15), calls=%async_computation.1 | async-start | bytes 2097152 | tf_op jit(solution)/shard_map/all_to_all | solution.py:520
  92.2 20.8 %all-to-all-start.2 = ((f32[16,32,128]{2,1,0:T(8,128)}), f32[16,32,128]{2,1,0:T(8,128)S(1)}, u32[]{:S(2)}, u32[]{:S(2)}) async-start(f32[16,32,128]{2,1,0:T(8,128)} %sum_plane.1), calls=%async_computation.2 | async-start | bytes 524288 | tf_op jit(solution)/shard_map/all_to_all | solution.py:531
